TPU v7x, 32 devices: a whole 2x2x4 slice. The times are simulated.
32 devices in a mesh: width: 4 (over y, x), seq: 8 (over z, core).
Axes of the slice: x: 2, y: 2, z: 4, core: 2. Of those that a mesh axis runs over, the one named last changes fastest.
Arguments:
- hidden_in: bfloat16 [4, 2, 1024, 2048], P('width', None, 'seq'), may hold values from -6 to 6
- starts: int32 [4, 2, 4], P('width'), may hold values from 0 to 1023, as said below
- in_gain: float32 [2048], replicated, may hold values from 0.1 to 1.9
- in_weight: bfloat16 [2048, 8512], P('seq'), may hold values from -0.125 to 0.125
- conv_weight: float32 [4, 4352], replicated, may hold values from -3 to 3
- conv_bias: float32 [4352], replicated, may hold values from -3 to 3
- step_bias: float32 [64], replicated, may hold values from -5 to -2
- decay_log: float32 [64], replicated, may hold values from -9 to 1.5
- skip_gain: float32 [64], replicated, may hold values from 0.5 to 1.5
- gate_gain: float32 [4096], replicated, may hold values from 0.1 to 1.9
- out_weight: bfloat16 [4096, 2048], P('seq'), may hold values from -0.125 to 0.125
- cotangent: bfloat16 [4, 2, 1024, 2048], P('width', None, 'seq'), may hold values from -6 to 6
Outputs:
- output: bfloat16 [4, 2, 1024, 2048], P('width', None, 'seq')
- grad_hidden: bfloat16 [4, 2, 1024, 2048], P('width', None, 'seq')
- grad_in_gain: float32 [2048], replicated
- grad_in_weight: float32 [2048, 8512], P('seq', 'width')
- grad_conv_weight: float32 [4, 4352], replicated
- grad_conv_bias: float32 [4352], replicated
- grad_step_bias: float32 [64], replicated
- grad_decay_log: float32 [64], replicated
- grad_skip_gain: float32 [64], replicated
- grad_gate_gain: float32 [4096], replicated
- grad_out_weight: float32 [4096, 2048], P('width', 'seq')
Inputs may be any that keep to these rules, and one draw needn't show every extreme that they name: In each group and micro-batch the 4 starts increase strictly from 0; the second lies below 128 and the third above 896, so one document runs from the first index of seq to the last.
All inputs are finite; a program needn't handle non-finite values.
Results may differ from a plain program's by a relative error of at most 0.0087.
Values may be sent and summed in bfloat16 or wider, within the bound.
A program may use at most 384 MiB of HBM per device.

v0:
```python
from functools import partial

import jax
import jax.numpy as jnp
from jax import lax
from jax.sharding import PartitionSpec as P

INNER = 4096
HEADS = 64
HEAD_DIM = 64
STATE = 128
CONV = 4352


EPSILON = 1e-05
PRECISION = lax.Precision.HIGHEST


def shifted(value, axis, steps):
    count = lax.axis_size(axis)
    first, last = (max(0, -steps), min(count, count - steps))
    return lax.ppermute(value, axis, [(source, source + steps) for source in range(first, last)])


def input_norm(hidden, in_gain):
    return hidden * lax.rsqrt(jnp.mean(hidden * hidden, axis=1, keepdims=True) + EPSILON) * in_gain


def doc_number(doc_starts, positions):
    return jnp.sum((doc_starts[None, :] <= positions[:, None]).astype(jnp.int32), axis=1) - 1


def doc_masks(doc_starts, positions, tap_count):
    doc_ids = doc_number(doc_starts, positions)
    columns = [
        (doc_ids == doc_number(doc_starts, positions - offset)).astype(jnp.float32)
        for offset in range(1, tap_count)
    ]
    start_flags = jnp.sum((positions[:, None] == doc_starts[None, :]).astype(jnp.int32), axis=1)
    return (jnp.stack(columns, axis=1), start_flags)


def conv_block(xbc_ext, conv_weight, conv_bias, same_doc):
    tap_count = conv_weight.shape[0]
    row_count = xbc_ext.shape[0] - tap_count + 1
    conv_sum = conv_bias + conv_weight[tap_count - 1] * xbc_ext[tap_count - 1 :]
    for offset in range(1, tap_count):
        first_row = tap_count - 1 - offset
        conv_sum = (
            conv_sum
            + conv_weight[first_row]
            * xbc_ext[first_row : first_row + row_count]
            * same_doc[:, offset - 1 : offset]
        )
    return conv_sum


def mixer_front(
    xbc_ext, step_raw, conv_weight, conv_bias, step_bias, decay_log, same_doc, start_flags
):
    row_count = step_raw.shape[0]
    activated = jax.nn.silu(conv_block(xbc_ext, conv_weight, conv_bias, same_doc))
    x_heads = activated[:, :INNER].reshape(row_count, HEADS, HEAD_DIM)
    write_vecs = activated[:, INNER : INNER + STATE]
    read_vecs = activated[:, INNER + STATE :]
    step_size = jax.nn.softplus(step_raw + step_bias)
    log_cum = jnp.cumsum(-step_size * jnp.exp(decay_log), axis=0).T
    reset_count = jnp.cumsum(start_flags)
    row_index = jnp.arange(row_count)
    causal_keep = (row_index[:, None] >= row_index[None, :]) & (
        reset_count[:, None] == reset_count[None, :]
    )
    keep_float = causal_keep.astype(jnp.float32)
    decays = (
        jnp.exp(jnp.where(causal_keep[None], log_cum[:, :, None] - log_cum[:, None, :], 0.0))
        * keep_float[None]
    )
    scores = jnp.dot(read_vecs, write_vecs.T, precision=PRECISION)
    inputs = x_heads * step_size[:, :, None]
    local_out = jnp.einsum("hij,jhp->ihp", decays * scores[None], inputs, precision=PRECISION)
    carry_in = jnp.exp(log_cum.T) * (reset_count == 0).astype(jnp.float32)[:, None]
    local_state = jnp.einsum(
        "hj,jhp,jn->hpn", decays[:, -1, :], inputs, write_vecs, precision=PRECISION
    )
    return (x_heads, read_vecs, carry_in, local_out, local_state, carry_in[-1])


def mixer_rear(
    local_out,
    x_heads,
    read_vecs,
    carry_in,
    state_in,
    gate_z,
    skip_gain,
    gate_gain,
    head_mask,
    active,
):
    row_count = local_out.shape[0]
    from_state = (
        jnp.einsum("in,hpn->ihp", read_vecs, state_in, precision=PRECISION) * carry_in[:, :, None]
    )
    mixed = (local_out + from_state + skip_gain[None, :, None] * x_heads) * head_mask[None, :, None]
    gated = mixed.reshape(row_count, INNER) * jax.nn.silu(gate_z)
    return (
        gated
        * lax.rsqrt(jnp.sum(gated * gated, axis=1, keepdims=True) / active + EPSILON)
        * gate_gain
    )


def combine(earlier, later):
    return (earlier[0] * later[0], later[0][:, :, None, None] * earlier[1] + later[1])


def shift_amounts(seq_total):
    amounts = [1]
    distance = 1
    while distance < seq_total:
        amounts.append(distance)
        distance = distance * 2
    return amounts


def chain_forward(values, seq_index, seq_total):
    identity = (jnp.ones_like(values[0]), jnp.zeros_like(values[1]))
    for turn, amount in enumerate(shift_amounts(seq_total)):
        received = shifted((values[0], values[1]), "seq", amount)
        valid = seq_index >= amount
        if turn == 0:
            joined = identity
            values = (
                jnp.where(valid, received[0], joined[0]),
                jnp.where(valid, received[1], joined[1]),
            )
        else:
            joined = combine(received, values)
            values = (
                jnp.where(valid, joined[0], values[0]),
                jnp.where(valid, joined[1], values[1]),
            )
    return values


def chain_backward(values, seq_index, seq_total):
    identity = (jnp.ones_like(values[0]), jnp.zeros_like(values[1]))
    for turn, amount in enumerate(shift_amounts(seq_total)):
        received = shifted((values[0], values[1]), "seq", -amount)
        valid = seq_index + amount < seq_total
        if turn == 0:
            joined = identity
            values = (
                jnp.where(valid, received[0], joined[0]),
                jnp.where(valid, received[1], joined[1]),
            )
        else:
            joined = combine(received, values)
            values = (
                jnp.where(valid, joined[0], values[0]),
                jnp.where(valid, joined[1], values[1]),
            )
    return values


def per_device(
    hidden_in,
    starts,
    in_gain,
    in_weight,
    conv_weight,
    conv_bias,
    step_bias,
    decay_log,
    skip_gain,
    gate_gain,
    out_weight,
    cotangent,
):
    full_in, full_out = (
        lax.all_gather(in_weight, "seq", axis=0, tiled=True),
        lax.all_gather(out_weight, "seq", axis=0, tiled=True),
    )
    group_index = lax.axis_index("width")
    head_count = HEADS // 8 * jnp.left_shift(jnp.int32(1), group_index)
    head_mask = (jnp.arange(HEADS, dtype=jnp.int32) < head_count).astype(jnp.float32)
    active = head_count.astype(jnp.float32) * HEAD_DIM
    micro_count = hidden_in.shape[1]
    row_count = hidden_in.shape[2]
    model_width = hidden_in.shape[3]
    tap_count = conv_weight.shape[0]
    seq_index = lax.axis_index("seq")
    seq_total = lax.axis_size("seq")
    positions = seq_index * row_count + jnp.arange(row_count, dtype=jnp.int32)
    flat_hidden = hidden_in[0].astype(jnp.float32).reshape(micro_count * row_count, model_width)
    flat_grad = cotangent[0].reshape(micro_count * row_count, model_width)
    normed, norm_back = jax.vjp(input_norm, flat_hidden, in_gain)
    normed_low = normed.astype(jnp.bfloat16)
    projected = jnp.dot(normed_low, full_in, preferred_element_type=jnp.float32).astype(
        jnp.bfloat16
    )
    projected = projected.reshape(micro_count, row_count, projected.shape[1])
    tail_rows = shifted(projected[:, row_count - tap_count + 1 :, INNER : INNER + CONV], "seq", 1)
    xbc_all = jnp.concatenate([tail_rows, projected[:, :, INNER : INNER + CONV]], axis=1).astype(
        jnp.float32
    )
    gate_all = projected[:, :, :INNER].astype(jnp.float32)
    steps_all = projected[:, :, INNER + CONV :].astype(jnp.float32)
    fronts, front_backs = ([], [])
    for micro_index in range(micro_count):
        same_doc, start_flags = doc_masks(starts[0, micro_index], positions, tap_count)
        front_out, front_back = jax.vjp(
            partial(mixer_front, same_doc=same_doc, start_flags=start_flags),
            xbc_all[micro_index],
            steps_all[micro_index],
            conv_weight,
            conv_bias,
            step_bias,
            decay_log,
        )
        fronts.append(front_out)
        front_backs.append(front_back)
    decay_stack = jnp.stack([front_out[5] for front_out in fronts])
    local_stack = jnp.stack([front_out[4] for front_out in fronts])
    state_in = chain_forward((decay_stack, local_stack), seq_index, seq_total)[1]
    gated_list, rear_backs = ([], [])
    for micro_index in range(micro_count):
        x_heads, read_vecs, carry_in, local_out, local_state, block_decay = fronts[micro_index]
        gated_norm, rear_back = jax.vjp(
            partial(mixer_rear, head_mask=head_mask, active=active),
            local_out,
            x_heads,
            read_vecs,
            carry_in,
            state_in[micro_index],
            gate_all[micro_index],
            skip_gain,
            gate_gain,
        )
        gated_list.append(gated_norm)
        rear_backs.append(rear_back)
    norm_low = jnp.concatenate(gated_list, axis=0).astype(jnp.bfloat16)
    branch = jnp.dot(norm_low, full_out, preferred_element_type=jnp.float32)
    output = (
        (flat_hidden + branch).astype(jnp.bfloat16).reshape(micro_count, row_count, model_width)
    )
    grad_out_w = lax.dot_general(
        norm_low, flat_grad, (((0,), (0,)), ((), ())), preferred_element_type=jnp.float32
    )
    grad_norm = lax.dot_general(
        flat_grad, full_out, (((1,), (1,)), ((), ())), preferred_element_type=jnp.float32
    )
    grad_norm = grad_norm.reshape(micro_count, row_count, INNER)
    rear_grads = [
        rear_backs[micro_index](grad_norm[micro_index]) for micro_index in range(micro_count)
    ]
    grad_state_stack = jnp.stack([rear_item[4] for rear_item in rear_grads])
    grad_state_out = chain_backward((decay_stack, grad_state_stack), seq_index, seq_total)[1]
    small_grads = tuple(
        (
            jnp.zeros(weight_item.shape, jnp.float32)
            for weight_item in (conv_weight, conv_bias, step_bias, decay_log, skip_gain, gate_gain)
        )
    )
    ext_list, step_list = ([], [])
    for micro_index in range(micro_count):
        (
            grad_local,
            grad_heads,
            grad_read,
            grad_carry,
            grad_state_in,
            grad_gate,
            grad_skip,
            grad_gate_gain,
        ) = rear_grads[micro_index]
        grad_decay = jnp.sum(grad_state_out[micro_index] * state_in[micro_index], axis=(1, 2))
        grad_ext, grad_steps, grad_taps, grad_conv_b, grad_step_b, grad_decay_l = front_backs[
            micro_index
        ]((grad_heads, grad_read, grad_carry, grad_local, grad_state_out[micro_index], grad_decay))
        ext_list.append(grad_ext)
        step_list.append(grad_steps)
        small_grads = tuple(
            (
                running + addition
                for running, addition in zip(
                    small_grads,
                    (grad_taps, grad_conv_b, grad_step_b, grad_decay_l, grad_skip, grad_gate_gain),
                )
            )
        )
    grad_exts = jnp.stack(ext_list)
    returned = shifted(grad_exts[:, : tap_count - 1].astype(jnp.bfloat16), "seq", -1).astype(
        jnp.float32
    )
    grad_conv_in = grad_exts[:, tap_count - 1 :] + jnp.concatenate(
        [jnp.zeros((micro_count, row_count - tap_count + 1, CONV), jnp.float32), returned], axis=1
    )
    grad_gates = jnp.stack([rear_item[5] for rear_item in rear_grads])
    grad_proj = jnp.concatenate([grad_gates, grad_conv_in, jnp.stack(step_list)], axis=2).astype(
        jnp.bfloat16
    )
    grad_proj = grad_proj.reshape(micro_count * row_count, grad_proj.shape[2])
    grad_in_w = lax.dot_general(
        normed_low, grad_proj, (((0,), (0,)), ((), ())), preferred_element_type=jnp.float32
    )
    grad_normed = lax.dot_general(
        grad_proj, full_in, (((1,), (1,)), ((), ())), preferred_element_type=jnp.float32
    )
    grad_hidden, grad_gain_in = norm_back(grad_normed)
    hidden_grads = (
        (flat_grad.astype(jnp.float32) + grad_hidden)
        .astype(jnp.bfloat16)
        .reshape(micro_count, row_count, model_width)
    )
    small_grads = (grad_gain_in,) + small_grads
    rows_in, rows_out = (
        lax.psum_scatter(grad_in_w, "seq", scatter_dimension=0, tiled=True),
        lax.psum_scatter(grad_out_w, "seq", scatter_dimension=1, tiled=True),
    )
    shard_in, shard_out = (
        lax.psum_scatter(rows_in, "width", scatter_dimension=1, tiled=True),
        lax.psum_scatter(rows_out, "width", scatter_dimension=0, tiled=True),
    )
    summed = lax.psum(small_grads, ("width", "seq"))
    return (
        output[None],
        hidden_grads[None],
        summed[0],
        shard_in,
        summed[1],
        summed[2],
        summed[3],
        summed[4],
        summed[5],
        summed[6],
        shard_out,
    )


def solution(mesh):
    in_specs = (
        P("width", None, "seq", None),
        P("width", None, None),
        P(),
        P("seq", None),
        P(),
        P(),
        P(),
        P(),
        P(),
        P(),
        P("seq", None),
        P("width", None, "seq", None),
    )
    out_specs = (
        P("width", None, "seq", None),
        P("width", None, "seq", None),
        P(),
        P("seq", "width"),
        P(),
        P(),
        P(),
        P(),
        P(),
        P(),
        P("width", "seq"),
    )
    return jax.shard_map(
        per_device, mesh=mesh, in_specs=in_specs, out_specs=out_specs, check_vma=False
    )
```

profile of v0, /device:TPU:0, one launch (start us, length us, event | category | flops | bytes accessed | tf_op | source)
XLA Modules:
  0.0 2693.3 jit_solution(891471997299611031)
XLA Ops:
  10.9 305.1 %all-gather.3.cloned.1.call-done = bf16[2048,8512]{0,1:T(8,128)(2,1)} async-done(((bf16[256,8512]{0,1:T(8,128)(2,1)}), bf16[2048,8512]{0,1:T(8,128)(2,1)}) %all-gather.3.cloned.1.call-update) | async-done | bytes 34865168 | tf_op jit(solution)/shard_map/all_gather | solution.py:181
  316.1 19.6 convolution_convert_fusion
  335.7 6.6 copy.251
  355.9 4.8 fusion.22
  377.7 3.9 collective-permute-start.4
  381.5 5.1 collective-permute-done.4
  389.5 127.3 %collective-permute-start.5 = (f32[2,64,64,128]{3,2,1,0:T(8,128)}, f32[2,64,64,128]{3,2,1,0:T(8,128)}, u32[]{:S(2)}, u32[]{:S(2)}) collective-permute-start(f32[2,64,64,128]{3,2,1,0:T(8,128)} %broadcast_select_fusion.1), channel_id=1, source_target_pairs={{0,1},{1,2},{2,3},{3,4},{4,5},{5,6},{6,7},{8,9},{9,10},{10,11},{11... | collective-permute-start | bytes 12582920 | tf_op jit(solution)/shard_map/ppermute | solution.py:22
  521.9 4.7 add_select_fusion.5
  526.7 48.6 %collective-permute-start.6 = (f32[2,64,64,128]{3,2,1,0:T(8,128)}, f32[2,64,64,128]{3,2,1,0:T(8,128)}, u32[]{:S(2)}, u32[]{:S(2)}) collective-permute-start(f32[2,64,64,128]{3,2,1,0:T(8,128)} %add_select_fusion.5), channel_id=1, source_target_pairs={{0,2},{1,3},{2,4},{3,5},{4,6},{5,7},{8,10},{9,11},{10,12},{11,13},... | collective-permute-start | bytes 12582920 | tf_op jit(solution)/shard_map/ppermute | solution.py:22
  577.9 84.7 %collective-permute-done.6 = f32[2,64,64,128]{3,2,1,0:T(8,128)} collective-permute-done((f32[2,64,64,128]{3,2,1,0:T(8,128)}, f32[2,64,64,128]{3,2,1,0:T(8,128)}, u32[]{:S(2)}, u32[]{:S(2)}) %collective-permute-start.6) | collective-permute-done | bytes 4194336 | tf_op jit(solution)/shard_map/ppermute | solution.py:22
  662.6 6.0 add_select_fusion.4
  668.6 7.4 collective-permute-start.7
  678.6 10.1 fusion.255
  702.2 60.5 %collective-permute-done.3 = f32[2,64]{1,0:T(2,128)} collective-permute-done((f32[2,64]{1,0:T(2,128)}, f32[2,64]{1,0:T(2,128)}, u32[]{:S(2)}, u32[]{:S(2)}) %collective-permute-start.3) | collective-permute-done | bytes 544 | tf_op jit(solution)/shard_map/ppermute | solution.py:22
  765.7 4.0 add_select_fusion.3
  775.7 8.9 multiply_reduce_fusion.25
  785.1 8.9 multiply_reduce_fusion.24
  800.6 6.8 multiply_reduce_fusion.13
  810.3 5.2 multiply_reduce_fusion.14
  816.8 13.1 fusion.144
  845.7 8.1 collective-permute-done.11
  859.0 224.5 %collective-permute-done.8 = f32[2,64]{1,0:T(2,128)S(1)} collective-permute-done((f32[2,64]{1,0:T(2,128)S(1)}, f32[2,64]{1,0:T(2,128)S(1)}, u32[]{:S(2)}, u32[]{:S(2)}) %collective-permute-start.8) | collective-permute-done | bytes 544 | tf_op jit(solution)/shard_map/ppermute | solution.py:22
  1083.5 4.8 add_select_fusion.2
  1091.0 133.0 %collective-permute-done.9 = f32[2,64]{1,0:T(2,128)S(1)} collective-permute-done((f32[2,64]{1,0:T(2,128)S(1)}, f32[2,64]{1,0:T(2,128)S(1)}, u32[]{:S(2)}, u32[]{:S(2)}) %collective-permute-start.9) | collective-permute-done | bytes 544 | tf_op jit(solution)/shard_map/ppermute | solution.py:22
  1224.0 178.0 %collective-permute-done.13 = f32[2,64,64,128]{3,2,1,0:T(8,128)} collective-permute-done((f32[2,64,64,128]{3,2,1,0:T(8,128)}, f32[2,64,64,128]{3,2,1,0:T(8,128)}, u32[]{:S(2)}, u32[]{:S(2)}) %collective-permute-start.13) | collective-permute-done | bytes 4194336 | tf_op jit(solution)/shard_map/ppermute | solution.py:22
  1402.0 6.0 add_select_fusion.1
  1419.4 6.4 multiply_multiply_fusion.7
  1432.1 4.7 fusion.183
  1438.4 163.3 %collective-permute-done.14 = f32[2,64,64,128]{3,2,1,0:T(8,128)} collective-permute-done((f32[2,64,64,128]{3,2,1,0:T(8,128)}, f32[2,64,64,128]{3,2,1,0:T(8,128)}, u32[]{:S(2)}, u32[]{:S(2)}) %collective-permute-start.14) | collective-permute-done | bytes 4194336 | tf_op jit(solution)/shard_map/ppermute | solution.py:22
  1601.7 4.0 add_select_fusion
  1609.0 6.2 multiply_reduce_fusion.21
  1615.3 4.1 multiply_reduce_fusion.19
  1619.5 3.8 multiply_reduce_fusion.10
  1623.4 10.2 fusion.91
  1633.7 7.3 multiply_reduce_fusion.20
  1642.5 10.8 fusion.93
  1665.3 5.7 fusion.160
  1671.1 5.2 fusion.159
  1680.0 5.8 fusion.156
  1685.9 7.9 multiply_reduce_fusion.9
  1701.0 25.7 fusion.100
  1729.2 681.8 %reduce-scatter.5.cloned.1.call-done = f32[256,8512]{0,1:T(8,128)} async-done(((f32[2048,8512]{0,1:T(8,128)}), f32[256,8512]{0,1:T(8,128)}) %reduce-scatter.5.cloned.1.call-update) | async-done | bytes 8716304 | tf_op jit(solution)/shard_map/reduce_scatter | solution.py:318
  2412.3 11.9 fusion.17
  2424.3 17.5 fusion.52
  2441.8 39.0 %all-reduce.27 = (f32[2048]{0:T(1024)}, f32[4352]{0:T(1024)}, f32[64]{0:T(128)}, f32[64]{0:T(128)}, f32[64]{0:T(128)}, /*index=5*/f32[4096]{0:T(1024)}) all-reduce(f32[2048]{0:T(1024)S(1)} %get-tuple-element.45, f32[4352]{0:T(1024)S(1)} %add.376, f32[64]{0:T(128)S(1)} %add.377, ...), channel_id=1, replica_groups=mesh['width'=4,'seq'=8] {'width','seq'}, use_global_device_ids=true, to_apply=%region_35.37 | all-reduce | flops 10688 | bytes 85504 | tf_op jit(solution)/shard_map/psum | solution.py:325
  2484.4 48.8 %all-reduce.30.cloned.1.call-done = f32[4,4352]{1,0:T(4,128)} async-done(((f32[4,4352]{1,0:T(4,128)}), f32[4,4352]{1,0:T(4,128)}) %all-reduce.30.cloned.1.call-update) | async-done | bytes 69648 | tf_op jit(solution)/shard_map/psum | solution.py:325
  2533.2 58.4 %reduce-scatter.11.cloned.1.call-done = f32[1024,256]{1,0:T(8,128)} async-done(((f32[4096,256]{1,0:T(8,128)}), f32[1024,256]{1,0:T(8,128)}) %reduce-scatter.11.cloned.1.call-update) | async-done | bytes 1048592 | tf_op jit(solution)/shard_map/reduce_scatter | solution.py:323
  2591.6 93.2 %reduce-scatter.7.cloned.1.call-done = f32[256,2128]{0,1:T(8,128)} async-done(((f32[256,8512]{0,1:T(8,128)}), f32[256,2128]{0,1:T(8,128)}) %reduce-scatter.7.cloned.1.call-update) | async-done | bytes 2179088 | tf_op jit(solution)/shard_map/reduce_scatter | solution.py:322
  (423 shorter events, 159.4 us)
Async XLA Ops:
  7.2 308.9 %all-gather.3.cloned.1.call-start = ((), (), s32[]{:S(2)}) async-start(), calls=%async_computation.4 | async-start | bytes 39223296 | tf_op jit(solution)/shard_map/all_gather | solution.py:181
  8.0 670.7 %all-gather.5.cloned.1.call-start = ((), (), s32[]{:S(2)}) async-start(), calls=%async_computation.5 | async-start | bytes 18874368 | tf_op jit(solution)/shard_map/all_gather | solution.py:182
  8.7 1719.7 %reduce-scatter.9.cloned.1.call-start = ((), (), s32[]{:S(2)}) async-start(), calls=%async_computation.9 | async-start | bytes 37748736 | tf_op jit(solution)/shard_map/reduce_scatter | solution.py:319
  8.8 337.5 %copy-start.103 = (f32[64]{0:T(128)}, f32[64]{0:T(128)S(1)}, u32[]{:S(2)}) copy-start(f32[64]{0:T(128)S(1)} %exp.51) | copy-start | bytes 772
  10.0 345.8 %copy-start.49 = (f32[4352]{0:T(1024)}, f32[4352]{0:T(1024)S(1)}, u32[]{:S(2)}) copy-start(f32[4352]{0:T(1024)S(1)} %get-tuple-element.49) | copy-start | bytes 52228
  10.0 345.8 %copy-start.51 = (f32[4352]{0:T(1024)}, f32[4352]{0:T(1024)S(1)}, u32[]{:S(2)}) copy-start(f32[4352]{0:T(1024)S(1)} %get-tuple-element.50) | copy-start | bytes 52228
  10.0 345.8 %copy-start.53 = (f32[4352]{0:T(1024)}, f32[4352]{0:T(1024)S(1)}, u32[]{:S(2)}) copy-start(f32[4352]{0:T(1024)S(1)} %get-tuple-element.51) | copy-start | bytes 52228
  10.0 345.8 %copy-start.55 = (f32[4352]{0:T(1024)}, f32[4352]{0:T(1024)S(1)}, u32[]{:S(2)}) copy-start(f32[4352]{0:T(1024)S(1)} %get-tuple-element.52) | copy-start | bytes 52228
  10.3 325.4 %copy-start.79 = (f32[2,128]{1,0:T(2,128)}, f32[2,128]{1,0:T(2,128)S(1)}, u32[]{:S(2)}) copy-start(f32[2,128]{1,0:T(2,128)S(1)} %fusion.53) | copy-start | bytes 3076
  10.3 325.4 %copy-start.77 = (f32[256]{0:T(256)}, f32[256]{0:T(256)S(1)}, u32[]{:S(2)}) copy-start(f32[256]{0:T(256)S(1)} %bitcast_rsqrt_fusion) | copy-start | bytes 3076
  10.3 345.4 %copy-start.86 = (f32[128]{0:T(128)}, f32[128]{0:T(128)S(1)}, u32[]{:S(2)}) copy-start(f32[128]{0:T(128)S(1)} %get-tuple-element.133) | copy-start | bytes 1540
  10.3 345.4 %copy-start.88 = (f32[128]{0:T(128)}, f32[128]{0:T(128)S(1)}, u32[]{:S(2)}) copy-start(f32[128]{0:T(128)S(1)} %get-tuple-element.134) | copy-start | bytes 1540
  10.3 345.4 %copy-start.90 = (f32[128]{0:T(128)}, f32[128]{0:T(128)S(1)}, u32[]{:S(2)}) copy-start(f32[128]{0:T(128)S(1)} %get-tuple-element.135) | copy-start | bytes 1540
  10.4 345.4 %copy-start.92 = (f32[128]{0:T(128)}, f32[128]{0:T(128)S(1)}, u32[]{:S(2)}) copy-start(f32[128]{0:T(128)S(1)} %get-tuple-element.136) | copy-start | bytes 1540
  10.4 345.4 %copy-start.94 = (f32[128]{0:T(128)}, f32[128]{0:T(128)S(1)}, u32[]{:S(2)}) copy-start(f32[128]{0:T(128)S(1)} %get-tuple-element.137) | copy-start | bytes 1540
  10.4 345.4 %copy-start.96 = (f32[128]{0:T(128)}, f32[128]{0:T(128)S(1)}, u32[]{:S(2)}) copy-start(f32[128]{0:T(128)S(1)} %get-tuple-element.138) | copy-start | bytes 1540
  10.6 339.7 %copy-start.46 = (f32[128,128]{1,0:T(8,128)}, f32[128,128]{1,0:T(8,128)S(1)}, u32[]{:S(2)}) copy-start(f32[128,128]{1,0:T(8,128)S(1)} %get-tuple-element.130) | copy-start | bytes 196612
  10.6 339.7 %copy-start.67 = (pred[128,128]{1,0:T(8,128)(4,1)}, pred[128,128]{1,0:T(8,128)(4,1)S(1)}, u32[]{:S(2)}) copy-start(pred[128,128]{1,0:T(8,128)(4,1)S(1)} %get-tuple-element.129) | copy-start | bytes 49156
  10.9 324.7 %copy-start.29 = (bf16[256,2048]{1,0:T(8,128)(2,1)}, bf16[256,2048]{1,0:T(8,128)(2,1)S(1)}, u32[]{:S(2)}) copy-start(bf16[256,2048]{1,0:T(8,128)(2,1)S(1)} %fusion.51) | copy-start | bytes 3145732
  343.2 12.0 collective-permute-start
  377.7 9.0 collective-permute-start.4
  389.5 132.5 %collective-permute-start.5 = (f32[2,64,64,128]{3,2,1,0:T(8,128)}, f32[2,64,64,128]{3,2,1,0:T(8,128)}, u32[]{:S(2)}, u32[]{:S(2)}) collective-permute-start(f32[2,64,64,128]{3,2,1,0:T(8,128)} %broadcast_select_fusion.1), channel_id=1, source_target_pairs={{0,1},{1,2},{2,3},{3,4},{4,5},{5,6},{6,7},{8,9},{9,10},{10,11},{11... | collective-permute-start | bytes 12582920 | tf_op jit(solution)/shard_map/ppermute | solution.py:22
  517.6 3.9 collective-permute-start.1
  526.7 136.0 %collective-permute-start.6 = (f32[2,64,64,128]{3,2,1,0:T(8,128)}, f32[2,64,64,128]{3,2,1,0:T(8,128)}, u32[]{:S(2)}, u32[]{:S(2)}) collective-permute-start(f32[2,64,64,128]{3,2,1,0:T(8,128)} %add_select_fusion.5), channel_id=1, source_target_pairs={{0,2},{1,3},{2,4},{3,5},{4,6},{5,7},{8,10},{9,11},{10,12},{11,13},... | collective-permute-start | bytes 12582920 | tf_op jit(solution)/shard_map/ppermute | solution.py:22
  575.3 2.1 collective-permute-start.2
  577.9 100.7 %copy-start.31 = (bf16[1,2,128,2048]{3,2,1,0:T(8,128)(2,1)S(1)}, bf16[1,2,128,2048]{3,2,1,0:T(8,128)(2,1)}, u32[]{:S(2)}) copy-start(bf16[1,2,128,2048]{3,2,1,0:T(8,128)(2,1)} %param.24) | copy-start | bytes 3145732
  668.6 97.1 %collective-permute-start.7 = (f32[2,64,64,128]{3,2,1,0:T(8,128)}, f32[2,64,64,128]{3,2,1,0:T(8,128)}, u32[]{:S(2)}, u32[]{:S(2)}) collective-permute-start(f32[2,64,64,128]{3,2,1,0:T(8,128)} %add_select_fusion.4), channel_id=1, source_target_pairs={{0,4},{1,5},{2,6},{3,7},{8,12},{9,13},{10,14},{11,15},{16,20},{17,... | collective-permute-start | bytes 12582920 | tf_op jit(solution)/shard_map/ppermute | solution.py:22
  690.9 71.8 %collective-permute-start.3 = (f32[2,64]{1,0:T(2,128)}, f32[2,64]{1,0:T(2,128)}, u32[]{:S(2)}, u32[]{:S(2)}) collective-permute-start(f32[2,64]{1,0:T(2,128)} %multiply_select_fusion.5), channel_id=1, source_target_pairs={{0,2},{1,3},{2,4},{3,5},{4,6},{5,7},{8,10},{9,11},{10,12},{11,13},... | collective-permute-start | bytes 1544 | tf_op jit(solution)/shard_map/ppermute | solution.py:22
  765.7 19.4 copy-start.44
  772.6 12.0 copy-start.25
  830.0 1581.0 %reduce-scatter.5.cloned.1.call-start = ((), (), s32[]{:S(2)}) async-start(), calls=%async_computation.6 | async-start | bytes 78446592 | tf_op jit(solution)/shard_map/reduce_scatter | solution.py:318
  844.4 9.4 collective-permute-start.11
  845.7 12.0 copy-start.114
  856.4 227.1 %collective-permute-start.12 = (f32[2,64,64,128]{3,2,1,0:T(8,128)S(1)}, f32[2,64,64,128]{3,2,1,0:T(8,128)S(1)}, u32[]{:S(2)}, u32[]{:S(2)}) collective-permute-start(f32[2,64,64,128]{3,2,1,0:T(8,128)S(1)} %broadcast_select_fusion), channel_id=1, source_target_pairs={{1,0},{2,1},{3,2},{4,3},{5,4},{6,5},{7,6},{9,8},{10,9},{11,10},{12... | collective-permute-start | bytes 12582920 | tf_op jit(solution)/shard_map/ppermute | solution.py:22
  857.7 225.8 %collective-permute-start.8 = (f32[2,64]{1,0:T(2,128)S(1)}, f32[2,64]{1,0:T(2,128)S(1)}, u32[]{:S(2)}, u32[]{:S(2)}) collective-permute-start(f32[2,64]{1,0:T(2,128)S(1)} %copy-done.114), channel_id=1, source_target_pairs={{1,0},{2,1},{3,2},{4,3},{5,4},{6,5},{7,6},{9,8},{10,9},{11,10},{12... | collective-permute-start | bytes 1544 | tf_op jit(solution)/shard_map/ppermute | solution.py:22
  1088.4 313.6 %collective-permute-start.13 = (f32[2,64,64,128]{3,2,1,0:T(8,128)}, f32[2,64,64,128]{3,2,1,0:T(8,128)}, u32[]{:S(2)}, u32[]{:S(2)}) collective-permute-start(f32[2,64,64,128]{3,2,1,0:T(8,128)} %add_select_fusion.2), channel_id=1, source_target_pairs={{2,0},{3,1},{4,2},{5,3},{6,4},{7,5},{10,8},{11,9},{12,10},{13,11},... | collective-permute-start | bytes 12582920 | tf_op jit(solution)/shard_map/ppermute | solution.py:22
  1089.7 134.3 %collective-permute-start.9 = (f32[2,64]{1,0:T(2,128)S(1)}, f32[2,64]{1,0:T(2,128)S(1)}, u32[]{:S(2)}, u32[]{:S(2)}) collective-permute-start(f32[2,64]{1,0:T(2,128)S(1)} %broadcast_select_fusion.2), channel_id=1, source_target_pairs={{1,0},{2,1},{3,2},{4,3},{5,4},{6,5},{7,6},{9,8},{10,9},{11,10},{12... | collective-permute-start | bytes 1544 | tf_op jit(solution)/shard_map/ppermute | solution.py:22
  1407.9 193.8 %collective-permute-start.14 = (f32[2,64,64,128]{3,2,1,0:T(8,128)}, f32[2,64,64,128]{3,2,1,0:T(8,128)}, u32[]{:S(2)}, u32[]{:S(2)}) collective-permute-start(f32[2,64,64,128]{3,2,1,0:T(8,128)} %add_select_fusion.1), channel_id=1, source_target_pairs={{4,0},{5,1},{6,2},{7,3},{12,8},{13,9},{14,10},{15,11},{20,16},{21,... | collective-permute-start | bytes 12582920 | tf_op jit(solution)/shard_map/ppermute | solution.py:22
  1409.2 10.2 collective-permute-start.10
  1438.4 167.4 %copy-start.10 = (f32[128,4096]{0,1:T(8,128)S(1)}, f32[128,4096]{0,1:T(8,128)}, u32[]{:S(2)}) copy-start(f32[128,4096]{0,1:T(8,128)} %copy.203) | copy-start | bytes 6291460
  1671.1 14.7 slice-start
  1697.2 3.3 collective-permute-start.15
  1726.7 806.5 %all-reduce.30.cloned.1.call-start = ((), (), s32[]{:S(2)}) async-start(), calls=%async_computation.8 | async-start | bytes 139264 | tf_op jit(solution)/shard_map/psum | solution.py:325
  1728.4 863.2 %reduce-scatter.11.cloned.1.call-start = ((), (), s32[]{:S(2)}) async-start(), calls=%async_computation.10 | async-start | bytes 5242880 | tf_op jit(solution)/shard_map/reduce_scatter | solution.py:323
  1729.0 955.8 %reduce-scatter.7.cloned.1.call-start = ((), (), s32[]{:S(2)}) async-start(), calls=%async_computation.7 | async-start | bytes 10895360 | tf_op jit(solution)/shard_map/reduce_scatter | solution.py:322
  2412.3 12.0 copy-start.75
  2412.3 12.0 copy-start.78
  2424.3 56.5 %copy-start.80 = (f32[2,128]{1,0:T(2,128)S(1)}, f32[2,128]{1,0:T(2,128)}, u32[]{:S(2)}) copy-start(f32[2,128]{1,0:T(2,128)} %copy-done.79) | copy-start | bytes 3076
  (100 other events, 550.0 us)
Sparse Core Ops, SparseCore 0:
  9.6 306.3 all-gather.2
  317.7 186.5 all-gather.4
  830.1 597.2 reduce-scatter.8
  1726.9 684.0 reduce-scatter.4
  2416.9 116.2 all-reduce.29
  2536.6 54.9 reduce-scatter.10
  2595.6 89.0 reduce-scatter.6
where the time goes:
time: 2700 us; the launch traced here: 2690 us
  waiting for transfers between devices  2050 us (76%)
  starting transfers between devices  207 us (8%)
  matrix products  202 us (7%)
  other arithmetic  105 us (4%)
  local copies, waits for them, and re-layouts  73.9 us (3%)
  blocking collectives  39 us (1%)
    ppermute x16, waiting for transfers between devices, shifted(): lax.ppermute(value, axis, [(source, source + steps) for source in range(f...  861 us
    reduce_scatter x1, waiting for transfers between devices, per_device(): lax.psum_scatter(grad_in_w, 'seq', scatter_dimension=0, tiled=True)  682 us
    all_gather x1, waiting for transfers between devices, per_device(): lax.all_gather(in_weight, 'seq', axis=0, tiled=True)  305 us
    ppermute x16, starting transfers between devices, shifted(): lax.ppermute(value, axis, [(source, source + steps) for source in range(f...  206 us
    reduce_scatter x1, waiting for transfers between devices, per_device(): lax.psum_scatter(rows_in, 'width', scatter_dimension=1, tiled=True)  93.2 us
    reduce_scatter x1, waiting for transfers between devices, per_device(): lax.psum_scatter(rows_out, 'width', scatter_dimension=0, tiled=True)  58.4 us
  transfers between devices with their start and end apart: 23, of which 17 were waited for; matrix products, arithmetic and copies ran while one was open for 12% of the time, Pallas kernels for 0%

commit v1 on v0

v1 whole, which is shorter than its diff:
```python
from functools import partial

import jax
import jax.numpy as jnp
from jax import lax
from jax.experimental import pallas as pl
from jax.experimental.pallas import tpu as pltpu
from jax.sharding import PartitionSpec as P

INNER = 4096
HEADS = 64
HEAD_DIM = 64
STATE = 128
CONV = 4352
EPSILON = 1e-05
LANES = 128
TAPS = 4
NEG = -1e30
F32 = jnp.float32
BF16 = jnp.bfloat16


def mm(a, b):
    return lax.dot_general(a, b, (((1,), (0,)), ((), ())), preferred_element_type=F32)


def mm_nt(a, b):
    return lax.dot_general(a, b, (((1,), (1,)), ((), ())), preferred_element_type=F32)


def mm_tn(a, b):
    return lax.dot_general(a, b, (((0,), (0,)), ((), ())), preferred_element_type=F32)


def halves(value, axis):
    high = value.astype(BF16)
    low = (value - high.astype(F32)).astype(BF16)
    return jnp.concatenate([high, low], axis=axis)


def sigmoid(value):
    return 0.5 * jnp.tanh(0.5 * value) + 0.5


def prefix_sum(tri, value):
    high = value.astype(BF16)
    rest = value - high.astype(F32)
    middle = rest.astype(BF16)
    low = (rest - middle.astype(F32)).astype(BF16)
    parts = mm(tri, jnp.concatenate([high, middle, low], axis=1))
    width = value.shape[1]
    return parts[:, :width] + parts[:, width : 2 * width] + parts[:, 2 * width :]


def doc_number(starts_ref, micro, positions):
    count = jnp.zeros_like(positions)
    for item in range(starts_ref.shape[1]):
        count = count + (starts_ref[micro, item] <= positions).astype(jnp.int32)
    return count


class Chunk:
    def __init__(self, starts_ref, micro, chunk, rows, raw_dt, head_ref, expand, tri):
        first = chunk * rows
        column = lax.broadcasted_iota(jnp.int32, (rows, 1), 0) + first
        line = lax.broadcasted_iota(jnp.int32, (1, rows), 1) + first
        doc_col = doc_number(starts_ref, micro, column)
        doc_row = doc_number(starts_ref, micro, line)
        self.same = [
            (doc_number(starts_ref, micro, column - offset) == doc_col).astype(F32)
            for offset in range(1, TAPS)
        ]
        before = jnp.int32(0)
        last = jnp.int32(0)
        for item in range(starts_ref.shape[1]):
            before = before + (starts_ref[micro, item] <= first - 1).astype(jnp.int32)
            last = last + (starts_ref[micro, item] <= first + rows - 1).astype(jnp.int32)
        carry = (doc_col == before).astype(F32)
        same_last = (doc_col == last).astype(F32)
        self.bias = jnp.where((column >= line) & (doc_col == doc_row), 0.0, NEG)
        self.shifted_dt = raw_dt + head_ref[0:1]
        self.step = jnp.maximum(self.shifted_dt, 0.0) + jnp.log1p(
            jnp.exp(-jnp.abs(self.shifted_dt))
        )
        self.log_keep = self.step * head_ref[1:2]
        self.cum = prefix_sum(tri, self.log_keep)
        self.cum_t = self.cum.T
        carried = jnp.exp(self.cum) * carry
        left = jnp.exp(self.cum[rows - 1 :] - self.cum) * same_last
        spread = mm(
            halves(jnp.concatenate([self.step, carried, left], axis=0), 1), expand
        )
        self.step_cols = spread[:rows]
        self.carry_cols = spread[rows : 2 * rows]
        self.left_cols = spread[2 * rows :]
        self.keep_all = self.carry_cols[rows - 1 :]

    def decay(self, head):
        return jnp.exp(self.cum[:, head : head + 1] - self.cum_t[head : head + 1] + self.bias)


def head_groups(heads):
    size = 2 if heads % 2 == 0 else 1
    return size, heads // size


def stacked(value, size):
    if size == 1:
        return value.astype(BF16)
    lane = lax.broadcasted_iota(jnp.int32, value.shape, 1)
    first = jnp.where(lane < HEAD_DIM, value, 0.0)
    second = jnp.where(lane < HEAD_DIM, 0.0, value)
    return jnp.concatenate([first, second], axis=0).astype(BF16)


def convolved(ext, micro, rows, taps_ref, same):
    current = ext[micro, 8 : 8 + rows, :]
    total = taps_ref[TAPS : TAPS + 1] + taps_ref[TAPS - 1 : TAPS] * current
    views = []
    for offset in range(1, TAPS):
        view = ext[micro, 8 - offset : 8 - offset + rows, :] * same[offset - 1]
        views.append(view)
        total = total + taps_ref[TAPS - 1 - offset : TAPS - offset] * view
    return current, views, total


def forward_kernel(
    micros,
    heads,
    starts_ref,
    proj_ref,
    dnorm_ref,
    taps_ref,
    head_ref,
    cols_ref,
    expand_ref,
    tri_ref,
    gg_ref,
    mixed_ref,
    states_ref,
    tails_ref,
    sums_ref,
    ext,
    state,
):
    chunk = pl.program_id(0)
    rows = proj_ref.shape[0] // micros
    width = heads * HEAD_DIM
    conv_width = 2 * STATE + width
    size, groups = head_groups(heads)

    @pl.when(chunk == 0)
    def _():
        ext[:, :8, :] = jnp.zeros((micros, 8, conv_width), F32)
        state[...] = jnp.zeros_like(state)

    skip, gain, mask = cols_ref[0:1], cols_ref[1:2], cols_ref[2:3]
    sums = []
    for micro in range(micros):
        part = slice(micro * rows, (micro + 1) * rows)
        tails_ref[micro] = ext[micro, :8, :]
        ext[micro, 8 : 8 + rows, :] = proj_ref[part, :conv_width].astype(F32)
        raw_dt = proj_ref[part, conv_width + width :].astype(F32)
        at = Chunk(
            starts_ref, micro, chunk, rows, raw_dt, head_ref, expand_ref[...], tri_ref[...]
        )
        conv = convolved(ext, micro, rows, taps_ref, at.same)[2]
        act = conv * sigmoid(conv)
        write = act[:, :STATE].astype(BF16)
        read = act[:, STATE : 2 * STATE].astype(BF16)
        x_heads = act[:, 2 * STATE :]
        scores = mm_nt(read, write)
        inputs = x_heads * at.step_cols
        state_in = state[micro]
        state_low = state_in.astype(BF16)
        states_ref[micro] = state_low
        outs = []
        for group in range(groups):
            matrices = [
                (at.decay(group * size + item) * scores).astype(BF16) for item in range(size)
            ]
            span = slice(group * size * HEAD_DIM, (group + 1) * size * HEAD_DIM)
            outs.append(mm(jnp.concatenate(matrices, axis=1), stacked(inputs[:, span], size)))
        mixed = jnp.concatenate(outs, axis=1) + at.carry_cols * mm(read, state_low)
        state[micro] = at.keep_all * state_in + mm_tn(
            write, (inputs * at.left_cols).astype(BF16)
        )
        mixed = mixed + skip * x_heads
        mixed_ref[part, :] = mixed
        gate = proj_ref[part, conv_width : conv_width + width].astype(F32)
        gated = mask * mixed * (gate * sigmoid(gate))
        gg_ref[part, :] = (gated * gain).astype(BF16)
        square = jnp.sum(gated * gated, axis=1, keepdims=True)
        cross = jnp.sum(dnorm_ref[part, :] * gain * gated, axis=1, keepdims=True)
        lane = lax.broadcasted_iota(jnp.int32, (rows, LANES), 1)
        both = jnp.where(lane == 0, square, jnp.where(lane == 1, cross, 0.0))
        sums.append(both.T[:2])
        ext[micro, :8, :] = ext[micro, rows : rows + 8, :]
    pad = sums_ref.shape[0] - 2 * micros
    if pad:
        sums.append(jnp.zeros((pad, rows), F32))
    sums_ref[...] = jnp.concatenate(sums, axis=0)


def backward_kernel(
    micros,
    heads,
    starts_ref,
    active_ref,
    proj_ref,
    dnorm_ref,
    mixed_ref,
    states_ref,
    tails_ref,
    sums_ref,
    taps_ref,
    head_ref,
    cols_ref,
    expand_ref,
    gather_ref,
    tri_ref,
    dproj_ref,
    gnorm_ref,
    gconv_ref,
    gcols_ref,
    ghead_ref,
    ext,
    heads_ext,
    dstate,
):
    chunks = pl.num_programs(0)
    step_index = pl.program_id(0)
    chunk = chunks - 1 - step_index
    rows = proj_ref.shape[0] // micros
    width = heads * HEAD_DIM
    conv_width = 2 * STATE + width
    size, groups = head_groups(heads)

    @pl.when(step_index == 0)
    def _():
        heads_ext[:, :, rows:, :] = jnp.zeros((micros, TAPS - 1, 8, conv_width), F32)
        dstate[...] = jnp.zeros_like(dstate)
        gconv_ref[...] = jnp.zeros_like(gconv_ref)
        gcols_ref[...] = jnp.zeros_like(gcols_ref)
        ghead_ref[...] = jnp.zeros_like(ghead_ref)

    skip, gain, mask = cols_ref[0:1], cols_ref[1:2], cols_ref[2:3]
    tri = tri_ref[...]
    gather = gather_ref[...]
    inverse_active = 1.0 / active_ref[0]
    sums = jnp.concatenate(
        [sums_ref[...], jnp.zeros((LANES - sums_ref.shape[0], rows), F32)], axis=0
    ).T
    for micro in range(micros):
        part = slice(micro * rows, (micro + 1) * rows)
        ext[micro, :8, :] = tails_ref[micro]
        ext[micro, 8 : 8 + rows, :] = proj_ref[part, :conv_width].astype(F32)
        raw_dt = proj_ref[part, conv_width + width :].astype(F32)
        at = Chunk(starts_ref, micro, chunk, rows, raw_dt, head_ref, expand_ref[...], tri)
        current, views, conv = convolved(ext, micro, rows, taps_ref, at.same)
        conv_sig = sigmoid(conv)
        act = conv * conv_sig
        write = act[:, :STATE].astype(BF16)
        read = act[:, STATE : 2 * STATE].astype(BF16)
        x_heads = act[:, 2 * STATE :]
        scores = mm_nt(read, write)
        inputs = x_heads * at.step_cols

        gate = proj_ref[part, conv_width : conv_width + width].astype(F32)
        gate_sig = sigmoid(gate)
        gate_act = gate * gate_sig
        masked = mask * mixed_ref[part, :]
        gated = masked * gate_act
        root = lax.rsqrt(sums[:, 2 * micro : 2 * micro + 1] * inverse_active + EPSILON)
        pull = root * root * root * sums[:, 2 * micro + 1 : 2 * micro + 2] * inverse_active
        dnorm = dnorm_ref[part, :]
        scaled = gated * root
        gnorm_ref[part, :] = (scaled * gain).astype(BF16)
        d_gated = root * dnorm * gain - gated * pull
        d_gate = d_gated * masked * (gate_sig * (1.0 + gate * (1.0 - gate_sig)))
        d_mixed = mask * d_gated * gate_act
        gcols_ref[0:1] += jnp.sum(d_mixed * x_heads, axis=0, keepdims=True)
        gcols_ref[1:2] += jnp.sum(dnorm * scaled, axis=0, keepdims=True)

        state_low = states_ref[micro]
        d_state = dstate[micro]
        d_state_low = d_state.astype(BF16)
        from_state = (d_mixed * at.carry_cols).astype(BF16)
        left = inputs * at.left_cols
        left_low = left.astype(BF16)
        d_left = mm(write, d_state_low)
        state_out = mm(read, state_low)
        d_read = mm_nt(from_state, state_low)
        d_write = mm_nt(left_low, d_state_low)
        d_mixed_low = d_mixed.astype(BF16).astype(F32)
        inputs_low = inputs.astype(BF16).astype(F32)
        d_scores = jnp.zeros((rows, rows), F32)
        locals_out, d_locals = [], []
        for group in range(groups):
            span = slice(group * size * HEAD_DIM, (group + 1) * size * HEAD_DIM)
            decays = [at.decay(group * size + item) for item in range(size)]
            matrices = [(decay * scores).astype(BF16) for decay in decays]
            in_stack = stacked(inputs[:, span], size)
            out_stack = stacked(d_mixed[:, span], size)
            locals_out.append(mm(jnp.concatenate(matrices, axis=1), in_stack))
            d_locals.append(mm_tn(jnp.concatenate(matrices, axis=0), out_stack))
            d_matrices = mm_nt(out_stack, inputs[:, span].astype(BF16))
            for item in range(size):
                d_scores = (
                    d_scores + d_matrices[item * rows : (item + 1) * rows] * decays[item]
                )
        local_out = jnp.concatenate(locals_out, axis=1)
        d_local = jnp.concatenate(d_locals, axis=1)
        d_scores_low = d_scores.astype(BF16)
        d_read = d_read + mm(d_scores_low, write)
        d_write = d_write + mm_tn(d_scores_low, read)
        d_inputs = d_local + at.left_cols * d_left
        d_x = skip * d_mixed + d_inputs * at.step_cols

        passed = left * d_left
        cum_terms = (
            d_mixed_low * local_out
            + d_mixed * at.carry_cols * state_out
            - inputs_low * d_local
            - passed
        )
        kept = jnp.sum(d_state * at.keep_all * state_low.astype(F32), axis=0, keepdims=True)
        final = jnp.sum(passed, axis=0, keepdims=True) + kept
        stack = jnp.concatenate(
            [cum_terms, d_inputs * x_heads, jnp.broadcast_to(final, (8, width))], axis=0
        )
        reduced = mm(halves(stack, 1), gather)
        d_cum = reduced[:rows]
        d_step = reduced[rows : 2 * rows]
        final_row = reduced[2 * rows : 2 * rows + 1]
        total = jnp.sum(d_cum, axis=0, keepdims=True) + final_row
        d_log = total - prefix_sum(tri, d_cum) + d_cum
        d_step = d_step + d_log * head_ref[1:2]
        d_dt = d_step * sigmoid(at.shifted_dt)
        ghead_ref[0:1] += jnp.sum(d_log * at.log_keep, axis=0, keepdims=True)
        ghead_ref[1:2] += jnp.sum(d_dt, axis=0, keepdims=True)
        dstate[micro] = at.keep_all * d_state + mm_tn(read, from_state)

        d_conv = jnp.concatenate([d_write, d_read, d_x], axis=1) * (
            conv_sig * (1.0 + conv * (1.0 - conv_sig))
        )
        gconv_ref[TAPS : TAPS + 1] += jnp.sum(d_conv, axis=0, keepdims=True)
        gconv_ref[TAPS - 1 : TAPS] += jnp.sum(d_conv * current, axis=0, keepdims=True)
        d_raw = taps_ref[TAPS - 1 : TAPS] * d_conv
        for offset in range(1, TAPS):
            tap = TAPS - 1 - offset
            gconv_ref[tap : tap + 1] += jnp.sum(
                d_conv * views[offset - 1], axis=0, keepdims=True
            )
            heads_ext[micro, offset - 1, :rows, :] = d_conv * at.same[offset - 1]
            d_raw = d_raw + taps_ref[tap : tap + 1] * (
                heads_ext[micro, offset - 1, offset : offset + rows, :]
            )
            heads_ext[micro, offset - 1, rows:, :] = heads_ext[micro, offset - 1, :8, :]
        dproj_ref[part, :conv_width] = d_raw.astype(BF16)
        dproj_ref[part, conv_width : conv_width + width] = d_gate.astype(BF16)
        dproj_ref[part, conv_width + width :] = d_dt.astype(BF16)


def constant(shape):
    return pl.BlockSpec(shape, lambda index: (0,) * len(shape))


def run_forward(micros, heads, rows, chunks, starts, proj, dnorm, taps, head, cols, expand, tri):
    width = heads * HEAD_DIM
    conv_width = 2 * STATE + width
    block = micros * rows
    sum_rows = -(-2 * micros // 8) * 8
    return pl.pallas_call(
        partial(forward_kernel, micros, heads),
        grid=(chunks,),
        in_specs=[
            pl.BlockSpec(memory_space=pltpu.SMEM),
            pl.BlockSpec((block, proj.shape[1]), lambda index: (index, 0)),
            pl.BlockSpec((block, width), lambda index: (index, 0)),
            constant(taps.shape),
            constant(head.shape),
            constant(cols.shape),
            constant(expand.shape),
            constant(tri.shape),
        ],
        out_specs=[
            pl.BlockSpec((block, width), lambda index: (index, 0)),
            pl.BlockSpec((block, width), lambda index: (index, 0)),
            pl.BlockSpec((None, micros, STATE, width), lambda index: (index, 0, 0, 0)),
            pl.BlockSpec((None, micros, 8, conv_width), lambda index: (index, 0, 0, 0)),
            pl.BlockSpec((None, sum_rows, rows), lambda index: (index, 0, 0)),
        ],
        out_shape=[
            jax.ShapeDtypeStruct((chunks * block, width), BF16),
            jax.ShapeDtypeStruct((chunks * block, width), F32),
            jax.ShapeDtypeStruct((chunks, micros, STATE, width), BF16),
            jax.ShapeDtypeStruct((chunks, micros, 8, conv_width), F32),
            jax.ShapeDtypeStruct((chunks, sum_rows, rows), F32),
        ],
        scratch_shapes=[
            pltpu.VMEM((micros, rows + 8, conv_width), F32),
            pltpu.VMEM((micros, STATE, width), F32),
        ],
        compiler_params=pltpu.CompilerParams(vmem_limit_bytes=48 << 20),
        name="mixer_forward",
    )(starts, proj, dnorm, taps, head, cols, expand, tri)


def run_backward(
    micros,
    heads,
    rows,
    chunks,
    starts,
    active,
    proj,
    dnorm,
    mixed,
    states,
    tails,
    sums,
    taps,
    head,
    cols,
    expand,
    gather,
    tri,
):
    width = heads * HEAD_DIM
    conv_width = 2 * STATE + width
    block = micros * rows

    def back(index):
        return (chunks - 1 - index, 0)

    return pl.pallas_call(
        partial(backward_kernel, micros, heads),
        grid=(chunks,),
        in_specs=[
            pl.BlockSpec(memory_space=pltpu.SMEM),
            pl.BlockSpec(memory_space=pltpu.SMEM),
            pl.BlockSpec((block, proj.shape[1]), back),
            pl.BlockSpec((block, width), back),
            pl.BlockSpec((block, width), back),
            pl.BlockSpec(
                (None, micros, STATE, width), lambda index: (chunks - 1 - index, 0, 0, 0)
            ),
            pl.BlockSpec(
                (None, micros, 8, conv_width), lambda index: (chunks - 1 - index, 0, 0, 0)
            ),
            pl.BlockSpec((None, sums.shape[1], rows), lambda index: (chunks - 1 - index, 0, 0)),
            constant(taps.shape),
            constant(head.shape),
            constant(cols.shape),
            constant(expand.shape),
            constant(gather.shape),
            constant(tri.shape),
        ],
        out_specs=[
            pl.BlockSpec((block, proj.shape[1]), back),
            pl.BlockSpec((block, width), back),
            constant((8, conv_width)),
            constant((8, width)),
            constant((8, LANES)),
        ],
        out_shape=[
            jax.ShapeDtypeStruct((chunks * block, proj.shape[1]), BF16),
            jax.ShapeDtypeStruct((chunks * block, width), BF16),
            jax.ShapeDtypeStruct((8, conv_width), F32),
            jax.ShapeDtypeStruct((8, width), F32),
            jax.ShapeDtypeStruct((8, LANES), F32),
        ],
        scratch_shapes=[
            pltpu.VMEM((micros, rows + 8, conv_width), F32),
            pltpu.VMEM((micros, TAPS - 1, rows + 8, conv_width), F32),
            pltpu.VMEM((micros, STATE, width), F32),
        ],
        compiler_params=pltpu.CompilerParams(vmem_limit_bytes=48 << 20),
        name="mixer_backward",
    )(
        starts,
        active,
        proj,
        dnorm,
        mixed,
        states,
        tails,
        sums,
        taps,
        head,
        cols,
        expand,
        gather,
        tri,
    )


def tables(heads, rows):
    width = heads * HEAD_DIM
    expand = (
        jnp.arange(LANES)[:, None] == jnp.arange(width)[None, :] // HEAD_DIM
    ).astype(BF16)
    tri = (jnp.arange(rows)[:, None] >= jnp.arange(rows)[None, :]).astype(BF16)
    return (
        jnp.concatenate([expand, expand], axis=0),
        jnp.concatenate([expand.T, expand.T], axis=0),
        tri,
    )


def input_norm(hidden, in_gain):
    return hidden * lax.rsqrt(jnp.mean(hidden * hidden, axis=1, keepdims=True) + EPSILON) * in_gain


def own(value, start, count, axis=0):
    return lax.dynamic_slice_in_dim(value, start, count, axis)


def placed(value, total, start):
    whole = jnp.zeros(value.shape[:-1] + (total,), F32)
    return lax.dynamic_update_slice_in_dim(whole, value, start, value.ndim - 1)


def per_device(
    hidden_in,
    starts,
    in_gain,
    in_weight,
    conv_weight,
    conv_bias,
    step_bias,
    decay_log,
    skip_gain,
    gate_gain,
    out_weight,
    cotangent,
):
    seq_total = lax.axis_size("seq")
    seq_index = lax.axis_index("seq")
    group_index = lax.axis_index("width")
    micros, rows, model_width = hidden_in.shape[1:]
    heads = HEADS // seq_total
    width = heads * HEAD_DIM
    head_first = seq_index * heads
    col_first = seq_index * width
    depth = in_weight.shape[0]
    head_count = HEADS // 8 * jnp.left_shift(jnp.int32(1), group_index)
    active = head_count.astype(F32) * HEAD_DIM

    flat_hidden = hidden_in[0].reshape(micros * rows, model_width).astype(F32)
    flat_grad = cotangent[0].reshape(micros * rows, model_width)
    normed, norm_back = jax.vjp(input_norm, flat_hidden, in_gain)
    all_normed = lax.all_gather(normed.astype(BF16), "seq", axis=0, tiled=True)
    all_grad = lax.all_gather(flat_grad, "seq", axis=0, tiled=True)

    dt_pad = LANES
    gates = in_weight[:, :INNER].reshape(depth, seq_total, width)
    xs = in_weight[:, INNER : 2 * INNER].reshape(depth, seq_total, width)
    bc = jnp.broadcast_to(
        in_weight[:, None, 2 * INNER : INNER + CONV], (depth, seq_total, 2 * STATE)
    )
    dts = in_weight[:, INNER + CONV :].reshape(depth, seq_total, heads)
    dts = jnp.pad(dts, ((0, 0), (0, 0), (0, dt_pad - heads)))
    pieces = jnp.concatenate([bc, xs, gates, dts], axis=2).transpose(1, 0, 2)
    columns = lax.all_to_all(pieces, "seq", split_axis=0, concat_axis=0)
    columns = columns.reshape(seq_total * depth, columns.shape[2])

    conv_width = 2 * STATE + width

    def conv_columns(value):
        return jnp.concatenate(
            [value[..., INNER:], own(value, col_first, width, value.ndim - 1)], axis=-1
        )

    taps = jnp.concatenate(
        [
            conv_columns(conv_weight),
            conv_columns(conv_bias[None]),
            jnp.zeros((8 - TAPS - 1, conv_width), F32),
        ],
        axis=0,
    )
    head_rows = jnp.stack(
        [own(step_bias, head_first, heads), -jnp.exp(own(decay_log, head_first, heads))]
    )
    head_table = jnp.pad(head_rows, ((0, 6), (0, LANES - heads)))
    head_mask = (head_first + jnp.arange(heads, dtype=jnp.int32) < head_count).astype(F32)
    cols = jnp.stack(
        [
            jnp.repeat(own(skip_gain, head_first, heads), HEAD_DIM),
            own(gate_gain, col_first, width),
            jnp.repeat(head_mask, HEAD_DIM),
        ]
    )
    cols = jnp.pad(cols, ((0, 5), (0, 0)))
    expand, gather, tri = tables(heads, rows)

    proj = mm(all_normed, columns).astype(BF16)
    dnorm = mm_nt(all_grad, out_weight)
    gg, mixed, states, tails, sums = run_forward(
        micros, heads, rows, seq_total, starts[0], proj, dnorm, taps, head_table, cols, expand, tri
    )
    sums = lax.psum(sums, "seq")
    branch = lax.psum_scatter(
        mm(gg, out_weight).astype(BF16), "seq", scatter_dimension=0, tiled=True
    )
    squares = own(sums, seq_index, 1)[0, : 2 * micros : 2].reshape(micros * rows, 1)
    output = flat_hidden + branch.astype(F32) * lax.rsqrt(squares / active + EPSILON)

    dproj, gnorm, gconv, gcols, ghead = run_backward(
        micros,
        heads,
        rows,
        seq_total,
        starts[0],
        active[None],
        proj,
        dnorm,
        mixed,
        states,
        tails,
        sums,
        taps,
        head_table,
        cols,
        expand,
        gather,
        tri,
    )
    grad_normed = lax.psum_scatter(
        mm_nt(dproj, columns).astype(BF16), "seq", scatter_dimension=0, tiled=True
    ).astype(F32)
    grad_hidden, grad_gain_in = norm_back(grad_normed)
    hidden_grads = (flat_grad.astype(F32) + grad_hidden).astype(BF16)

    grad_out = mm_tn(gnorm, all_grad).astype(BF16)
    grad_out = grad_out.reshape(width, seq_total, model_width // seq_total).transpose(1, 0, 2)
    grad_out = lax.all_to_all(grad_out, "seq", split_axis=0, concat_axis=0)
    grad_out = grad_out.reshape(seq_total * width, model_width // seq_total)
    shard_out = lax.psum_scatter(
        grad_out.astype(F32), "width", scatter_dimension=0, tiled=True
    )

    grad_in = mm_tn(all_normed, dproj).astype(BF16)[:, : conv_width + width + heads]
    grad_in = grad_in.reshape(seq_total, depth, grad_in.shape[1])
    grad_in = lax.all_to_all(grad_in, "seq", split_axis=0, concat_axis=0)
    grad_in = grad_in.astype(F32)

    def joined(value):
        return value.transpose(1, 0, 2).reshape(depth, seq_total * value.shape[2])

    grad_in = jnp.concatenate(
        [
            joined(grad_in[:, :, conv_width : conv_width + width]),
            joined(grad_in[:, :, 2 * STATE : conv_width]),
            jnp.sum(grad_in[:, :, : 2 * STATE], axis=0),
            joined(grad_in[:, :, conv_width + width :]),
        ],
        axis=1,
    )
    shard_in = lax.psum_scatter(grad_in, "width", scatter_dimension=1, tiled=True)

    skip_heads = jnp.sum(gcols[0].reshape(heads, HEAD_DIM), axis=1)
    conv_small = jnp.concatenate(
        [placed(gconv[:5, 2 * STATE :], INNER, col_first), gconv[:5, : 2 * STATE]], axis=1
    )
    small = jnp.concatenate(
        [
            conv_small.reshape(-1),
            grad_gain_in,
            placed(gcols[1], INNER, col_first),
            placed(ghead[1, :heads], HEADS, head_first),
            placed(ghead[0, :heads], HEADS, head_first),
            placed(skip_heads, HEADS, head_first),
        ]
    )
    small = lax.psum(small, ("width", "seq"))
    edge = 5 * CONV
    conv_small = small[:edge].reshape(5, CONV)
    in_gain_sum = small[edge : edge + model_width]
    edge = edge + model_width
    gain_sum = small[edge : edge + INNER]
    edge = edge + INNER
    shape = hidden_in.shape
    return (
        output.astype(BF16).reshape(shape),
        hidden_grads.reshape(shape),
        in_gain_sum,
        shard_in,
        conv_small[:4],
        conv_small[4],
        small[edge : edge + HEADS],
        small[edge + HEADS : edge + 2 * HEADS],
        small[edge + 2 * HEADS : edge + 3 * HEADS],
        gain_sum,
        shard_out,
    )


def solution(mesh):
    in_specs = (
        P("width", None, "seq", None),
        P("width", None, None),
        P(),
        P("seq", None),
        P(),
        P(),
        P(),
        P(),
        P(),
        P(),
        P("seq", None),
        P("width", None, "seq", None),
    )
    out_specs = (
        P("width", None, "seq", None),
        P("width", None, "seq", None),
        P(),
        P("seq", "width"),
        P(),
        P(),
        P(),
        P(),
        P(),
        P(),
        P("width", "seq"),
    )
    return jax.shard_map(
        per_device, mesh=mesh, in_specs=in_specs, out_specs=out_specs, check_vma=False
    )
```

time: 2700 us -> 1030 us (0.38)
  waiting for transfers between devices: 2050 us -> 748 us
  starting transfers between devices: 207 us -> 15.6 us
  matrix products: 202 us -> 79.4 us
  other arithmetic: 105 us -> 34.4 us
  Pallas kernels: 0 us -> 63.4 us
  local copies, waits for them, and re-layouts: 73.9 us -> 38.4 us
    ppermute x16 -> x0, waiting for transfers between devices: 861 us -> none  [shifted(): lax.ppermute(value, axis, [(source, source + steps) for source in range(f...]
    reduce_scatter x4, waiting for transfers between devices: 833 us -> 177 us  [the longest x1 93.2 us: per_device(): lax.psum_scatter(grad_in, 'width', scatter_dimension=1, tiled=True)]
    all_to_all x0 -> x3, waiting for transfers between devices: none -> 443 us  [the longest x1 234 us: per_device(): columns = lax.all_to_all(pieces, 'seq', split_axis=0, concat_axis=0)]
    all_gather x2, waiting for transfers between devices: 305 us -> 0.01 us  [the longest x1 0.01 us: per_device(): all_normed = lax.all_gather(normed.astype(BF16), 'seq', axis=0, tiled=True)]
    ppermute x16 -> x0, starting transfers between devices: 206 us -> none  [shifted(): lax.ppermute(value, axis, [(source, source + steps) for source in range(f...]
    dot_general x30 -> x6, matrix products: 202 us -> 79.4 us  [the longest x2 28.1 us: mm_nt(): lax.dot_general(a, b, (((1,), (1,)), ((), ())), preferred_element_type=F32)]
    psum x1, waiting for transfers between devices: 48.8 us -> 127 us  [per_device(): small = lax.psum(small, ('width', 'seq'))]
    pallas_call x0 -> x2, Pallas kernels: none -> 63.4 us  [the longest x1 42.6 us: run_backward(): pl.pallas_call(partial(backward_kernel, micros, heads), grid=(chunks,), i...]
  transfers between devices with their start and end apart: 23 -> 10, of which waited for: 17 -> 8; matrix products, arithmetic and copies ran while one was open for 12% -> 11% of each run, Pallas kernels for 0% -> 0%
where the time goes in v1:
time: 1030 us; the launch traced here: 1020 us
  waiting for transfers between devices  748 us (73%)
  matrix products  79.4 us (8%)
  Pallas kernels  63.4 us (6%)
  local copies, waits for them, and re-layouts  38.4 us (4%)
  other arithmetic  34.4 us (3%)
  blocking collectives  26.1 us (3%)
  starting transfers between devices  15.6 us (2%)
  between operations  14.9 us (1%)
    all_to_all x1, waiting for transfers between devices, per_device(): columns = lax.all_to_all(pieces, 'seq', split_axis=0, concat_axis=0)  234 us
    all_to_all x1, waiting for transfers between devices, per_device(): grad_in = lax.all_to_all(grad_in, 'seq', split_axis=0, concat_axis=0)  146 us
    psum x1, waiting for transfers between devices, per_device(): small = lax.psum(small, ('width', 'seq'))  127 us
    reduce_scatter x1, waiting for transfers between devices, per_device(): lax.psum_scatter(grad_in, 'width', scatter_dimension=1, tiled=True)  93.2 us
    all_to_all x1, waiting for transfers between devices, per_device(): grad_out = lax.all_to_all(grad_out, 'seq', split_axis=0, concat_axis=0)  63.8 us
    reduce_scatter x1, waiting for transfers between devices, per_device(): lax.psum_scatter(grad_out.astype(F32), 'width', scatter_dimension=0, tile...  50 us
    pallas_call x1, Pallas kernels, run_backward(): pl.pallas_call(partial(backward_kernel, micros, heads), grid=(chunks,), i...  42.6 us
    dot_general x2, matrix products, mm_nt(): lax.dot_general(a, b, (((1,), (1,)), ((), ())), preferred_element_type=F32)  28.1 us
  transfers between devices with their start and end apart: 10, of which 8 were waited for; matrix products, arithmetic and copies ran while one was open for 11% of the time, Pallas kernels for 0%

profile of v1, /device:TPU:0, one launch (start us, length us, event | category | flops | bytes accessed | tf_op | source)
XLA Modules:
  0.0 1020.3 jit_solution(5225602954240746481)
XLA Ops:
  7.2 1.6 fusion.11
  10.0 2.5 fusion.10
  12.6 0.7 all-gather.5.cloned.1.call-update
  13.3 2.6 fusion.18
  16.0 0.8 slice-done.1
  16.9 5.9 fusion.2
  22.8 6.5 all-to-all-start
  29.8 0.8 dynamic_slice.26
  31.2 234.0 %all-to-all-done = bf16[8,256,1408]{1,2,0:T(8,128)(2,1)} async-done(((bf16[8,256,1408]{1,2,0:T(8,128)(2,1)}), bf16[8,256,1408]{1,2,0:T(8,128)(2,1)}, u32[]{:S(2)}, u32[]{:S(2)}) %all-to-all-start) | async-done | bytes 5767200 | tf_op jit(solution)/shard_map/all_to_all | solution.py:566
  265.2 8.3 copy.37
  273.4 18.3 %convolution_convert_fusion.2.proj_ref = bf16[2048,1408]{1,0:T(8,128)(2,1)} fusion(bf16[2048,2048]{1,0:T(8,128)(2,1)} %all-gather.3.cloned.1.call-done, bf16[2048,1408]{1,0:T(8,128)(2,1)} %bitcast.93), kind=kOutput, calls=%fused_computation.6 | convolution fusion | flops 11814043648 | bytes 19922944 | tf_op jit(solution)/shard_map/dot_general | solution.py:24
  291.8 9.6 fusion.20.dnorm_ref
  301.4 20.8 %mixer_forward.1 = (bf16[2048,512]{1,0:T(8,128)(2,1)S(1)}, f32[2048,512]{1,0:T(8,128)}, bf16[8,2,128,512]{3,2,1,0:T(8,128)(2,1)S(1)}, f32[8,2,8,768]{3,2,1,0:T(8,128)S(1)}, f32[8,8,128]{2,1,0:T(8,128)S(1)}) custom-call(s32[2,4]{1,0:T(2,128)S(1)} %bitcast.84, bf16[2048,1408]{1,0:T(8,128)(2,1)} %convolution_convert_fusion.2.proj_ref, ...), custom_call_target="tpu_custom_call" | custom-call | tf_op jit(solution)/shard_map/mixer_forward/pallas_call | solution.py:374
  322.2 1.3 copy-done.2
  323.5 1.3 copy-done.7
  324.8 26.1 %psum.14.sums_ref = f32[8,8,128]{2,1,0:T(8,128)S(1)} all-reduce(f32[8,8,128]{2,1,0:T(8,128)S(1)} %get-tuple-element.22), channel_id=1, replica_groups=mesh['width'=4,'seq'=8] {'seq'}, use_global_device_ids=true, to_apply=%region_2.3 | all-reduce | flops 8192 | bytes 65536 | tf_op jit(solution)/shard_map/psum | solution.py:604
  350.9 1.6 copy-done.3
  352.5 42.6 %mixer_backward.1 = (bf16[2048,1408]{1,0:T(8,128)(2,1)}, bf16[2048,512]{1,0:T(8,128)(2,1)S(1)}, f32[8,768]{1,0:T(8,128)S(1)}, f32[8,512]{1,0:T(8,128)S(1)}, f32[8,128]{1,0:T(8,128)S(1)}) custom-call(s32[2,4]{1,0:T(2,128)S(1)} %bitcast.85, f32[1]{0:T(128)} %bitcast.15.active_ref, bf16[2048,1408]{1,0:T(8,128)(2,1)} %convolution_convert_fusion.2.proj_ref, ...), custom_call_target="tpu_custom_call" | custom-call | tf_op jit(solution)/shard_map/mixer_backward/pallas_call | solution.py:437
  395.1 1.3 copy-done.5
  396.4 18.5 %convolution_convert_fusion = bf16[2048,2048]{1,0:T(8,128)(2,1)} fusion(bf16[2048,1408]{1,0:T(8,128)(2,1)} %get-tuple-element.26, bf16[2048,1408]{1,0:T(8,128)(2,1)} %bitcast.94), kind=kOutput, calls=%fused_computation.4 | convolution fusion | flops 11815354368 | bytes 19922944 | tf_op jit(solution)/shard_map/dot_general | solution.py:28
  415.0 8.4 convolution_convert_fusion.1
  423.4 1.6 copy-done.6
  425.0 8.2 convolution_convert_fusion.3
  433.2 1.5 copy.45
  434.6 3.8 all-to-all-start.2
  438.5 16.4 %fusion.21 = bf16[2048,1408]{0,1:T(8,128)(2,1)S(1)} fusion(bf16[2048,2048]{1,0:T(8,128)(2,1)} %all-gather.3.cloned.1.call-done, bf16[2048,1408]{1,0:T(8,128)(2,1)} %get-tuple-element.26), kind=kOutput, calls=%fused_computation.72 | convolution fusion | flops 11811160064 | bytes 19922944 | tf_op jit(solution)/shard_map/dot_general | solution.py:32
  455.5 2.7 copy.44
  458.3 63.8 %all-to-all-done.2 = bf16[8,512,256]{2,1,0:T(8,128)(2,1)S(1)} async-done(((bf16[8,512,256]{2,1,0:T(8,128)(2,1)}), bf16[8,512,256]{2,1,0:T(8,128)(2,1)S(1)}, u32[]{:S(2)}, u32[]{:S(2)}) %all-to-all-start.2) | async-done | bytes 2097184 | tf_op jit(solution)/shard_map/all_to_all | solution.py:639
  522.1 4.8 all-to-all-start.1
  527.9 10.5 %reduce-scatter.7.cloned.1.call-done = bf16[256,2048]{1,0:T(8,128)(2,1)} async-done(((bf16[2048,2048]{1,0:T(8,128)(2,1)}), bf16[256,2048]{1,0:T(8,128)(2,1)}) %reduce-scatter.7.cloned.1.call-update) | async-done | bytes 1048592 | tf_op jit(solution)/shard_map/reduce_scatter | solution.py:631
  538.4 2.3 fusion.6
  540.7 0.7 concatenate.40
  541.4 2.5 bitcast_convert_fusion
  544.3 145.6 %all-to-all-done.1 = bf16[8,256,1288]{1,2,0:T(8,128)(2,1)} async-done(((bf16[8,256,1288]{1,2,0:T(8,128)(2,1)}), bf16[8,256,1288]{1,2,0:T(8,128)(2,1)}, u32[]{:S(2)}, u32[]{:S(2)}) %all-to-all-start.1) | async-done | bytes 5275680 | tf_op jit(solution)/shard_map/all_to_all | solution.py:647
  689.9 3.3 convert_element_type.86
  693.4 3.2 fusion.17
  696.6 11.3 %pad_maximum_fusion = f32[256,8512]{0,1:T(8,128)} fusion(f32[256,64]{0,1:T(8,128)S(1)} %slice_bitcast_fusion, f32[256,256]{0,1:T(8,128)S(1)} %slice_reduce_fusion, f32[256,4096]{0,1:T(8,128)S(1)} %bitcast.89, f32[256,4096]{0,1:T(8,128)S(1)} %bitcast.88), kind=kLoop, calls=%fused_computation.3 | loop fusion | flops 6537216 | bytes 17432576 | tf_op jit(solution)/shard_map/concatenate | solution.py:653
  708.6 23.0 %reduce-scatter.5.cloned.1.call-done = bf16[256,2048]{1,0:T(8,128)(2,1)} async-done(((bf16[2048,2048]{1,0:T(8,128)(2,1)}), bf16[256,2048]{1,0:T(8,128)(2,1)}) %reduce-scatter.5.cloned.1.call-update) | async-done | bytes 1048592 | tf_op jit(solution)/shard_map/reduce_scatter | solution.py:605
  731.6 4.2 fusion.8
  735.8 127.2 %all-reduce.5.cloned.1.call-done = f32[28096]{0:T(1024)} async-done(((f32[28096]{0:T(1024)}), f32[28096]{0:T(1024)}) %all-reduce.5.cloned.1.call-update) | async-done | bytes 112400 | tf_op jit(solution)/shard_map/psum | solution.py:678
  863.0 0.9 slice.117
  863.9 0.7 slice.104
  864.6 1.3 slice.118
  865.9 1.3 slice.122
  867.2 1.3 slice.111
  868.5 1.4 fusion.19
  869.9 50.0 %reduce-scatter.11.cloned.1.call-done = f32[1024,256]{1,0:T(8,128)} async-done(((f32[4096,256]{1,0:T(8,128)}), f32[1024,256]{1,0:T(8,128)}) %reduce-scatter.11.cloned.1.call-update) | async-done | bytes 1048592 | tf_op jit(solution)/shard_map/reduce_scatter | solution.py:641
  919.9 93.2 %reduce-scatter.9.cloned.1.call-done = f32[256,2128]{0,1:T(8,128)} async-done(((f32[256,8512]{0,1:T(8,128)}), f32[256,2128]{0,1:T(8,128)}) %reduce-scatter.9.cloned.1.call-update) | async-done | bytes 2179088 | tf_op jit(solution)/shard_map/reduce_scatter | solution.py:662
  (104 shorter events, 5.3 us)
Async XLA Ops:
  7.2 284.6 %copy-start = (bf16[512,2048]{1,0:T(8,128)(2,1)S(1)}, bf16[512,2048]{1,0:T(8,128)(2,1)}, u32[]{:S(2)}) copy-start(bf16[512,2048]{1,0:T(8,128)(2,1)} %param.22) | copy-start | bytes 6291460
  7.2 266.2 %all-gather.3.cloned.1.call-start = ((), (), s32[]{:S(2)}) async-start(), calls=%async_computation.7 | async-start | bytes 9437184 | tf_op jit(solution)/shard_map/all_gather | solution.py:554
  8.9 0.6 copy-start.14
  9.5 0.6 copy-start.11
  12.6 279.2 %all-gather.5.cloned.1.call-start = ((), (), s32[]{:S(2)}) async-start(), calls=%async_computation.8 | async-start | bytes 9437184 | tf_op jit(solution)/shard_map/all_gather | solution.py:555
  12.6 3.4 slice-start
  13.3 3.5 slice-start.1
  13.3 3.5 slice-start.2
  22.7 6.6 copy-start.18
  22.7 7.0 copy-start.10
  22.7 7.9 copy-start.16
  22.7 7.9 copy-start.17
  22.8 8.0 copy-start.13
  22.8 8.3 slice-start.3
  22.8 242.4 %all-to-all-start = ((bf16[8,256,1408]{1,2,0:T(8,128)(2,1)}), bf16[8,256,1408]{1,2,0:T(8,128)(2,1)}, u32[]{:S(2)}, u32[]{:S(2)}) async-start(bf16[8,256,1408]{1,2,0:T(8,128)(2,1)} %fusion.2), calls=%async_computation | async-start | bytes 11534336 | tf_op jit(solution)/shard_map/all_to_all | solution.py:566
  29.2 509.1 %reduce-scatter.7.cloned.1.call-start = ((), (), s32[]{:S(2)}) async-start(), calls=%async_computation.10 | async-start | bytes 9437184 | tf_op jit(solution)/shard_map/reduce_scatter | solution.py:631
  291.8 9.6 copy-start.4
  322.2 1.3 copy-start.2
  323.5 1.3 copy-start.7
  350.9 1.6 copy-start.3
  395.1 1.3 copy-start.5
  414.9 316.7 %reduce-scatter.5.cloned.1.call-start = ((), (), s32[]{:S(2)}) async-start(), calls=%async_computation.9 | async-start | bytes 9437184 | tf_op jit(solution)/shard_map/reduce_scatter | solution.py:605
  423.4 1.6 copy-start.6
  434.6 87.4 %all-to-all-start.2 = ((bf16[8,512,256]{2,1,0:T(8,128)(2,1)}), bf16[8,512,256]{2,1,0:T(8,128)(2,1)S(1)}, u32[]{:S(2)}, u32[]{:S(2)}) async-start(bf16[8,512,256]{2,1,0:T(8,128)(2,1)} %bitcast.90), calls=%async_computation.5 | async-start | bytes 4194304 | tf_op jit(solution)/shard_map/all_to_all | solution.py:639
  522.1 16.3 %copy-start.8 = (bf16[1,2,128,2048]{3,2,1,0:T(8,128)(2,1)S(1)}, bf16[1,2,128,2048]{3,2,1,0:T(8,128)(2,1)}, u32[]{:S(2)}) copy-start(bf16[1,2,128,2048]{3,2,1,0:T(8,128)(2,1)} %param.12) | copy-start | bytes 3145732
  522.1 16.3 %copy-start.9 = (f32[2048]{0:T(1024)S(1)}, f32[2048]{0:T(1024)}, u32[]{:S(2)}) copy-start(f32[2048]{0:T(1024)} %param.14) | copy-start | bytes 24580
  522.1 16.3 %copy-start.12 = (f32[256]{0:T(256)S(1)}, f32[256]{0:T(256)}, u32[]{:S(2)}) copy-start(f32[256]{0:T(256)} %copy-done.11) | copy-start | bytes 3076
  522.1 167.8 %all-to-all-start.1 = ((bf16[8,256,1288]{1,2,0:T(8,128)(2,1)}), bf16[8,256,1288]{1,2,0:T(8,128)(2,1)}, u32[]{:S(2)}, u32[]{:S(2)}) async-start(bf16[8,256,1288]{1,2,0:T(8,128)(2,1)} %bitcast.86), calls=%async_computation.3 | async-start | bytes 10551296 | tf_op jit(solution)/shard_map/all_to_all | solution.py:647
  526.9 336.1 %all-reduce.5.cloned.1.call-start = ((), (), s32[]{:S(2)}) async-start(), calls=%async_computation.11 | async-start | bytes 229376 | tf_op jit(solution)/shard_map/psum | solution.py:678
  541.4 378.5 %reduce-scatter.11.cloned.1.call-start = ((), (), s32[]{:S(2)}) async-start(), calls=%async_computation.13 | async-start | bytes 5242880 | tf_op jit(solution)/shard_map/reduce_scatter | solution.py:641
  544.0 469.1 %reduce-scatter.9.cloned.1.call-start = ((), (), s32[]{:S(2)}) async-start(), calls=%async_computation.12 | async-start | bytes 10895360 | tf_op jit(solution)/shard_map/reduce_scatter | solution.py:662
  707.9 0.7 copy-start.15
  707.9 305.1 %copy-start.1 = (bf16[512,2048]{1,0:T(8,128)(2,1)S(1)}, bf16[512,2048]{1,0:T(8,128)(2,1)}, u32[]{:S(2)}) copy-start(bf16[512,2048]{1,0:T(8,128)(2,1)} %param.22) | copy-start | bytes 6291460
Sparse Core Ops, SparseCore 0:
  12.7 177.3 all-gather.2
  191.6 96.7 all-gather.4
  415.0 123.3 reduce-scatter.6
  540.5 191.0 reduce-scatter.4
  737.1 125.9 all-reduce.4
  866.4 53.4 reduce-scatter.10
  923.9 89.0 reduce-scatter.8

commit v2 on v1

--- a/solution.py
+++ b/solution.py
@@ -508,6 +508,456 @@
         tri,
     )
 
+MESH = pl.DeviceIdType.MESH
+ANY = pl.BlockSpec(memory_space=pl.ANY)
+
+
+def greet(axes):
+    barrier = pltpu.get_barrier_semaphore()
+    waits = 0
+    for axis in axes:
+        count, me = lax.axis_size(axis), lax.axis_index(axis)
+
+        def hello(turn, carry):
+            pl.semaphore_signal(
+                barrier,
+                inc=1,
+                device_id={axis: lax.rem(me + turn, count)},
+                device_id_type=MESH,
+            )
+            return carry
+
+        lax.fori_loop(1, count, hello, 0)
+        waits += count - 1
+    pl.semaphore_wait(barrier, waits)
+
+
+def remote(source, target, send, receive, device):
+    return pltpu.make_async_remote_copy(
+        src_ref=source,
+        dst_ref=target,
+        send_sem=send,
+        recv_sem=receive,
+        device_id=device,
+        device_id_type=MESH,
+    )
+
+
+def exchange_kernel(axis, total, *refs):
+    ins, outs = refs[:total], refs[total : 2 * total]
+    send, receive, keep = refs[2 * total :]
+    count, me = lax.axis_size(axis), lax.axis_index(axis)
+    greet((axis,))
+
+    def copy(item, turn, slot):
+        peer = lax.rem(me + turn, count)
+        owner = me if slot is None else slot
+        return remote(
+            ins[item].at[peer],
+            outs[item].at[owner],
+            send.at[item, peer],
+            receive.at[item, owner],
+            {axis: peer},
+        )
+
+    def start(turn, carry):
+        for item in range(total):
+            copy(item, turn, None).start()
+        return carry
+
+    def finish(turn, carry):
+        for item in range(total):
+            copy(item, turn, None).wait_send()
+            copy(item, turn, lax.rem(me + turn, count)).wait_recv()
+        return carry
+
+    lax.fori_loop(1, count, start, 0)
+    stays = [
+        pltpu.make_async_copy(ins[item].at[me], outs[item].at[me], keep.at[item])
+        for item in range(total)
+    ]
+    for stay in stays:
+        stay.start()
+    lax.fori_loop(1, count, finish, 0)
+    for stay in stays:
+        stay.wait()
+
+
+def exchange(arrays, axis, collective_id):
+    total, count = len(arrays), arrays[0].shape[0]
+    return pl.pallas_call(
+        partial(exchange_kernel, axis, total),
+        in_specs=[ANY] * total,
+        out_specs=[ANY] * total,
+        out_shape=[jax.ShapeDtypeStruct(item.shape, item.dtype) for item in arrays],
+        scratch_shapes=[
+            pltpu.SemaphoreType.DMA((total, count)),
+            pltpu.SemaphoreType.DMA((total, count)),
+            pltpu.SemaphoreType.DMA((total,)),
+        ],
+        compiler_params=pltpu.CompilerParams(
+            collective_id=collective_id, has_side_effects=True
+        ),
+        name="exchange_" + axis,
+    )(*arrays)
+
+
+def share_kernel(axis, in_ref, out_ref, slots, send, receive):
+    count, me = lax.axis_size(axis), lax.axis_index(axis)
+    greet((axis,))
+
+    def copy(turn, owner):
+        peer = lax.rem(me + turn, count)
+        return remote(in_ref, slots.at[owner], send.at[peer], receive.at[owner], {axis: peer})
+
+    def start(turn, carry):
+        copy(turn, me).start()
+        return carry
+
+    def finish(turn, carry):
+        copy(turn, me).wait_send()
+        copy(turn, lax.rem(me + turn, count)).wait_recv()
+        return carry
+
+    lax.fori_loop(1, count, start, 0)
+    slots[me] = in_ref[...]
+    lax.fori_loop(1, count, finish, 0)
+
+    def add(owner, total):
+        return total + slots[owner]
+
+    out_ref[...] = lax.fori_loop(1, count, add, slots[0])
+
+
+def share(value, axis, collective_id):
+    count = lax.axis_size(axis)
+    return pl.pallas_call(
+        partial(share_kernel, axis),
+        in_specs=[pl.BlockSpec(memory_space=pltpu.VMEM)],
+        out_specs=pl.BlockSpec(memory_space=pltpu.VMEM),
+        out_shape=jax.ShapeDtypeStruct(value.shape, value.dtype),
+        scratch_shapes=[
+            pltpu.VMEM((count,) + value.shape, value.dtype),
+            pltpu.SemaphoreType.DMA((count,)),
+            pltpu.SemaphoreType.DMA((count,)),
+        ],
+        compiler_params=pltpu.CompilerParams(
+            collective_id=collective_id, has_side_effects=True, vmem_limit_bytes=48 << 20
+        ),
+        name="share_" + axis,
+    )(value)
+
+
+def total_kernel(in_ref, out_ref, slots, sent, send, receive, send_back, receive_back):
+    seq_total, width_total = lax.axis_size("seq"), lax.axis_size("width")
+    count = seq_total * width_total
+    me = lax.axis_index("width") * seq_total + lax.axis_index("seq")
+    barrier = pltpu.get_barrier_semaphore()
+
+    def device(turn):
+        peer = lax.rem(me + turn, count)
+        return peer, {"width": peer // seq_total, "seq": lax.rem(peer, seq_total)}
+
+    def hello(turn, carry):
+        pl.semaphore_signal(barrier, inc=1, device_id=device(turn)[1], device_id_type=MESH)
+        return carry
+
+    lax.fori_loop(1, count, hello, 0)
+    pl.semaphore_wait(barrier, count - 1)
+
+    def first(turn, from_peer):
+        peer, where = device(turn)
+        owner = peer if from_peer else me
+        return remote(
+            in_ref.at[peer], slots.at[owner], send.at[peer], receive.at[owner], where
+        )
+
+    def second(turn, from_peer):
+        peer, where = device(turn)
+        owner = peer if from_peer else me
+        return remote(
+            sent, out_ref.at[owner], send_back.at[peer], receive_back.at[owner], where
+        )
+
+    def loop(make, action):
+        def body(turn, carry):
+            action(make, turn)
+            return carry
+
+        lax.fori_loop(1, count, body, 0)
+
+    def start(make, turn):
+        make(turn, False).start()
+
+    def finish(make, turn):
+        make(turn, False).wait_send()
+        make(turn, True).wait_recv()
+
+    loop(first, start)
+    slots[me] = in_ref[me]
+    loop(first, finish)
+
+    def add(owner, total):
+        return total + slots[owner]
+
+    sent[...] = lax.fori_loop(1, count, add, slots[0])
+    loop(second, start)
+    out_ref[me] = sent[...]
+    loop(second, finish)
+
+
+def total_over_all(vector, collective_id):
+    count = lax.axis_size("seq") * lax.axis_size("width")
+    length = vector.shape[0]
+    tiles = -(-length // (count * 8 * LANES))
+    padded = jnp.pad(vector, (0, count * tiles * 8 * LANES - length))
+    shape = (count, tiles * 8, LANES)
+    summed = pl.pallas_call(
+        total_kernel,
+        in_specs=[pl.BlockSpec(memory_space=pltpu.VMEM)],
+        out_specs=pl.BlockSpec(memory_space=pltpu.VMEM),
+        out_shape=jax.ShapeDtypeStruct(shape, F32),
+        scratch_shapes=[
+            pltpu.VMEM(shape, F32),
+            pltpu.VMEM(shape[1:], F32),
+            pltpu.SemaphoreType.DMA((count,)),
+            pltpu.SemaphoreType.DMA((count,)),
+            pltpu.SemaphoreType.DMA((count,)),
+            pltpu.SemaphoreType.DMA((count,)),
+        ],
+        compiler_params=pltpu.CompilerParams(
+            collective_id=collective_id, has_side_effects=True, vmem_limit_bytes=16 << 20
+        ),
+        name="total_over_all",
+    )(padded.reshape(shape))
+    return summed.reshape(-1)[:length]
+
+
+PARTS = 2
+
+
+def gather_kernel(
+    x_ref,
+    g_ref,
+    w_ref,
+    x_out,
+    g_out,
+    w_out,
+    w_send,
+    w_receive,
+    f_send,
+    f_receive,
+    up_send,
+    down_send,
+    line_receive,
+    side_send,
+    side_receive,
+    keep,
+):
+    seq_total, width_total = lax.axis_size("seq"), lax.axis_size("width")
+    me, mine = lax.axis_index("seq"), lax.axis_index("width")
+    chips, chip, core = seq_total // 2, me // 2, lax.rem(me, 2)
+    sibling = me + 1 - 2 * core
+    quarter = w_ref.shape[1]
+    depth = quarter * width_total
+    block = x_ref.shape[0]
+    piece = block // PARTS
+    greet(("seq", "width"))
+
+    def rows(source, group):
+        return pl.ds(pl.multiple_of(source * depth + group * quarter, 8), quarter)
+
+    def deal(turn, from_peer):
+        peer = lax.rem(me + turn, seq_total)
+        owner = peer if from_peer else me
+        return remote(
+            w_ref.at[peer],
+            w_out.at[rows(owner, mine)],
+            w_send.at[peer],
+            w_receive.at[owner],
+            {"seq": peer},
+        )
+
+    def deal_start(turn, carry):
+        deal(turn, False).start()
+        return carry
+
+    lax.fori_loop(1, seq_total, deal_start, 0)
+    w_own = pltpu.make_async_copy(w_ref.at[me], w_out.at[rows(me, mine)], keep.at[0])
+    w_own.start()
+    x_own = pltpu.make_async_copy(x_ref, x_out.at[pl.ds(me * block, block)], keep.at[1])
+    g_own = pltpu.make_async_copy(g_ref, g_out.at[pl.ds(me * block, block)], keep.at[2])
+    x_own.start()
+    g_own.start()
+
+    def at(out, owner, part):
+        return out.at[pl.ds(pl.multiple_of(owner * block + part * piece, 8), piece)]
+
+    def line(item, out, source, owner_chip, part, target_chip, sems):
+        owner = owner_chip * 2 + core
+        return remote(
+            source,
+            at(out, owner, part),
+            sems.at[item, owner_chip, part],
+            line_receive.at[item, owner_chip, part],
+            {"seq": target_chip * 2 + core},
+        )
+
+    def side(item, out, source, owner_chip, part, from_sibling):
+        owner = owner_chip * 2 + (1 - core if from_sibling else core)
+        return remote(
+            source,
+            at(out, owner, part),
+            side_send.at[item, owner_chip, part],
+            side_receive.at[item, owner_chip, part],
+            {"seq": sibling},
+        )
+
+    pairs = ((x_ref, x_out), (g_ref, g_out))
+
+    def own_start(item):
+        source, out = pairs[item]
+        for part in range(PARTS):
+            here = source.at[pl.ds(part * piece, piece)]
+
+            @pl.when(chip + 1 < chips)
+            def _():
+                line(item, out, here, chip, part, chip + 1, up_send).start()
+
+            @pl.when(chip >= 1)
+            def _():
+                line(item, out, here, chip, part, chip - 1, down_send).start()
+
+            side(item, out, here, chip, part, False).start()
+
+    def pass_on(item):
+        out = pairs[item][1]
+
+        def hop(turn, carry):
+            below, above = chip - turn, chip + turn
+            for part in range(PARTS):
+
+                @pl.when(below >= 0)
+                def _():
+                    here = at(out, below * 2 + core, part)
+                    line(item, out, here, below, part, chip, up_send).wait_recv()
+
+                    @pl.when(chip + 1 < chips)
+                    def _():
+                        line(item, out, here, below, part, chip + 1, up_send).start()
+
+                    side(item, out, here, below, part, False).start()
+
+                @pl.when(above < chips)
+                def _():
+                    here = at(out, above * 2 + core, part)
+                    line(item, out, here, above, part, chip, down_send).wait_recv()
+
+                    @pl.when(chip >= 1)
+                    def _():
+                        line(item, out, here, above, part, chip - 1, down_send).start()
+
+                    side(item, out, here, above, part, False).start()
+
+            return carry
+
+        lax.fori_loop(1, chips, hop, 0)
+
+    def forward(source, turn, from_peer):
+        peer = lax.rem(mine + turn, width_total)
+        group = peer if from_peer else mine
+        where = w_out.at[rows(source, group)]
+        return remote(
+            where, where, f_send.at[peer, source], f_receive.at[group, source], {"width": peer}
+        )
+
+    def forward_start(source):
+        for turn in range(1, width_total):
+            forward(source, turn, False).start()
+
+    def deal_pass(turn, carry):
+        deal(turn, True).wait_recv()
+        forward_start(lax.rem(me + turn, seq_total))
+        return carry
+
+    own_start(0)
+    w_own.wait()
+    forward_start(me)
+    lax.fori_loop(1, seq_total, deal_pass, 0)
+    pass_on(0)
+    own_start(1)
+    pass_on(1)
+
+    def deal_end(turn, carry):
+        deal(turn, False).wait_send()
+        return carry
+
+    lax.fori_loop(1, seq_total, deal_end, 0)
+
+    def forward_end(source, carry):
+        for turn in range(1, width_total):
+            forward(source, turn, False).wait_send()
+            forward(source, turn, True).wait_recv()
+        return carry
+
+    lax.fori_loop(0, seq_total, forward_end, 0)
+    for item in range(2):
+        out = pairs[item][1]
+
+        def line_end(owner_chip, carry):
+            for part in range(PARTS):
+                here = at(out, owner_chip * 2 + core, part)
+
+                @pl.when((owner_chip <= chip) & (chip + 1 < chips))
+                def _():
+                    line(item, out, here, owner_chip, part, chip + 1, up_send).wait_send()
+
+                @pl.when((owner_chip >= chip) & (chip >= 1))
+                def _():
+                    line(item, out, here, owner_chip, part, chip - 1, down_send).wait_send()
+
+                side(item, out, here, owner_chip, part, False).wait_send()
+                side(item, out, here, owner_chip, part, True).wait_recv()
+            return carry
+
+        lax.fori_loop(0, chips, line_end, 0)
+    x_own.wait()
+    g_own.wait()
+
+
+def gather_rows(x, g, pieces, collective_id):
+    seq_total, width_total = lax.axis_size("seq"), lax.axis_size("width")
+    chips = seq_total // 2
+    whole = (x.shape[0] * seq_total, x.shape[1])
+    weight = (seq_total * width_total * pieces.shape[1], pieces.shape[2])
+    dma = pltpu.SemaphoreType.DMA
+    return pl.pallas_call(
+        gather_kernel,
+        in_specs=[ANY] * 3,
+        out_specs=[ANY] * 3,
+        out_shape=[
+            jax.ShapeDtypeStruct(whole, x.dtype),
+            jax.ShapeDtypeStruct(whole, g.dtype),
+            jax.ShapeDtypeStruct(weight, pieces.dtype),
+        ],
+        scratch_shapes=[
+            dma((seq_total,)),
+            dma((seq_total,)),
+            dma((width_total, seq_total)),
+            dma((width_total, seq_total)),
+            dma((2, chips, PARTS)),
+            dma((2, chips, PARTS)),
+            dma((2, chips, PARTS)),
+            dma((2, chips, PARTS)),
+            dma((2, chips, PARTS)),
+            dma((3,)),
+        ],
+        compiler_params=pltpu.CompilerParams(
+            collective_id=collective_id, has_side_effects=True
+        ),
+        name="gather_rows",
+    )(x, g, pieces)
+
 
 def input_norm(hidden, in_gain):
     return hidden * lax.rsqrt(jnp.mean(hidden * hidden, axis=1, keepdims=True) + EPSILON) * in_gain
@@ -551,20 +1001,19 @@
     flat_hidden = hidden_in[0].reshape(micros * rows, model_width).astype(F32)
     flat_grad = cotangent[0].reshape(micros * rows, model_width)
     normed, norm_back = jax.vjp(input_norm, flat_hidden, in_gain)
-    all_normed = lax.all_gather(normed.astype(BF16), "seq", axis=0, tiled=True)
-    all_grad = lax.all_gather(flat_grad, "seq", axis=0, tiled=True)
-
     dt_pad = LANES
-    gates = in_weight[:, :INNER].reshape(depth, seq_total, width)
-    xs = in_weight[:, INNER : 2 * INNER].reshape(depth, seq_total, width)
+    width_total = lax.axis_size("width")
+    quarter = depth // width_total
+    in_quarter = own(in_weight, group_index * quarter, quarter)
+    gates = in_quarter[:, :INNER].reshape(quarter, seq_total, width)
+    xs = in_quarter[:, INNER : 2 * INNER].reshape(quarter, seq_total, width)
     bc = jnp.broadcast_to(
-        in_weight[:, None, 2 * INNER : INNER + CONV], (depth, seq_total, 2 * STATE)
-    )
-    dts = in_weight[:, INNER + CONV :].reshape(depth, seq_total, heads)
+        in_quarter[:, None, 2 * INNER : INNER + CONV], (quarter, seq_total, 2 * STATE)
+    )
+    dts = in_quarter[:, INNER + CONV :].reshape(quarter, seq_total, heads)
     dts = jnp.pad(dts, ((0, 0), (0, 0), (0, dt_pad - heads)))
     pieces = jnp.concatenate([bc, xs, gates, dts], axis=2).transpose(1, 0, 2)
-    columns = lax.all_to_all(pieces, "seq", split_axis=0, concat_axis=0)
-    columns = columns.reshape(seq_total * depth, columns.shape[2])
+    all_normed, all_grad, columns = gather_rows(normed.astype(BF16), flat_grad, pieces, 0)
 
     conv_width = 2 * STATE + width
 
@@ -601,7 +1050,7 @@
     gg, mixed, states, tails, sums = run_forward(
         micros, heads, rows, seq_total, starts[0], proj, dnorm, taps, head_table, cols, expand, tri
     )
-    sums = lax.psum(sums, "seq")
+    sums = share(sums, "seq", 1)
     branch = lax.psum_scatter(
         mm(gg, out_weight).astype(BF16), "seq", scatter_dimension=0, tiled=True
     )
@@ -634,32 +1083,39 @@
     grad_hidden, grad_gain_in = norm_back(grad_normed)
     hidden_grads = (flat_grad.astype(F32) + grad_hidden).astype(BF16)
 
-    grad_out = mm_tn(gnorm, all_grad).astype(BF16)
-    grad_out = grad_out.reshape(width, seq_total, model_width // seq_total).transpose(1, 0, 2)
-    grad_out = lax.all_to_all(grad_out, "seq", split_axis=0, concat_axis=0)
-    grad_out = grad_out.reshape(seq_total * width, model_width // seq_total)
-    shard_out = lax.psum_scatter(
-        grad_out.astype(F32), "width", scatter_dimension=0, tiled=True
-    )
-
-    grad_in = mm_tn(all_normed, dproj).astype(BF16)[:, : conv_width + width + heads]
-    grad_in = grad_in.reshape(seq_total, depth, grad_in.shape[1])
-    grad_in = lax.all_to_all(grad_in, "seq", split_axis=0, concat_axis=0)
-    grad_in = grad_in.astype(F32)
+    sub = width // width_total
+    grad_out = mm_tn(gnorm, all_grad).astype(BF16).reshape(width_total, sub, model_width)
+    grad_in = mm_tn(all_normed, dproj).astype(BF16)
+    grad_in = grad_in.reshape(seq_total, width_total, quarter, grad_in.shape[1])
+    grad_in = grad_in.transpose(1, 0, 2, 3)
+    grad_out, grad_in = exchange([grad_out, grad_in], "width", 2)
+
+    def added(value):
+        return jnp.sum(value.astype(F32), axis=0).astype(BF16)
+
+    grad_in = added(grad_in)
+    grad_out = added(grad_out).reshape(sub, seq_total, model_width // seq_total)
+    grad_out, grad_in = exchange([grad_out.transpose(1, 0, 2), grad_in], "seq", 3)
 
     def joined(value):
-        return value.transpose(1, 0, 2).reshape(depth, seq_total * value.shape[2])
+        return value.transpose(1, 0, 2).reshape(quarter, seq_total * value.shape[2])
 
     grad_in = jnp.concatenate(
         [
             joined(grad_in[:, :, conv_width : conv_width + width]),
             joined(grad_in[:, :, 2 * STATE : conv_width]),
-            jnp.sum(grad_in[:, :, : 2 * STATE], axis=0),
-            joined(grad_in[:, :, conv_width + width :]),
+            jnp.sum(grad_in[:, :, : 2 * STATE].astype(F32), axis=0).astype(BF16),
+            joined(grad_in[:, :, conv_width + width : conv_width + width + heads]),
         ],
         axis=1,
     )
-    shard_in = lax.psum_scatter(grad_in, "width", scatter_dimension=1, tiled=True)
+    shard_cols = grad_in.shape[1] // width_total
+    grad_in = grad_in.reshape(quarter, width_total, shard_cols).transpose(1, 0, 2)
+    blocks = seq_total // width_total
+    grad_out = grad_out.reshape(width_total, blocks, sub, model_width // seq_total)
+    grad_out, grad_in = exchange([grad_out, grad_in], "width", 4)
+    shard_in = grad_in.reshape(depth, shard_cols).astype(F32)
+    shard_out = grad_out.transpose(1, 0, 2, 3).reshape(blocks * width, -1).astype(F32)
 
     skip_heads = jnp.sum(gcols[0].reshape(heads, HEAD_DIM), axis=1)
     conv_small = jnp.concatenate(
@@ -675,7 +1131,7 @@
             placed(skip_heads, HEADS, head_first),
         ]
     )
-    small = lax.psum(small, ("width", "seq"))
+    small = total_over_all(small, 5)
     edge = 5 * CONV
     conv_small = small[:edge].reshape(5, CONV)
     in_gain_sum = small[edge : edge + model_width]

time: 1030 us -> 599 us (0.58)
  waiting for transfers between devices: 748 us -> 0.04 us
  Pallas kernels: 63.4 us -> 441 us
  blocking collectives: 26.1 us -> 0 us
  starting transfers between devices: 15.6 us -> 0.08 us
    all_to_all x3 -> x0, waiting for transfers between devices: 443 us -> none  [the longest x1 234 us: per_device(): columns = lax.all_to_all(pieces, 'seq', split_axis=0, concat_axis=0)]
    pallas_call x0 -> x6, Pallas kernels: none -> 378 us  [the longest x3 173 us: exchange(): pl.pallas_call(partial(exchange_kernel, axis, total), in_specs=[ANY] * to...]
    reduce_scatter x2 -> x0, waiting for transfers between devices: 143 us -> none  [the longest x1 93.2 us: per_device(): lax.psum_scatter(grad_in, 'width', scatter_dimension=1, tiled=True)]
    psum x1 -> x0, waiting for transfers between devices: 127 us -> none  [per_device(): small = lax.psum(small, ('width', 'seq'))]
    psum x1 -> x0, blocking collectives: 26.1 us -> none  [per_device(): sums = lax.psum(sums, 'seq')]
    reduce_scatter x1, waiting for transfers between devices: 23 us -> 0.01 us  [per_device(): lax.psum_scatter(mm(gg, out_weight).astype(BF16), 'seq', scatter_dimensio...]
    all_to_all x3 -> x0, starting transfers between devices: 15.1 us -> none  [the longest x1 6.47 us: per_device(): columns = lax.all_to_all(pieces, 'seq', split_axis=0, concat_axis=0)]
    reduce_scatter x1, waiting for transfers between devices: 10.5 us -> 0.01 us  [per_device(): lax.psum_scatter(mm_nt(dproj, columns).astype(BF16), 'seq', scatter_dimen...]
  transfers between devices with their start and end apart: 10 -> 2, of which waited for: 8 -> 0; matrix products, arithmetic and copies ran while one was open for 11% -> 11% of each run, Pallas kernels for 0% -> 34%
where the time goes in v2:
time: 599 us; the launch traced here: 598 us
  Pallas kernels  441 us (74%)
  matrix products  78.3 us (13%)
  local copies, waits for them, and re-layouts  38.9 us (6%)
  other arithmetic  25.3 us (4%)
  between operations  14.5 us (2%)
    pallas_call x3, Pallas kernels, exchange(): pl.pallas_call(partial(exchange_kernel, axis, total), in_specs=[ANY] * to...  173 us
    pallas_call x1, Pallas kernels, gather_rows(): pl.pallas_call(gather_kernel, in_specs=[ANY] * 3, out_specs=[ANY] * 3, ou...  168 us
    pallas_call x1, Pallas kernels, run_backward(): pl.pallas_call(partial(backward_kernel, micros, heads), grid=(chunks,), i...  42.6 us
    pallas_call x1, Pallas kernels, total_over_all(): pl.pallas_call(total_kernel, in_specs=[pl.BlockSpec(memory_space=pltpu.VM...  28.4 us
    dot_general x2, matrix products, mm(): lax.dot_general(a, b, (((1,), (0,)), ((), ())), preferred_element_type=F32)  27.1 us
    dot_general x2, matrix products, mm_tn(): lax.dot_general(a, b, (((0,), (0,)), ((), ())), preferred_element_type=F32)  26.4 us
    dot_general x2, matrix products, mm_nt(): lax.dot_general(a, b, (((1,), (1,)), ((), ())), preferred_element_type=F32)  24.9 us
    pallas_call x1, Pallas kernels, run_forward(): pl.pallas_call(partial(forward_kernel, micros, heads), grid=(chunks,), in...  20.8 us
  transfers between devices with their start and end apart: 2, of which 0 were waited for; matrix products, arithmetic and copies ran while one was open for 11% of the time, Pallas kernels for 34%

profile of v2, /device:TPU:0, one launch (start us, length us, event | category | flops | bytes accessed | tf_op | source)
XLA Modules:
  0.0 598.4 jit_solution(11816317742278697489)
XLA Ops:
  7.2 0.9 broadcast_in_dim.37
  8.1 0.8 dynamic-slice.3
  8.9 0.7 constant_dynamic-slice_fusion.2
  10.3 0.8 iota_compare_fusion.1
  11.1 3.6 fusion.17
  14.7 2.4 copy.44
  17.1 2.4 copy.45
  19.5 0.9 dynamic-slice.4
  20.5 0.8 dynamic-slice_bitcast_fusion
  21.3 0.8 copy.43
  23.4 1.0 add_convert_fusion.expand_ref
  24.4 1.3 fusion.8.x_ref
  25.7 1.2 fusion.12.w_ref
  26.9 168.3 %gather_rows.1 = (bf16[2048,2048]{1,0:T(8,128)(2,1)}, bf16[2048,2048]{1,0:T(8,128)(2,1)}, bf16[2048,1408]{1,0:T(8,128)(2,1)}) custom-call(bf16[256,2048]{1,0:T(8,128)(2,1)} %fusion.8.x_ref, bf16[256,2048]{1,0:T(8,128)(2,1)} %bitcast.99, bf16[8,64,1408]{2,1,0:T(8,128)(2,1)} %fusion.12.w_ref), custom_call_target="tpu_custom_call" | custom-call | tf_op jit(solution)/shard_map/gather_rows/pallas_call | solution.py:934
  195.2 18.5 %convolution_convert_fusion.2.proj_ref = bf16[2048,1408]{1,0:T(8,128)(2,1)} fusion(bf16[2048,2048]{1,0:T(8,128)(2,1)} %get-tuple-element.30, bf16[2048,1408]{1,0:T(8,128)(2,1)} %get-tuple-element.31), kind=kOutput, calls=%fused_computation.2 | convolution fusion | flops 11814043648 | bytes 19922944 | tf_op jit(solution)/shard_map/dot_general | solution.py:24
  213.7 0.8 dynamic_slice.30
  214.5 6.4 %fusion.19.dnorm_ref = f32[2048,512]{1,0:T(8,128)} fusion(bf16[2048,2048]{1,0:T(8,128)(2,1)S(1)} %copy-done.21, bf16[512,2048]{1,0:T(8,128)(2,1)S(1)} %copy-done), kind=kOutput, calls=%fused_computation.75 | convolution fusion | flops 4294967296 | bytes 14680064 | tf_op jit(solution)/shard_map/dot_general | solution.py:28
  221.2 20.8 %mixer_forward.1 = (bf16[2048,512]{1,0:T(8,128)(2,1)S(1)}, f32[2048,512]{1,0:T(8,128)}, bf16[8,2,128,512]{3,2,1,0:T(8,128)(2,1)S(1)}, f32[8,2,8,768]{3,2,1,0:T(8,128)S(1)}, f32[8,8,128]{2,1,0:T(8,128)S(1)}) custom-call(s32[2,4]{1,0:T(2,128)S(1)} %bitcast.94, bf16[2048,1408]{1,0:T(8,128)(2,1)} %convolution_convert_fusion.2.proj_ref, ...), custom_call_target="tpu_custom_call" | custom-call | tf_op jit(solution)/shard_map/mixer_forward/pallas_call | solution.py:374
  242.0 1.3 copy-done.1
  243.4 1.3 copy-done.6
  244.7 7.9 %share_seq.1.sums_ref = f32[8,8,128]{2,1,0:T(8,128)S(1)} custom-call(f32[8,8,128]{2,1,0:T(8,128)S(1)} %get-tuple-element.34.in_ref), custom_call_target="tpu_custom_call" | custom-call | tf_op jit(solution)/shard_map/share_seq/pallas_call | solution.py:634
  252.6 1.6 copy-done.2
  254.2 42.6 %mixer_backward.1 = (bf16[2048,1408]{1,0:T(8,128)(2,1)}, bf16[2048,512]{1,0:T(8,128)(2,1)S(1)}, f32[8,768]{1,0:T(8,128)S(1)}, f32[8,512]{1,0:T(8,128)S(1)}, f32[8,128]{1,0:T(8,128)S(1)}) custom-call(s32[2,4]{1,0:T(2,128)S(1)} %bitcast.95, f32[1]{0:T(128)} %bitcast.14.active_ref, bf16[2048,1408]{1,0:T(8,128)(2,1)} %convolution_convert_fusion.2.proj_ref, ...), custom_call_target="tpu_custom_call" | custom-call | tf_op jit(solution)/shard_map/mixer_backward/pallas_call | solution.py:437
  296.8 1.3 copy-done.4
  298.1 18.5 %convolution_convert_fusion = bf16[2048,2048]{1,0:T(8,128)(2,1)} fusion(bf16[2048,1408]{1,0:T(8,128)(2,1)} %get-tuple-element.38, bf16[2048,1408]{1,0:T(8,128)(2,1)} %get-tuple-element.31), kind=kOutput, calls=%fused_computation | convolution fusion | flops 11815354368 | bytes 19922944 | tf_op jit(solution)/shard_map/dot_general | solution.py:28
  316.7 8.6 %convolution_convert_fusion.1 = bf16[2048,2048]{1,0:T(8,128)(2,1)} fusion(bf16[2048,512]{1,0:T(8,128)(2,1)} %copy-done.6, bf16[512,2048]{1,0:T(8,128)(2,1)S(1)} %copy-done), kind=kOutput, calls=%fused_computation.1 | convolution fusion | flops 4299161600 | bytes 12582912 | tf_op jit(solution)/shard_map/dot_general | solution.py:24
  325.3 17.2 %convolution_convert_fusion.3 = bf16[2048,1408]{1,0:T(8,128)(2,1)S(1)} fusion(bf16[2048,2048]{1,0:T(8,128)(2,1)} %get-tuple-element.30, bf16[2048,1408]{1,0:T(8,128)(2,1)} %get-tuple-element.38), kind=kOutput, calls=%fused_computation.3 | convolution fusion | flops 11814043648 | bytes 19922944 | tf_op jit(solution)/shard_map/dot_general | solution.py:32
  342.5 3.1 copy.64
  345.6 9.2 %convolution_convert_fusion.4 = bf16[512,2048]{1,0:T(8,128)(2,1)} fusion(bf16[2048,512]{1,0:T(8,128)(2,1)S(1)} %copy-done.5, bf16[2048,2048]{1,0:T(8,128)(2,1)} %get-tuple-element.32), kind=kOutput, calls=%fused_computation.6 | convolution fusion | flops 4296015872 | bytes 12582912 | tf_op jit(solution)/shard_map/dot_general | solution.py:32
  354.7 89.2 %exchange_width.2 = (bf16[4,128,2048]{2,1,0:T(8,128)(2,1)}, bf16[4,8,64,1408]{3,2,1,0:T(8,128)(2,1)}) custom-call(bf16[4,128,2048]{2,1,0:T(8,128)(2,1)} %bitcast.106, bf16[4,8,64,1408]{3,2,1,0:T(8,128)(2,1)} %bitcast.96), custom_call_target="tpu_custom_call" | custom-call | tf_op jit(solution)/shard_map/exchange_width/pallas_call | solution.py:588
  443.9 2.0 reduce_sum.84
  446.2 1.0 copy.48
  447.2 5.1 reduce_sum.85.refs_1_
  452.4 62.8 %exchange_seq.1 = (bf16[8,128,256]{2,1,0:T(8,128)(2,1)}, bf16[8,64,1408]{2,1,0:T(8,128)(2,1)}) custom-call(bf16[8,128,256]{2,1,0:T(8,128)(2,1)} %bitcast.105, bf16[8,64,1408]{2,1,0:T(8,128)(2,1)} %reduce_sum.85.refs_1_), custom_call_target="tpu_custom_call" | custom-call | tf_op jit(solution)/shard_map/exchange_seq/pallas_call | solution.py:588
  515.2 1.3 slice_bitcast_fusion.1
  516.6 0.9 slice_bitcast_fusion.2
  517.7 1.0 slice_reduce_fusion
  518.7 1.1 pad_maximum_fusion
  519.8 1.9 reshape.184
  521.7 1.1 copy.65
  522.8 21.4 %exchange_width.3 = (bf16[4,2,128,256]{3,2,1,0:T(8,128)(2,1)}, bf16[4,64,2128]{2,1,0:T(8,128)(2,1)}) custom-call(bf16[4,2,128,256]{3,2,1,0:T(8,128)(2,1)} %bitcast.110, bf16[4,64,2128]{2,1,0:T(8,128)(2,1)} %bitcast.98), custom_call_target="tpu_custom_call" | custom-call | tf_op jit(solution)/shard_map/exchange_width/pallas_call | solution.py:588
  544.2 2.8 bitcast_convert_fusion
  546.9 3.0 copy.55
  549.9 1.2 convert_bitcast_fusion
  551.1 1.0 copy.54
  553.5 2.3 fusion.4
  555.8 28.4 %total_over_all.1 = f32[32,8,128]{2,1,0:T(8,128)S(1)} custom-call(f32[32,8,128]{2,1,0:T(8,128)S(1)} %pad_bitcast_fusion.in_ref), custom_call_target="tpu_custom_call" | custom-call | tf_op jit(solution)/shard_map/total_over_all/pallas_call | solution.py:715
  587.4 4.2 fusion.6
  (105 shorter events, 7.5 us)
Async XLA Ops:
  7.2 207.3 %copy-start = (bf16[512,2048]{1,0:T(8,128)(2,1)S(1)}, bf16[512,2048]{1,0:T(8,128)(2,1)}, u32[]{:S(2)}) copy-start(bf16[512,2048]{1,0:T(8,128)(2,1)} %param.22) | copy-start | bytes 6291460
  7.2 546.3 %reduce-scatter.5.cloned.1.call-start = ((), (), s32[]{:S(2)}) async-start(), calls=%async_computation.3 | async-start | bytes 9437184 | tf_op jit(solution)/shard_map/reduce_scatter | solution.py:1080
  8.1 15.2 %copy-start.14 = (f32[1,4352]{1,0:T(1,128)}, f32[1,4352]{1,0:T(1,128)S(1)}, u32[]{:S(2)}) copy-start(f32[1,4352]{1,0:T(1,128)S(1)} %broadcast_in_dim.37) | copy-start | bytes 52228
  14.7 7.4 %copy-start.7 = (bf16[1,2,128,2048]{3,2,1,0:T(8,128)(2,1)S(1)}, bf16[1,2,128,2048]{3,2,1,0:T(8,128)(2,1)}, u32[]{:S(2)}) copy-start(bf16[1,2,128,2048]{3,2,1,0:T(8,128)(2,1)} %param.12) | copy-start | bytes 3145732
  14.7 8.3 %copy-start.22 = (f32[64]{0:T(128)S(1)}, f32[64]{0:T(128)}, u32[]{:S(2)}) copy-start(f32[64]{0:T(128)} %param.20) | copy-start | bytes 772
  17.1 7.2 %copy-start.13 = (f32[2048]{0:T(1024)S(1)}, f32[2048]{0:T(1024)}, u32[]{:S(2)}) copy-start(f32[2048]{0:T(1024)} %param.14) | copy-start | bytes 24580
  22.4 0.6 copy-start.17
  22.4 4.5 copy-start.15
  23.3 2.3 copy-start.9
  23.3 2.3 copy-start.10
  23.4 2.3 copy-start.11
  195.2 19.3 %copy-start.21 = (bf16[2048,2048]{1,0:T(8,128)(2,1)S(1)}, bf16[2048,2048]{1,0:T(8,128)(2,1)}, u32[]{:S(2)}) copy-start(bf16[2048,2048]{1,0:T(8,128)(2,1)} %get-tuple-element.32) | copy-start | bytes 25165828
  214.5 6.5 %copy-start.19 = (f32[64]{0:T(128)S(1)}, f32[64]{0:T(128)}, u32[]{:S(2)}) copy-start(f32[64]{0:T(128)} %param.19) | copy-start | bytes 772
  214.5 6.5 %copy-start.20 = (f32[64]{0:T(128)S(1)}, f32[64]{0:T(128)}, u32[]{:S(2)}) copy-start(f32[64]{0:T(128)} %param.18) | copy-start | bytes 772
  214.5 6.6 %slice-start = ((f32[1,4352]{1,0:T(1,128)}), f32[1,256]{1,0:T(1,128)S(1)}, s32[]{:S(2)}) async-start(f32[1,4352]{1,0:T(1,128)} %copy-done.14), calls=%async_computation.4 | async-start | bytes 2048 | tf_op jit(solution)/shard_map/slice | solution.py:1022
  214.5 6.6 %slice-start.1 = ((f32[4,4352]{1,0:T(4,128)}), f32[4,256]{1,0:T(4,128)S(1)}, s32[]{:S(2)}) async-start(f32[4,4352]{1,0:T(4,128)} %param.16), calls=%async_computation.5 | async-start | bytes 8192 | tf_op jit(solution)/shard_map/slice | solution.py:1022
  214.5 6.7 %copy-start.3 = (s32[1,2,4]{2,1,0:T(2,128)S(1)}, s32[1,2,4]{2,1,0:T(2,128)}, u32[]{:S(2)}) copy-start(s32[1,2,4]{2,1,0:T(2,128)} %param.13) | copy-start | bytes 100
  221.2 31.3 %copy-start.12 = (pred[512,128]{1,0:T(8,128)(4,1)S(1)}, pred[512,128]{1,0:T(8,128)(4,1)}, u32[]{:S(2)}) copy-start(pred[512,128]{1,0:T(8,128)(4,1)} %iota_compare_fusion.1) | copy-start | bytes 196612
  242.0 1.3 copy-start.1
  243.3 1.3 copy-start.6
  252.6 1.6 copy-start.2
  296.8 1.3 copy-start.4
  316.6 270.7 %reduce-scatter.3.cloned.1.call-start = ((), (), s32[]{:S(2)}) async-start(), calls=%async_computation.2 | async-start | bytes 9437184 | tf_op jit(solution)/shard_map/reduce_scatter | solution.py:1054
  342.5 3.1 copy-start.5
  549.9 3.6 copy-start.8
  549.9 3.6 copy-start.16
  552.2 34.6 %copy-start.18 = (f32[2,128]{1,0:T(2,128)S(1)}, f32[2,128]{1,0:T(2,128)}, u32[]{:S(2)}) copy-start(f32[2,128]{1,0:T(2,128)} %copy-done.17) | copy-start | bytes 3076
Sparse Core Ops, SparseCore 0:
  316.8 90.2 reduce-scatter.4
  409.3 119.5 reduce-scatter.2

commit v3 on v1

--- a/solution.py
+++ b/solution.py
@@ -57,6 +57,205 @@
     for item in range(starts_ref.shape[1]):
         count = count + (starts_ref[micro, item] <= positions).astype(jnp.int32)
     return count
+
+
+MESH = pl.DeviceIdType.MESH
+ANY = pl.BlockSpec(memory_space=pl.ANY)
+
+
+def greet(axes):
+    barrier = pltpu.get_barrier_semaphore()
+    waits = 0
+    for axis in axes:
+        count, me = lax.axis_size(axis), lax.axis_index(axis)
+
+        def hello(turn, carry):
+            pl.semaphore_signal(
+                barrier,
+                inc=1,
+                device_id={axis: lax.rem(me + turn, count)},
+                device_id_type=MESH,
+            )
+            return carry
+
+        lax.fori_loop(1, count, hello, 0)
+        waits += count - 1
+    pl.semaphore_wait(barrier, waits)
+
+
+def remote(source, target, send, receive, device):
+    return pltpu.make_async_remote_copy(
+        src_ref=source,
+        dst_ref=target,
+        send_sem=send,
+        recv_sem=receive,
+        device_id=device,
+        device_id_type=MESH,
+    )
+
+
+def share_kernel(axis, in_ref, out_ref, slots, send, receive):
+    count, me = lax.axis_size(axis), lax.axis_index(axis)
+    greet((axis,))
+
+    def copy(turn, owner):
+        peer = lax.rem(me + turn, count)
+        return remote(in_ref, slots.at[owner], send.at[peer], receive.at[owner], {axis: peer})
+
+    def start(turn, carry):
+        copy(turn, me).start()
+        return carry
+
+    def finish(turn, carry):
+        copy(turn, me).wait_send()
+        copy(turn, lax.rem(me + turn, count)).wait_recv()
+        return carry
+
+    lax.fori_loop(1, count, start, 0)
+    slots[me] = in_ref[...]
+    lax.fori_loop(1, count, finish, 0)
+
+    def add(owner, total):
+        return total + slots[owner]
+
+    out_ref[...] = lax.fori_loop(1, count, add, slots[0])
+
+
+def share(value, axis, collective_id):
+    count = lax.axis_size(axis)
+    return pl.pallas_call(
+        partial(share_kernel, axis),
+        in_specs=[pl.BlockSpec(memory_space=pltpu.VMEM)],
+        out_specs=pl.BlockSpec(memory_space=pltpu.VMEM),
+        out_shape=jax.ShapeDtypeStruct(value.shape, value.dtype),
+        scratch_shapes=[
+            pltpu.VMEM((count,) + value.shape, value.dtype),
+            pltpu.SemaphoreType.DMA((count,)),
+            pltpu.SemaphoreType.DMA((count,)),
+        ],
+        compiler_params=pltpu.CompilerParams(
+            collective_id=collective_id, has_side_effects=True, vmem_limit_bytes=48 << 20
+        ),
+        name="share_" + axis,
+    )(value)
+
+
+PARTS = 2
+
+
+class Line:
+    def __init__(self, source, out, sems):
+        self.source, self.out = source, out
+        self.up, self.down, self.receive, self.side_send, self.side_receive, self.keep = sems
+        self.me = lax.axis_index("seq")
+        self.chips = lax.axis_size("seq") // 2
+        self.chip, self.core = self.me // 2, lax.rem(self.me, 2)
+        self.block = source.shape[0]
+        self.piece = self.block // PARTS
+
+    def at(self, owner, part):
+        first = pl.multiple_of(owner * self.block + part * self.piece, 8)
+        return self.out.at[pl.ds(first, self.piece)]
+
+    def line(self, source, owner_chip, part, target_chip, sems):
+        return remote(
+            source,
+            self.at(owner_chip * 2 + self.core, part),
+            sems.at[owner_chip, part],
+            self.receive.at[owner_chip, part],
+            {"seq": target_chip * 2 + self.core},
+        )
+
+    def side(self, source, owner_chip, part, from_sibling):
+        core = 1 - self.core if from_sibling else self.core
+        return remote(
+            source,
+            self.at(owner_chip * 2 + core, part),
+            self.side_send.at[owner_chip, part],
+            self.side_receive.at[owner_chip, part],
+            {"seq": self.chip * 2 + 1 - self.core},
+        )
+
+    def stay(self):
+        first = pl.multiple_of(self.me * self.block, 8)
+        return pltpu.make_async_copy(
+            self.source, self.out.at[pl.ds(first, self.block)], self.keep.at[0]
+        )
+
+    def start(self):
+        for part in range(PARTS):
+            here = self.source.at[pl.ds(part * self.piece, self.piece)]
+
+            @pl.when(self.chip + 1 < self.chips)
+            def _():
+                self.line(here, self.chip, part, self.chip + 1, self.up).start()
+
+            @pl.when(self.chip >= 1)
+            def _():
+                self.line(here, self.chip, part, self.chip - 1, self.down).start()
+
+            self.side(here, self.chip, part, False).start()
+        self.stay().start()
+
+    def events(self):
+        return (self.chips - 1) * PARTS
+
+    def hop(self, event):
+        turn, part = event // PARTS + 1, lax.rem(event, PARTS)
+        below, above = self.chip - turn, self.chip + turn
+
+        @pl.when(below >= 0)
+        def _():
+            here = self.at(below * 2 + self.core, part)
+            self.line(here, below, part, self.chip, self.up).wait_recv()
+
+            @pl.when(self.chip + 1 < self.chips)
+            def _():
+                self.line(here, below, part, self.chip + 1, self.up).start()
+
+            self.side(here, below, part, False).start()
+
+        @pl.when(above < self.chips)
+        def _():
+            here = self.at(above * 2 + self.core, part)
+            self.line(here, above, part, self.chip, self.down).wait_recv()
+
+            @pl.when(self.chip >= 1)
+            def _():
+                self.line(here, above, part, self.chip - 1, self.down).start()
+
+            self.side(here, above, part, False).start()
+
+    def hops(self, first):
+        def body(event, carry):
+            self.hop(event)
+            return carry
+
+        lax.fori_loop(first, self.events(), body, 0)
+
+    def finish(self):
+        def body(owner_chip, carry):
+            for part in range(PARTS):
+                here = self.at(owner_chip * 2 + self.core, part)
+
+                @pl.when((owner_chip <= self.chip) & (self.chip + 1 < self.chips))
+                def _():
+                    self.line(here, owner_chip, part, self.chip + 1, self.up).wait_send()
+
+                @pl.when((owner_chip >= self.chip) & (self.chip >= 1))
+                def _():
+                    self.line(here, owner_chip, part, self.chip - 1, self.down).wait_send()
+
+                self.side(here, owner_chip, part, False).wait_send()
+                self.side(here, owner_chip, part, True).wait_recv()
+            return carry
+
+        lax.fori_loop(0, self.chips, body, 0)
+        self.stay().wait()
+
+
+def line_sems(chips):
+    return [pltpu.SemaphoreType.DMA((chips, PARTS))] * 5 + [pltpu.SemaphoreType.DMA((1,))]
 
 
 class Chunk:
@@ -128,26 +327,43 @@
     micros,
     heads,
     starts_ref,
-    proj_ref,
-    dnorm_ref,
+    x_ref,
+    weight_ref,
+    out_weight_ref,
+    g_ref,
     taps_ref,
     head_ref,
     cols_ref,
     expand_ref,
     tri_ref,
+    proj_ref,
     gg_ref,
+    branch_ref,
     mixed_ref,
     states_ref,
     tails_ref,
     sums_ref,
+    g_out,
     ext,
     state,
+    *sems,
 ):
-    chunk = pl.program_id(0)
-    rows = proj_ref.shape[0] // micros
+    chunk, chunks = pl.program_id(0), pl.num_programs(0)
+    rows = x_ref.shape[0] // micros
     width = heads * HEAD_DIM
     conv_width = 2 * STATE + width
     size, groups = head_groups(heads)
+    line = Line(g_ref, g_out, sems)
+    early = min((g_out.shape[0] // g_ref.shape[0] - 1) // 2, line.events())
+
+    @pl.when(chunk == 0)
+    def _():
+        greet(("seq",))
+        line.start()
+
+    @pl.when((lax.rem(chunk, 2) == 0) & (chunk >= 2) & (chunk // 2 - 1 < early))
+    def _():
+        line.hop(chunk // 2 - 1)
 
     @pl.when(chunk == 0)
     def _():
@@ -155,6 +371,7 @@
         state[...] = jnp.zeros_like(state)
 
     skip, gain, mask = cols_ref[0:1], cols_ref[1:2], cols_ref[2:3]
+    proj_ref[...] = mm(x_ref[...], weight_ref[...]).astype(BF16)
     sums = []
     for micro in range(micros):
         part = slice(micro * rows, (micro + 1) * rows)
@@ -191,15 +408,35 @@
         gated = mask * mixed * (gate * sigmoid(gate))
         gg_ref[part, :] = (gated * gain).astype(BF16)
         square = jnp.sum(gated * gated, axis=1, keepdims=True)
-        cross = jnp.sum(dnorm_ref[part, :] * gain * gated, axis=1, keepdims=True)
         lane = lax.broadcasted_iota(jnp.int32, (rows, LANES), 1)
-        both = jnp.where(lane == 0, square, jnp.where(lane == 1, cross, 0.0))
-        sums.append(both.T[:2])
+        sums.append(jnp.where(lane == 0, square, 0.0).T[:2])
         ext[micro, :8, :] = ext[micro, rows : rows + 8, :]
     pad = sums_ref.shape[0] - 2 * micros
     if pad:
         sums.append(jnp.zeros((pad, rows), F32))
     sums_ref[...] = jnp.concatenate(sums, axis=0)
+    branch_ref[...] = mm(gg_ref[...], out_weight_ref[...]).astype(BF16)
+
+    @pl.when(chunk == chunks - 1)
+    def _():
+        line.hops(early)
+        line.finish()
+
+
+def cross_kernel(micros, g_ref, out_weight_ref, gg_ref, sums_ref, dnorm_ref, both_ref):
+    rows = g_ref.shape[0] // micros
+    dnorm = mm_nt(g_ref[...], out_weight_ref[...])
+    dnorm_ref[...] = dnorm
+    cross = jnp.sum(dnorm * gg_ref[...].astype(F32), axis=1, keepdims=True)
+    lane = lax.broadcasted_iota(jnp.int32, (rows, LANES), 1)
+    lines = []
+    for micro in range(micros):
+        part = cross[micro * rows : (micro + 1) * rows]
+        lines.append(jnp.where(lane == 1, part, 0.0).T[:2])
+    pad = sums_ref.shape[0] - 2 * micros
+    if pad:
+        lines.append(jnp.zeros((pad, rows), F32))
+    both_ref[...] = sums_ref[...] + jnp.concatenate(lines, axis=0)
 
 
 def backward_kernel(
@@ -220,7 +457,6 @@
     gather_ref,
     tri_ref,
     dproj_ref,
-    gnorm_ref,
     gconv_ref,
     gcols_ref,
     ghead_ref,
@@ -275,7 +511,6 @@
         pull = root * root * root * sums[:, 2 * micro + 1 : 2 * micro + 2] * inverse_active
         dnorm = dnorm_ref[part, :]
         scaled = gated * root
-        gnorm_ref[part, :] = (scaled * gain).astype(BF16)
         d_gated = root * dnorm * gain - gated * pull
         d_gate = d_gated * masked * (gate_sig * (1.0 + gate * (1.0 - gate_sig)))
         d_mixed = mask * d_gated * gate_act
@@ -366,45 +601,98 @@
     return pl.BlockSpec(shape, lambda index: (0,) * len(shape))
 
 
-def run_forward(micros, heads, rows, chunks, starts, proj, dnorm, taps, head, cols, expand, tri):
+def run_forward(
+    micros, heads, rows, chunks, starts, x, weight, out_weight, g, taps, head, cols, expand, tri, collective_id
+):
     width = heads * HEAD_DIM
     conv_width = 2 * STATE + width
     block = micros * rows
     sum_rows = -(-2 * micros // 8) * 8
+    columns = weight.shape[1]
+    model_width = x.shape[1]
+
+    def whole(value):
+        return pl.BlockSpec(
+            value.shape, lambda index: (0,) * value.ndim, pipeline_mode=pl.Buffered(1)
+        )
+
+    def row_block(size):
+        return pl.BlockSpec((block, size), lambda index: (index, 0))
+
     return pl.pallas_call(
         partial(forward_kernel, micros, heads),
         grid=(chunks,),
         in_specs=[
             pl.BlockSpec(memory_space=pltpu.SMEM),
-            pl.BlockSpec((block, proj.shape[1]), lambda index: (index, 0)),
-            pl.BlockSpec((block, width), lambda index: (index, 0)),
-            constant(taps.shape),
-            constant(head.shape),
-            constant(cols.shape),
-            constant(expand.shape),
-            constant(tri.shape),
+            row_block(model_width),
+            whole(weight),
+            whole(out_weight),
+            ANY,
+            whole(taps),
+            whole(head),
+            whole(cols),
+            whole(expand),
+            whole(tri),
         ],
         out_specs=[
-            pl.BlockSpec((block, width), lambda index: (index, 0)),
-            pl.BlockSpec((block, width), lambda index: (index, 0)),
+            row_block(columns),
+            row_block(width),
+            row_block(model_width),
+            row_block(width),
             pl.BlockSpec((None, micros, STATE, width), lambda index: (index, 0, 0, 0)),
             pl.BlockSpec((None, micros, 8, conv_width), lambda index: (index, 0, 0, 0)),
             pl.BlockSpec((None, sum_rows, rows), lambda index: (index, 0, 0)),
+            ANY,
         ],
         out_shape=[
+            jax.ShapeDtypeStruct((chunks * block, columns), BF16),
             jax.ShapeDtypeStruct((chunks * block, width), BF16),
+            jax.ShapeDtypeStruct((chunks * block, model_width), BF16),
             jax.ShapeDtypeStruct((chunks * block, width), F32),
             jax.ShapeDtypeStruct((chunks, micros, STATE, width), BF16),
             jax.ShapeDtypeStruct((chunks, micros, 8, conv_width), F32),
             jax.ShapeDtypeStruct((chunks, sum_rows, rows), F32),
+            jax.ShapeDtypeStruct((chunks * block, model_width), BF16),
         ],
         scratch_shapes=[
             pltpu.VMEM((micros, rows + 8, conv_width), F32),
             pltpu.VMEM((micros, STATE, width), F32),
+        ]
+        + line_sems(chunks // 2),
+        compiler_params=pltpu.CompilerParams(
+            collective_id=collective_id, has_side_effects=True, vmem_limit_bytes=48 << 20
+        ),
+        cost_estimate=pl.CostEstimate(
+            flops=60 * 10**9, bytes_accessed=150 * 10**6, transcendentals=0
+        ),
+        name="mixer_forward",
+    )(starts, x, weight, out_weight, g, taps, head, cols, expand, tri)
+
+
+def run_cross(micros, chunks, g, out_weight, gg, sums):
+    block = g.shape[0] // chunks
+    width = gg.shape[1]
+    sum_block = pl.BlockSpec((None,) + sums.shape[1:], lambda index: (index, 0, 0))
+    return pl.pallas_call(
+        partial(cross_kernel, micros),
+        grid=(chunks,),
+        in_specs=[
+            pl.BlockSpec((block, g.shape[1]), lambda index: (index, 0)),
+            constant(out_weight.shape),
+            pl.BlockSpec((block, width), lambda index: (index, 0)),
+            sum_block,
         ],
-        compiler_params=pltpu.CompilerParams(vmem_limit_bytes=48 << 20),
-        name="mixer_forward",
-    )(starts, proj, dnorm, taps, head, cols, expand, tri)
+        out_specs=[pl.BlockSpec((block, width), lambda index: (index, 0)), sum_block],
+        out_shape=[
+            jax.ShapeDtypeStruct((g.shape[0], width), F32),
+            jax.ShapeDtypeStruct(sums.shape, F32),
+        ],
+        compiler_params=pltpu.CompilerParams(vmem_limit_bytes=32 << 20),
+        cost_estimate=pl.CostEstimate(
+            flops=8 * 10**9, bytes_accessed=16 * 10**6, transcendentals=0
+        ),
+        name="cross_sums",
+    )(g, out_weight, gg, sums)
 
 
 def run_backward(
@@ -459,14 +747,12 @@
         ],
         out_specs=[
             pl.BlockSpec((block, proj.shape[1]), back),
-            pl.BlockSpec((block, width), back),
             constant((8, conv_width)),
             constant((8, width)),
             constant((8, LANES)),
         ],
         out_shape=[
             jax.ShapeDtypeStruct((chunks * block, proj.shape[1]), BF16),
-            jax.ShapeDtypeStruct((chunks * block, width), BF16),
             jax.ShapeDtypeStruct((8, conv_width), F32),
             jax.ShapeDtypeStruct((8, width), F32),
             jax.ShapeDtypeStruct((8, LANES), F32),
@@ -477,6 +763,9 @@
             pltpu.VMEM((micros, STATE, width), F32),
         ],
         compiler_params=pltpu.CompilerParams(vmem_limit_bytes=48 << 20),
+        cost_estimate=pl.CostEstimate(
+            flops=40 * 10**9, bytes_accessed=80 * 10**6, transcendentals=0
+        ),
         name="mixer_backward",
     )(
         starts,
@@ -509,17 +798,586 @@
     )
 
 
+def gather_kernel(
+    x_ref,
+    w_ref,
+    x_out,
+    w_out,
+    w_send,
+    w_receive,
+    f_send,
+    f_receive,
+    keep,
+    *sems,
+):
+    seq_total, width_total = lax.axis_size("seq"), lax.axis_size("width")
+    me, mine = lax.axis_index("seq"), lax.axis_index("width")
+    quarter = w_ref.shape[1]
+    depth = quarter * width_total
+    line = Line(x_ref, x_out, sems)
+    greet(("seq", "width"))
+
+    def rows(source, group):
+        return pl.ds(pl.multiple_of(source * depth + group * quarter, 8), quarter)
+
+    def deal(turn, from_peer):
+        peer = lax.rem(me + turn, seq_total)
+        owner = peer if from_peer else me
+        return remote(
+            w_ref.at[peer],
+            w_out.at[rows(owner, mine)],
+            w_send.at[peer],
+            w_receive.at[owner],
+            {"seq": peer},
+        )
+
+    def deal_start(turn, carry):
+        deal(turn, False).start()
+        return carry
+
+    lax.fori_loop(1, seq_total, deal_start, 0)
+    w_own = pltpu.make_async_copy(w_ref.at[me], w_out.at[rows(me, mine)], keep.at[0])
+    w_own.start()
+    line.start()
+
+    def forward(source, turn, from_peer):
+        peer = lax.rem(mine + turn, width_total)
+        group = peer if from_peer else mine
+        where = w_out.at[rows(source, group)]
+        return remote(
+            where, where, f_send.at[peer, source], f_receive.at[group, source], {"width": peer}
+        )
+
+    def forward_start(source):
+        for turn in range(1, width_total):
+            forward(source, turn, False).start()
+
+    def deal_pass(turn, carry):
+        deal(turn, True).wait_recv()
+        forward_start(lax.rem(me + turn, seq_total))
+        return carry
+
+    w_own.wait()
+    forward_start(me)
+    lax.fori_loop(1, seq_total, deal_pass, 0)
+    line.hops(0)
+
+    def deal_end(turn, carry):
+        deal(turn, False).wait_send()
+        return carry
+
+    lax.fori_loop(1, seq_total, deal_end, 0)
+
+    def forward_end(source, carry):
+        for turn in range(1, width_total):
+            forward(source, turn, False).wait_send()
+            forward(source, turn, True).wait_recv()
+        return carry
+
+    lax.fori_loop(0, seq_total, forward_end, 0)
+    line.finish()
+
+
+def gather_rows(x, pieces, collective_id):
+    seq_total, width_total = lax.axis_size("seq"), lax.axis_size("width")
+    whole = (x.shape[0] * seq_total, x.shape[1])
+    weight = (seq_total * width_total * pieces.shape[1], pieces.shape[2])
+    dma = pltpu.SemaphoreType.DMA
+    return pl.pallas_call(
+        gather_kernel,
+        in_specs=[ANY] * 2,
+        out_specs=[ANY] * 2,
+        out_shape=[
+            jax.ShapeDtypeStruct(whole, x.dtype),
+            jax.ShapeDtypeStruct(weight, pieces.dtype),
+        ],
+        scratch_shapes=[
+            dma((seq_total,)),
+            dma((seq_total,)),
+            dma((width_total, seq_total)),
+            dma((width_total, seq_total)),
+            dma((1,)),
+        ]
+        + line_sems(seq_total // 2),
+        compiler_params=pltpu.CompilerParams(
+            collective_id=collective_id, has_side_effects=True
+        ),
+        cost_estimate=pl.CostEstimate(
+            flops=80 * 10**9, bytes_accessed=200 * 10**6, transcendentals=0
+        ),
+        name="gather_rows",
+    )(x, pieces)
+
+
+TILE = 256
+
+
+def home_kernel(
+    layout,
+    normed_ref,
+    dproj_ref,
+    columns_ref,
+    small_ref,
+    grad_ref,
+    gnorm_ref,
+    zx_ref,
+    bc_ref,
+    go_ref,
+    small_out,
+    blocks_in,
+    acc,
+    out_acc,
+    stage,
+    arrived,
+    sum_x,
+    sum_z,
+    sum_b,
+    out_stage,
+    out_arrived,
+    sum_out,
+    small_stage,
+    small_slots,
+    fetch,
+    hop_send,
+    hop_receive,
+    zx_send,
+    zx_receive,
+    bc_send,
+    bc_receive,
+    oh_send,
+    oh_receive,
+    go_send,
+    go_receive,
+    small_send,
+    small_receive,
+    last_send,
+    last_receive,
+):
+    seq_total, width_total, quarter, width, slots, shard, gain_row = layout
+    me, mine = lax.axis_index("seq"), lax.axis_index("width")
+    depth = quarter * width_total
+    conv_width = 2 * STATE + width
+    per_tile = TILE // depth
+    tiles = seq_total // per_tile
+    chunk_rows = blocks_in.shape[1]
+    chunks = normed_ref.shape[0] // chunk_rows
+    owners = seq_total // width_total
+    barrier = pltpu.get_barrier_semaphore()
+    count = seq_total * width_total
+    place = mine * seq_total + me
+
+    def fetch_copy(source, step):
+        tile, chunk = step // chunks, lax.rem(step, chunks)
+        return pltpu.make_async_copy(
+            source.at[
+                pl.ds(pl.multiple_of(chunk * chunk_rows, 8), chunk_rows),
+                pl.ds(pl.multiple_of(tile * TILE, TILE), TILE),
+            ],
+            blocks_in.at[lax.rem(step, 2)],
+            fetch.at[lax.rem(step, 2)],
+        )
+
+    fetch_copy(grad_ref, 0).start()
+
+    def hello(turn, carry):
+        peer = lax.rem(place + turn, count)
+        pl.semaphore_signal(
+            barrier,
+            inc=1,
+            device_id={"width": peer // seq_total, "seq": lax.rem(peer, seq_total)},
+            device_id_type=MESH,
+        )
+        return carry
+
+    lax.fori_loop(1, count, hello, 0)
+    pl.semaphore_wait(barrier, count - 1)
+
+    def both(is_here, source, target, send, receive, device, action):
+        if action != "send":
+
+            @pl.when(is_here)
+            def _():
+                stay = pltpu.make_async_copy(source, target, receive)
+                if action == "start":
+                    stay.start()
+                else:
+                    stay.wait()
+
+        @pl.when(jnp.logical_not(is_here))
+        def _():
+            away = remote(source, target, send, receive, device)
+            if action == "start":
+                away.start()
+            elif action == "receive":
+                away.wait_recv()
+            else:
+                away.wait_send()
+
+    sub, cols = out_stage.shape[2:]
+    per_out = TILE // cols
+
+    def out_hop(block, turn, from_peer):
+        peer = lax.rem(mine + turn, width_total)
+        group = peer if from_peer else mine
+        return remote(
+            out_stage.at[block, peer],
+            out_arrived.at[block, group],
+            oh_send.at[block, peer],
+            oh_receive.at[block, group],
+            {"width": peer},
+        )
+
+    def place_of(step):
+        tile, chunk = step // chunks, lax.rem(step, chunks)
+        first = pl.ds(pl.multiple_of(chunk * chunk_rows, 8), chunk_rows)
+        return tile, chunk, first, lax.rem(step, 2)
+
+    def out_multiply(step, carry):
+        tile, chunk, first, slot = place_of(step)
+        fetch_copy(grad_ref, step).wait()
+
+        @pl.when(step + 1 < tiles * chunks)
+        def _():
+            fetch_copy(grad_ref, step + 1).start()
+
+        @pl.when(step + 1 == tiles * chunks)
+        def _():
+            fetch_copy(normed_ref, 0).start()
+
+        part = mm_tn(gnorm_ref[first, :], blocks_in[slot])
+        if chunks > 1:
+            out_acc[...] = jnp.where(chunk == 0, part, out_acc[...] + part)
+        else:
+            out_acc[...] = part
+
+        @pl.when(chunk == chunks - 1)
+        def _():
+            for item in range(per_out):
+                block = tile * per_out + item
+                for group in range(width_total):
+                    out_stage[block, group] = out_acc[
+                        group * sub : (group + 1) * sub, item * cols : (item + 1) * cols
+                    ].astype(BF16)
+                for turn in range(1, width_total):
+                    out_hop(block, turn, False).start()
+
+        return carry
+
+    lax.fori_loop(0, tiles * chunks, out_multiply, 0)
+    go_owner = me // owners
+
+    def go_copy(target, action):
+        both(
+            (go_owner == mine) & (target == me),
+            sum_out.at[target],
+            go_ref.at[lax.rem(me, owners), mine],
+            go_send.at[target],
+            go_receive.at[lax.rem(me, owners), mine],
+            {"width": go_owner, "seq": target},
+            action,
+        )
+
+    small_stage[...] = small_ref[...]
+
+    def hop(block, turn, from_peer):
+        peer = lax.rem(mine + turn, width_total)
+        group = peer if from_peer else mine
+        return remote(
+            stage.at[block, peer],
+            arrived.at[block, group],
+            hop_send.at[block, peer],
+            hop_receive.at[block, group],
+            {"width": peer},
+        )
+
+    def multiply(step, carry):
+        tile, chunk, first, _ = place_of(step)
+        slot = lax.rem(step + tiles * chunks, 2)
+        fetch_copy(normed_ref, step).wait()
+
+        @pl.when(step + 1 < tiles * chunks)
+        def _():
+            fetch_copy(normed_ref, step + 1).start()
+
+        part = mm_tn(blocks_in[slot], dproj_ref[first, :])
+        if chunks > 1:
+            acc[...] = jnp.where(chunk == 0, part, acc[...] + part)
+        else:
+            acc[...] = part
+
+        @pl.when(chunk == chunks - 1)
+        def _():
+            for item in range(per_tile):
+                block = tile * per_tile + item
+                for group in range(width_total):
+                    row = item * depth + group * quarter
+                    stage[block, group] = acc[row : row + quarter].astype(BF16)
+                for turn in range(1, width_total):
+                    hop(block, turn, False).start()
+            weights = columns_ref[pl.ds(pl.multiple_of(tile * TILE, TILE), TILE), :]
+            product = (acc[...] * weights.astype(F32)).astype(BF16)
+            line = mm_nt(jnp.ones((8, product.shape[1]), BF16), product)
+            for item in range(TILE // LANES):
+                small_stage[pl.ds(gain_row + tile * (TILE // LANES) + item, 1), :] = line[
+                    :1, item * LANES : (item + 1) * LANES
+                ]
+
+        return carry
+
+    lax.fori_loop(0, tiles * chunks, multiply, 0)
+
+    def small_hop(turn, from_peer):
+        peer = lax.rem(mine + turn, width_total)
+        group = peer if from_peer else mine
+        return remote(
+            small_stage,
+            small_slots.at[group],
+            small_send.at[peer],
+            small_receive.at[group],
+            {"width": peer},
+        )
+
+    for turn in range(1, width_total):
+        small_hop(turn, False).start()
+    small_slots[mine] = small_stage[...]
+
+    def block_copy(sums, sem_row, number, block, second, action):
+        low = (number * width) // shard
+        high = ((number + 1) * width - 1) // shard
+        owner = high if second else low
+        slot = number - (owner * shard) // width
+
+        def act():
+            both(
+                (owner == mine) & (block == me),
+                sums.at[block],
+                zx_ref.at[slot, mine],
+                zx_send.at[sem_row, block],
+                zx_receive.at[slot, mine],
+                {"width": owner, "seq": block},
+                action,
+            )
+
+        if second:
+            pl.when(high != low)(act)
+        else:
+            act()
+
+    def bc_copy(block, action):
+        both(
+            (mine == width_total - 1) & (block == me),
+            sum_b.at[block],
+            bc_ref.at[me, mine],
+            bc_send.at[block],
+            bc_receive.at[me, mine],
+            {"width": width_total - 1, "seq": block},
+            action,
+        )
+
+    def pieces_of(block, action):
+        for second in (False, True):
+            block_copy(sum_z, int(second), me, block, second, action)
+            block_copy(sum_x, 2 + int(second), seq_total + me, block, second, action)
+        bc_copy(block, action)
+
+    def out_combine(block, carry):
+        total = out_stage[block, mine].astype(F32)
+        for turn in range(1, width_total):
+            out_hop(block, turn, True).wait_recv()
+            total = total + out_arrived[block, lax.rem(mine + turn, width_total)].astype(F32)
+        sum_out[block] = total.astype(BF16)
+        go_copy(block, "start")
+        return carry
+
+    lax.fori_loop(0, seq_total, out_combine, 0)
+
+    def combine(block, carry):
+        total = stage[block, mine].astype(F32)
+        for turn in range(1, width_total):
+            hop(block, turn, True).wait_recv()
+            total = total + arrived[block, lax.rem(mine + turn, width_total)].astype(F32)
+        low = total.astype(BF16)
+        sum_b[block, :, : 2 * STATE] = low[:, : 2 * STATE]
+        sum_x[block] = low[:, 2 * STATE : conv_width]
+        sum_z[block] = low[:, conv_width : conv_width + width]
+        sum_b[block, :, 2 * STATE :] = low[:, conv_width + width :]
+        pieces_of(block, "start")
+        return carry
+
+    lax.fori_loop(0, seq_total, combine, 0)
+
+    for turn in range(1, width_total):
+        small_hop(turn, True).wait_recv()
+        small_hop(turn, False).wait_send()
+    total = small_slots[0]
+    for group in range(1, width_total):
+        total = total + small_slots[group]
+    small_stage[...] = total
+
+    def last_hop(turn, from_peer):
+        peer = lax.rem(me + turn, seq_total)
+        owner = peer if from_peer else me
+        return remote(
+            small_stage,
+            small_out.at[owner],
+            last_send.at[peer],
+            last_receive.at[owner],
+            {"seq": peer},
+        )
+
+    def last_start(turn, carry):
+        last_hop(turn, False).start()
+        return carry
+
+    lax.fori_loop(1, seq_total, last_start, 0)
+    small_out[me] = small_stage[...]
+
+    def sent(block, carry):
+        for turn in range(1, width_total):
+            hop(block, turn, False).wait_send()
+            out_hop(block, turn, False).wait_send()
+        pieces_of(block, "send")
+        go_copy(block, "send")
+        return carry
+
+    lax.fori_loop(0, seq_total, sent, 0)
+
+    first = (mine * shard) // width
+
+    def landed(slot, carry):
+        number = first + slot
+        source = lax.rem(number, seq_total)
+
+        @pl.when((number < 2 * seq_total) & (number * width < (mine + 1) * shard))
+        def _():
+            for group in range(width_total):
+                both(
+                    (source == me) & (mine == group),
+                    sum_z.at[me],
+                    zx_ref.at[slot, group],
+                    zx_send.at[0, me],
+                    zx_receive.at[slot, group],
+                    {"width": group, "seq": source},
+                    "receive",
+                )
+
+        return carry
+
+    lax.fori_loop(0, slots, landed, 0)
+
+    @pl.when(mine == width_total - 1)
+    def _():
+        def bc_landed(source, carry):
+            for group in range(width_total):
+                both(
+                    (source == me) & (mine == group),
+                    sum_b.at[me],
+                    bc_ref.at[source, group],
+                    bc_send.at[me],
+                    bc_receive.at[source, group],
+                    {"width": group, "seq": source},
+                    "receive",
+                )
+            return carry
+
+        lax.fori_loop(0, seq_total, bc_landed, 0)
+
+    for item in range(owners):
+        for group in range(width_total):
+            source = mine * owners + item
+            both(
+                (source == me) & (mine == group),
+                sum_out.at[me],
+                go_ref.at[item, group],
+                go_send.at[me],
+                go_receive.at[item, group],
+                {"width": group, "seq": source},
+                "receive",
+            )
+
+    def last_end(turn, carry):
+        last_hop(turn, False).wait_send()
+        last_hop(turn, True).wait_recv()
+        return carry
+
+    lax.fori_loop(1, seq_total, last_end, 0)
+
+
+def bring_home(normed, dproj, columns, small, grad, gnorm, heads, gain_row, collective_id):
+    seq_total, width_total = lax.axis_size("seq"), lax.axis_size("width")
+    width = heads * HEAD_DIM
+    total_rows, model_width = normed.shape
+    depth = model_width // seq_total
+    quarter = depth // width_total
+    shard = (INNER + CONV + HEADS) // width_total
+    slots = max(
+        ((group + 1) * shard - 1) // width - group * shard // width + 1
+        for group in range(width_total)
+    )
+    all_columns = dproj.shape[1]
+    layout = (seq_total, width_total, quarter, width, slots, shard, gain_row)
+    rest = all_columns - 2 * width
+    sub, cols = width // width_total, model_width // seq_total
+    owners = seq_total // width_total
+    dma = pltpu.SemaphoreType.DMA
+    vmem = pl.BlockSpec(memory_space=pltpu.VMEM)
+    flops = 2 * total_rows * model_width * all_columns
+    return layout, pl.pallas_call(
+        partial(home_kernel, layout),
+        in_specs=[ANY, vmem, vmem, vmem, ANY, vmem],
+        out_specs=[ANY, ANY, ANY, vmem],
+        out_shape=[
+            jax.ShapeDtypeStruct((slots, width_total, quarter, width), BF16),
+            jax.ShapeDtypeStruct((seq_total, width_total, quarter, rest), BF16),
+            jax.ShapeDtypeStruct((owners, width_total, sub, cols), BF16),
+            jax.ShapeDtypeStruct((seq_total,) + small.shape, F32),
+        ],
+        scratch_shapes=[
+            pltpu.VMEM((2, min(total_rows, 2048), TILE), BF16),
+            pltpu.VMEM((TILE, all_columns), F32),
+            pltpu.VMEM((width, TILE), F32),
+            pltpu.VMEM((seq_total, width_total, quarter, all_columns), BF16),
+            pltpu.VMEM((seq_total, width_total, quarter, all_columns), BF16),
+            pltpu.VMEM((seq_total, quarter, width), BF16),
+            pltpu.VMEM((seq_total, quarter, width), BF16),
+            pltpu.VMEM((seq_total, quarter, rest), BF16),
+            pltpu.VMEM((seq_total, width_total, sub, cols), BF16),
+            pltpu.VMEM((seq_total, width_total, sub, cols), BF16),
+            pltpu.VMEM((seq_total, sub, cols), BF16),
+            pltpu.VMEM(small.shape, F32),
+            pltpu.VMEM((width_total,) + small.shape, F32),
+            dma((2,)),
+            dma((seq_total, width_total)),
+            dma((seq_total, width_total)),
+            dma((4, seq_total)),
+            dma((slots, width_total)),
+            dma((seq_total,)),
+            dma((seq_total, width_total)),
+            dma((seq_total, width_total)),
+            dma((seq_total, width_total)),
+            dma((seq_total,)),
+            dma((owners, width_total)),
+            dma((width_total,)),
+            dma((width_total,)),
+            dma((seq_total,)),
+            dma((seq_total,)),
+        ],
+        compiler_params=pltpu.CompilerParams(
+            collective_id=collective_id, has_side_effects=True, vmem_limit_bytes=56 << 20
+        ),
+        cost_estimate=pl.CostEstimate(
+            flops=4 * flops, bytes_accessed=8 * normed.size, transcendentals=0
+        ),
+        name="bring_home",
+    )(normed, dproj, columns, small, grad, gnorm)
+
+
 def input_norm(hidden, in_gain):
     return hidden * lax.rsqrt(jnp.mean(hidden * hidden, axis=1, keepdims=True) + EPSILON) * in_gain
 
 
 def own(value, start, count, axis=0):
     return lax.dynamic_slice_in_dim(value, start, count, axis)
-
-
-def placed(value, total, start):
-    whole = jnp.zeros(value.shape[:-1] + (total,), F32)
-    return lax.dynamic_update_slice_in_dim(whole, value, start, value.ndim - 1)
 
 
 def per_device(
@@ -551,20 +1409,19 @@
     flat_hidden = hidden_in[0].reshape(micros * rows, model_width).astype(F32)
     flat_grad = cotangent[0].reshape(micros * rows, model_width)
     normed, norm_back = jax.vjp(input_norm, flat_hidden, in_gain)
-    all_normed = lax.all_gather(normed.astype(BF16), "seq", axis=0, tiled=True)
-    all_grad = lax.all_gather(flat_grad, "seq", axis=0, tiled=True)
-
     dt_pad = LANES
-    gates = in_weight[:, :INNER].reshape(depth, seq_total, width)
-    xs = in_weight[:, INNER : 2 * INNER].reshape(depth, seq_total, width)
+    width_total = lax.axis_size("width")
+    quarter = depth // width_total
+    in_quarter = own(in_weight, group_index * quarter, quarter)
+    gates = in_quarter[:, :INNER].reshape(quarter, seq_total, width)
+    xs = in_quarter[:, INNER : 2 * INNER].reshape(quarter, seq_total, width)
     bc = jnp.broadcast_to(
-        in_weight[:, None, 2 * INNER : INNER + CONV], (depth, seq_total, 2 * STATE)
+        in_quarter[:, None, 2 * INNER : INNER + CONV], (quarter, seq_total, 2 * STATE)
     )
-    dts = in_weight[:, INNER + CONV :].reshape(depth, seq_total, heads)
+    dts = in_quarter[:, INNER + CONV :].reshape(quarter, seq_total, heads)
     dts = jnp.pad(dts, ((0, 0), (0, 0), (0, dt_pad - heads)))
     pieces = jnp.concatenate([bc, xs, gates, dts], axis=2).transpose(1, 0, 2)
-    columns = lax.all_to_all(pieces, "seq", split_axis=0, concat_axis=0)
-    columns = columns.reshape(seq_total * depth, columns.shape[2])
+    all_normed, columns = gather_rows(normed.astype(BF16), pieces, 0)
 
     conv_width = 2 * STATE + width
 
@@ -596,19 +1453,31 @@
     cols = jnp.pad(cols, ((0, 5), (0, 0)))
     expand, gather, tri = tables(heads, rows)
 
-    proj = mm(all_normed, columns).astype(BF16)
-    dnorm = mm_nt(all_grad, out_weight)
-    gg, mixed, states, tails, sums = run_forward(
-        micros, heads, rows, seq_total, starts[0], proj, dnorm, taps, head_table, cols, expand, tri
+    proj, gg, branch, mixed, states, tails, sums, all_grad = run_forward(
+        micros,
+        heads,
+        rows,
+        seq_total,
+        starts[0],
+        all_normed,
+        columns,
+        out_weight,
+        flat_grad,
+        taps,
+        head_table,
+        cols,
+        expand,
+        tri,
+        3,
     )
-    sums = lax.psum(sums, "seq")
-    branch = lax.psum_scatter(
-        mm(gg, out_weight).astype(BF16), "seq", scatter_dimension=0, tiled=True
-    )
-    squares = own(sums, seq_index, 1)[0, : 2 * micros : 2].reshape(micros * rows, 1)
-    output = flat_hidden + branch.astype(F32) * lax.rsqrt(squares / active + EPSILON)
-
-    dproj, gnorm, gconv, gcols, ghead = run_backward(
+    branch = lax.psum_scatter(branch, "seq", scatter_dimension=0, tiled=True)
+    dnorm, sums = run_cross(micros, seq_total, all_grad, out_weight, gg, sums)
+    sums = share(sums, "seq", 1)
+    roots = lax.rsqrt(sums[:, : 2 * micros : 2] / active + EPSILON)
+    own_roots = own(roots, seq_index, 1).reshape(micros * rows, 1)
+
+    gnorm = (gg.astype(F32) * roots.reshape(seq_total * micros * rows, 1)).astype(BF16)
+    dproj, gconv, gcols, ghead = run_backward(
         micros,
         heads,
         rows,
@@ -631,57 +1500,57 @@
     grad_normed = lax.psum_scatter(
         mm_nt(dproj, columns).astype(BF16), "seq", scatter_dimension=0, tiled=True
     ).astype(F32)
-    grad_hidden, grad_gain_in = norm_back(grad_normed)
+    grad_hidden = norm_back(grad_normed)[0]
     hidden_grads = (flat_grad.astype(F32) + grad_hidden).astype(BF16)
 
-    grad_out = mm_tn(gnorm, all_grad).astype(BF16)
-    grad_out = grad_out.reshape(width, seq_total, model_width // seq_total).transpose(1, 0, 2)
-    grad_out = lax.all_to_all(grad_out, "seq", split_axis=0, concat_axis=0)
-    grad_out = grad_out.reshape(seq_total * width, model_width // seq_total)
-    shard_out = lax.psum_scatter(
-        grad_out.astype(F32), "width", scatter_dimension=0, tiled=True
-    )
-
-    grad_in = mm_tn(all_normed, dproj).astype(BF16)[:, : conv_width + width + heads]
-    grad_in = grad_in.reshape(seq_total, depth, grad_in.shape[1])
-    grad_in = lax.all_to_all(grad_in, "seq", split_axis=0, concat_axis=0)
-    grad_in = grad_in.astype(F32)
-
-    def joined(value):
-        return value.transpose(1, 0, 2).reshape(depth, seq_total * value.shape[2])
-
-    grad_in = jnp.concatenate(
+    skip_heads = jnp.sum(gcols[0].reshape(heads, HEAD_DIM), axis=1)
+    shared_part = gconv[:5, : 2 * STATE].reshape(-1)
+    gain_row = shared_part.shape[0] // LANES
+    own_part = jnp.concatenate(
         [
-            joined(grad_in[:, :, conv_width : conv_width + width]),
-            joined(grad_in[:, :, 2 * STATE : conv_width]),
-            jnp.sum(grad_in[:, :, : 2 * STATE], axis=0),
-            joined(grad_in[:, :, conv_width + width :]),
-        ],
-        axis=1,
-    )
-    shard_in = lax.psum_scatter(grad_in, "width", scatter_dimension=1, tiled=True)
-
-    skip_heads = jnp.sum(gcols[0].reshape(heads, HEAD_DIM), axis=1)
-    conv_small = jnp.concatenate(
-        [placed(gconv[:5, 2 * STATE :], INNER, col_first), gconv[:5, : 2 * STATE]], axis=1
-    )
-    small = jnp.concatenate(
-        [
-            conv_small.reshape(-1),
-            grad_gain_in,
-            placed(gcols[1], INNER, col_first),
-            placed(ghead[1, :heads], HEADS, head_first),
-            placed(ghead[0, :heads], HEADS, head_first),
-            placed(skip_heads, HEADS, head_first),
+            gconv[:5, 2 * STATE :].reshape(-1),
+            gcols[1],
+            ghead[1, :heads],
+            ghead[0, :heads],
+            skip_heads,
         ]
     )
-    small = lax.psum(small, ("width", "seq"))
-    edge = 5 * CONV
-    conv_small = small[:edge].reshape(5, CONV)
-    in_gain_sum = small[edge : edge + model_width]
-    edge = edge + model_width
-    gain_sum = small[edge : edge + INNER]
-    edge = edge + INNER
+    small = jnp.concatenate([shared_part, jnp.zeros(model_width, F32), own_part])
+    length = small.shape[0]
+    small = jnp.pad(small, (0, -length % (8 * LANES))).reshape(-1, LANES)
+    small, branch = lax.optimization_barrier((small, branch))
+    layout, (zx, bcs, grad_out, small) = bring_home(
+        all_normed, dproj, columns, small, all_grad, gnorm, heads, gain_row, 2
+    )
+    output = flat_hidden + branch.astype(F32) * own_roots
+    slots, shard = layout[4], layout[5]
+    tail = 2 * STATE + HEADS
+    bcs = bcs.reshape(seq_total, depth, bcs.shape[3])
+    bc_sum = jnp.sum(bcs[:, :, : 2 * STATE].astype(F32), axis=0).astype(BF16)
+    dt_sum = bcs[:, :, 2 * STATE : 2 * STATE + heads].transpose(1, 0, 2).reshape(depth, HEADS)
+    tail_slots = -(-tail // width)
+    ends = jnp.pad(
+        jnp.concatenate([bc_sum, dt_sum], axis=1), ((0, 0), (0, tail_slots * width - tail))
+    )
+    zx = zx.reshape(slots, depth, width).transpose(1, 0, 2).reshape(depth, slots * width)
+    is_last = group_index == width_total - 1
+    edge = (slots - tail_slots) * width
+    zx = jnp.concatenate([zx[:, :edge], jnp.where(is_last, ends, zx[:, edge:])], axis=1)
+    start = lax.rem(group_index * shard, width)
+    shard_in = own(zx, start, shard, 1).astype(F32)
+    shard_out = grad_out.reshape(seq_total // width_total * width, -1).astype(F32)
+    small = small.reshape(seq_total, -1)
+    shared_part = jnp.sum(small[:, : gain_row * LANES + model_width], axis=0)
+    own_part = small[:, gain_row * LANES + model_width : length]
+
+    bc_small = shared_part[: 10 * STATE].reshape(5, 2 * STATE)
+    in_gain_sum = shared_part[10 * STATE :] / in_gain
+    x_small = own_part[:, : 5 * width].reshape(seq_total, 5, width)
+    x_small = x_small.transpose(1, 0, 2).reshape(5, INNER)
+    conv_small = jnp.concatenate([x_small, bc_small], axis=1)
+    gain_sum = own_part[:, 5 * width : 6 * width].reshape(INNER)
+    head_sums = own_part[:, 6 * width :].reshape(seq_total, 3, heads)
+    head_sums = head_sums.transpose(1, 0, 2).reshape(3, HEADS)
     shape = hidden_in.shape
     return (
         output.astype(BF16).reshape(shape),
@@ -690,9 +1559,9 @@
         shard_in,
         conv_small[:4],
         conv_small[4],
-        small[edge : edge + HEADS],
-        small[edge + HEADS : edge + 2 * HEADS],
-        small[edge + 2 * HEADS : edge + 3 * HEADS],
+        head_sums[0],
+        head_sums[1],
+        head_sums[2],
         gain_sum,
         shard_out,
     )

time: 1030 us -> 491 us (0.48)
  the two profiles are of different devices: /device:TPU:0 before, /device:TPU:31 now
where the time goes in v3:
time: 491 us; the launch traced here: 489 us
  Pallas kernels  390 us (79%)
  local copies, waits for them, and re-layouts  46.2 us (9%)
  other arithmetic  19.2 us (4%)
  matrix products  18.5 us (4%)
  between operations  14.6 us (3%)
    pallas_call x1, Pallas kernels, bring_home(): pl.pallas_call(partial(home_kernel, layout), in_specs=[ANY, vmem, vmem, v...  151 us
    pallas_call x1, Pallas kernels, gather_rows(): pl.pallas_call(gather_kernel, in_specs=[ANY] * 2, out_specs=[ANY] * 2, ou...  97.6 us
    pallas_call x1, Pallas kernels, run_forward(): pl.pallas_call(partial(forward_kernel, micros, heads), grid=(chunks,), in...  78.6 us
    pallas_call x1, Pallas kernels, run_backward(): pl.pallas_call(partial(backward_kernel, micros, heads), grid=(chunks,), i...  42.3 us
    unnamed x73, local copies, waits for them, and re-layouts  19.9 us
    dot_general x1, matrix products, mm_nt(): lax.dot_general(a, b, (((1,), (1,)), ((), ())), preferred_element_type=F32)  18.5 us
    pallas_call x1, Pallas kernels, share(): pl.pallas_call(partial(share_kernel, axis), in_specs=[pl.BlockSpec(memory...  13.6 us
  transfers between devices with their start and end apart: 2, of which 0 were waited for; matrix products, arithmetic and copies ran while one was open for 7% of the time, Pallas kernels for 44%

profile of v3, /device:TPU:31, one launch (start us, length us, event | category | flops | bytes accessed | tf_op | source)
XLA Modules:
  0.0 489.1 jit_solution(1698969599443566461)
XLA Ops:
  7.3 0.7 constant_dynamic-slice_fusion.2
  8.0 0.8 dynamic-slice.3
  8.7 0.7 broadcast_in_dim.35
  9.5 1.5 fusion.3
  11.6 0.7 dynamic_slice.32
  12.7 0.8 dynamic-slice_bitcast_fusion
  13.5 0.9 dynamic-slice.4
  14.5 0.8 copy.46
  15.3 2.3 fusion.21
  17.7 1.1 copy.47
  19.3 0.8 dynamic_slice.33
  20.1 1.3 fusion.5.x_ref
  21.4 1.2 fusion.9.w_ref
  22.7 97.6 %gather_rows.1 = (bf16[2048,2048]{1,0:T(8,128)(2,1)}, bf16[2048,1408]{1,0:T(8,128)(2,1)}) custom-call(bf16[256,2048]{1,0:T(8,128)(2,1)} %fusion.5.x_ref, bf16[8,64,1408]{2,1,0:T(8,128)(2,1)} %fusion.9.w_ref), custom_call_target="tpu_custom_call" | custom-call | flops 80000000000 | bytes 200000000 | tf_op jit(solution)/shard_map/gather_rows/pallas_call | solution.py:886
  120.4 78.6 %mixer_forward.1 = (bf16[2048,1408]{1,0:T(8,128)(2,1)}, bf16[2048,512]{1,0:T(8,128)(2,1)S(1)}, bf16[2048,2048]{1,0:T(8,128)(2,1)}, f32[2048,512]{1,0:T(8,128)}, ...) custom-call(s32[2,4]{1,0:T(2,128)S(1)} %bitcast.77, ...), custom_call_target="tpu_custom_call" | custom-call | flops 60000002048 | bytes 150000000 | tf_op jit(solution)/shard_map/mixer_forward/pallas_call | solution.py:622
  199.0 1.3 copy-done.6
  200.4 0.7 copy-done.8
  201.4 1.6 copy-done.2
  203.0 3.4 copy-done.4
  206.3 6.8 %cross_sums.1 = (f32[2048,512]{1,0:T(8,128)S(1)}, f32[8,8,128]{2,1,0:T(8,128)S(1)}) custom-call(bf16[2048,2048]{1,0:T(8,128)(2,1)S(1)} %copy-done.4, bf16[512,2048]{1,0:T(8,128)(2,1)S(1)} %copy-done.2, bf16[2048,512]{1,0:T(8,128)(2,1)S(1)} %get-tuple-element.37.gg_ref, f32[8,8,128]{2,1,0:T(8,128)S(1)} %get-tuple-element.38.sums_ref), custom_call_target="tpu_custom_call" | custom-call | flops 8000000000 | bytes 16000000 | tf_op jit(solution)/shard_map/cross_sums/pallas_call | solution.py:676
  213.2 1.9 copy-done.5
  215.1 13.6 %share_seq.1.sums_ref = f32[8,8,128]{2,1,0:T(8,128)S(1)} custom-call(f32[8,8,128]{2,1,0:T(8,128)S(1)} %get-tuple-element.43.in_ref), custom_call_target="tpu_custom_call" | custom-call | tf_op jit(solution)/shard_map/share_seq/pallas_call | solution.py:126
  229.0 1.6 copy-done.7
  230.6 1.0 copy-done.9
  231.6 42.3 %mixer_backward.1 = (bf16[2048,1408]{1,0:T(8,128)(2,1)}, f32[8,768]{1,0:T(8,128)S(1)}, f32[8,512]{1,0:T(8,128)S(1)}, f32[8,128]{1,0:T(8,128)S(1)}) custom-call(s32[2,4]{1,0:T(2,128)S(1)} %bitcast.78, f32[1]{0:T(128)} %bitcast.2.active_ref, bf16[2048,1408]{1,0:T(8,128)(2,1)} %get-tuple-element.35.proj_ref, f32[2048,512]{1,0:T(8,128)} %copy-done.5, ...), custom_call_target="tpu_custom_call" | custom-call | flops 40000000000 | bytes 80000000 | tf_op jit(solution)/shard_map/mixer_backward/pallas_call | solution.py:725
  274.5 18.5 %convolution_convert_fusion = bf16[2048,2048]{1,0:T(8,128)(2,1)} fusion(bf16[2048,1408]{1,0:T(8,128)(2,1)} %get-tuple-element.49.dproj_ref, bf16[2048,1408]{1,0:T(8,128)(2,1)} %get-tuple-element.34.weight_ref.columns_ref), kind=kOutput, calls=%fused_computation | convolution fusion | flops 11815354368 | bytes 19922944 | tf_op jit(solution)/shard_map/dot_general | solution.py:28
  293.1 0.8 slice_reduce_fusion.6
  295.5 1.8 multiply_convert_fusion.gnorm_ref
  297.2 151.3 %bring_home.1 = (bf16[5,4,64,512]{3,2,1,0:T(8,128)(2,1)}, bf16[8,4,64,384]{3,2,1,0:T(8,128)(2,1)}, bf16[2,4,128,256]{3,2,1,0:T(8,128)(2,1)}, f32[8,56,128]{2,1,0:T(8,128)}) custom-call(bf16[2048,2048]{1,0:T(8,128)(2,1)} %get-tuple-element.33.x_ref.normed_ref, bf16[2048,1408]{1,0:T(8,128)(2,1)} %get-tuple-element.49.dproj_ref, ...), custom_call_target="tpu_custom_call" | custom-call | flops 47244640256 | bytes 33554432 | tf_op jit(solution)/shard_map/bring_home/pallas_call | solution.py:1325
  448.5 1.0 copy.64
  450.2 1.6 copy.49
  451.8 0.7 slice.136
  452.5 1.0 slice.133
  453.5 0.9 slice_reduce_fusion.1
  455.2 1.9 slice.135
  458.5 1.3 slice_bitcast_fusion
  459.9 1.6 fusion.7
  462.8 1.5 slice_reduce_fusion.3
  464.2 1.3 squeeze.32
  466.7 1.3 copy.62
  468.0 1.8 copy.58
  469.9 1.5 copy.51
  471.3 0.8 copy.59
  472.2 1.6 fusion.15
  473.8 1.1 copy.53
  474.9 2.1 bitcast_convert_fusion
  477.0 2.9 fusion.11
  479.9 2.4 fusion.2
  (118 shorter events, 9.6 us)
Async XLA Ops:
  7.2 290.1 %reduce-scatter.3.cloned.1.call-start = ((), (), s32[]{:S(2)}) async-start(), calls=%async_computation.2 | async-start | bytes 9437184 | tf_op jit(solution)/shard_map/reduce_scatter | solution.py:1473
  7.2 10.4 %copy-start.23 = (s32[512]{0:T(512)}, s32[512]{0:T(512)S(1)}, u32[]{:S(2)}) copy-start(s32[512]{0:T(512)S(1)} %add_select_fusion) | copy-start | bytes 6148
  9.5 8.1 %copy-start.22 = (f32[1,4352]{1,0:T(1,128)}, f32[1,4352]{1,0:T(1,128)S(1)}, u32[]{:S(2)}) copy-start(f32[1,4352]{1,0:T(1,128)S(1)} %broadcast_in_dim.35) | copy-start | bytes 52228
  11.0 0.6 copy-start.27
  11.1 9.0 %copy-start.25 = (f32[256]{0:T(256)}, f32[256]{0:T(256)S(1)}, u32[]{:S(2)}) copy-start(f32[256]{0:T(256)S(1)} %bitcast_rsqrt_fusion) | copy-start | bytes 3076
  17.6 1.6 copy-start.31
  17.6 1.6 copy-start.32
  17.6 2.5 copy-start.10
  17.7 2.5 copy-start.20
  18.8 2.6 copy-start.14
  19.1 2.3 copy-start.19
  22.7 97.6 %slice-start = ((f32[1,4352]{1,0:T(1,128)}), f32[1,256]{1,0:T(1,128)S(1)}, s32[]{:S(2)}) async-start(f32[1,4352]{1,0:T(1,128)} %copy-done.22), calls=%async_computation.4 | async-start | bytes 2048 | tf_op jit(solution)/shard_map/slice | solution.py:1430
  22.7 97.6 %slice-start.1 = ((f32[4,4352]{1,0:T(4,128)}), f32[4,256]{1,0:T(4,128)S(1)}, s32[]{:S(2)}) async-start(f32[4,4352]{1,0:T(4,128)} %param.16), calls=%async_computation.5 | async-start | bytes 8192 | tf_op jit(solution)/shard_map/slice | solution.py:1430
  22.7 97.7 %copy-start = (bf16[1,2,128,2048]{3,2,1,0:T(8,128)(2,1)S(1)}, bf16[1,2,128,2048]{3,2,1,0:T(8,128)(2,1)}, u32[]{:S(2)}) copy-start(bf16[1,2,128,2048]{3,2,1,0:T(8,128)(2,1)} %param.23) | copy-start | bytes 3145732
  22.7 97.7 %copy-start.3 = (s32[1,2,4]{2,1,0:T(2,128)S(1)}, s32[1,2,4]{2,1,0:T(2,128)}, u32[]{:S(2)}) copy-start(s32[1,2,4]{2,1,0:T(2,128)} %param.13) | copy-start | bytes 100
  199.0 1.3 copy-start.6
  200.4 0.7 copy-start.8
  201.1 258.7 %reduce-scatter.5.cloned.1.call-start = ((), (), s32[]{:S(2)}) async-start(), calls=%async_computation.3 | async-start | bytes 9437184 | tf_op jit(solution)/shard_map/reduce_scatter | solution.py:1500
  201.4 1.6 copy-start.2
  203.0 3.4 copy-start.4
  206.3 22.5 %copy-start.24 = (s32[512]{0:T(512)S(1)}, s32[512]{0:T(512)}, u32[]{:S(2)}) copy-start(s32[512]{0:T(512)} %copy-done.23) | copy-start | bytes 6148
  213.2 2.0 copy-start.5
  229.0 1.7 copy-start.7
  230.6 1.0 copy-start.9
  273.9 0.6 copy-start.1
  449.5 0.7 copy-start.18
  452.5 5.4 %copy-start.21 = (f32[2048]{0:T(1024)S(1)}, f32[2048]{0:T(1024)}, u32[]{:S(2)}) copy-start(f32[2048]{0:T(1024)} %param.14) | copy-start | bytes 24580
  452.5 7.4 %copy-start.11 = (bf16[1,2,128,2048]{3,2,1,0:T(8,128)(2,1)S(1)}, bf16[1,2,128,2048]{3,2,1,0:T(8,128)(2,1)}, u32[]{:S(2)}) copy-start(bf16[1,2,128,2048]{3,2,1,0:T(8,128)(2,1)} %param.12) | copy-start | bytes 3145732
  454.5 3.3 copy-start.15
  455.2 6.3 %copy-start.28 = (f32[2,128]{1,0:T(2,128)S(1)}, f32[2,128]{1,0:T(2,128)}, u32[]{:S(2)}) copy-start(f32[2,128]{1,0:T(2,128)} %copy-done.27) | copy-start | bytes 3076
  457.1 14.2 %copy-start.17 = (bf16[256,512]{0,1:T(8,128)(2,1)S(1)}, bf16[256,512]{0,1:T(8,128)(2,1)}, u32[]{:S(2)}) copy-start(bf16[256,512]{0,1:T(8,128)(2,1)} %slice.136) | copy-start | bytes 786436
  461.5 15.5 %copy-start.13 = (bf16[256,2048]{0,1:T(8,128)(2,1)S(1)}, bf16[256,2048]{0,1:T(8,128)(2,1)}, u32[]{:S(2)}) copy-start(bf16[256,2048]{0,1:T(8,128)(2,1)} %slice.133) | copy-start | bytes 3145732
  477.0 2.9 copy-start.12
  477.0 2.9 copy-start.16
  477.0 2.9 copy-start.26
  477.0 2.9 copy-start.29
  477.0 2.9 copy-start.30
Sparse Core Ops, SparseCore 0:
  201.2 91.6 reduce-scatter.2
  295.2 122.8 reduce-scatter.4

commit v4 on v3

v4 whole, which is shorter than its diff:
```python
from functools import partial

import jax
import jax.numpy as jnp
from jax import lax
from jax.experimental import pallas as pl
from jax.experimental.pallas import tpu as pltpu
from jax.sharding import PartitionSpec as P

INNER = 4096
HEADS = 64
HEAD_DIM = 64
STATE = 128
CONV = 4352
EPSILON = 1e-05
LANES = 128
TAPS = 4
NEG = -1e30
F32 = jnp.float32
BF16 = jnp.bfloat16


def mm(a, b):
    return lax.dot_general(a, b, (((1,), (0,)), ((), ())), preferred_element_type=F32)


def mm_nt(a, b):
    return lax.dot_general(a, b, (((1,), (1,)), ((), ())), preferred_element_type=F32)


def mm_tn(a, b):
    return lax.dot_general(a, b, (((0,), (0,)), ((), ())), preferred_element_type=F32)


def halves(value, axis):
    high = value.astype(BF16)
    low = (value - high.astype(F32)).astype(BF16)
    return jnp.concatenate([high, low], axis=axis)


def sigmoid(value):
    return 0.5 * jnp.tanh(0.5 * value) + 0.5


def prefix_sum(tri, value):
    high = value.astype(BF16)
    rest = value - high.astype(F32)
    middle = rest.astype(BF16)
    low = (rest - middle.astype(F32)).astype(BF16)
    parts = mm(tri, jnp.concatenate([high, middle, low], axis=1))
    width = value.shape[1]
    return parts[:, :width] + parts[:, width : 2 * width] + parts[:, 2 * width :]


def doc_number(starts_ref, micro, positions):
    count = jnp.zeros_like(positions)
    for item in range(starts_ref.shape[1]):
        count = count + (starts_ref[micro, item] <= positions).astype(jnp.int32)
    return count


MESH = pl.DeviceIdType.MESH
ANY = pl.BlockSpec(memory_space=pl.ANY)


def greet(axes):
    barrier = pltpu.get_barrier_semaphore()
    waits = 0
    for axis in axes:
        count, me = lax.axis_size(axis), lax.axis_index(axis)

        def hello(turn, carry):
            pl.semaphore_signal(
                barrier,
                inc=1,
                device_id={axis: lax.rem(me + turn, count)},
                device_id_type=MESH,
            )
            return carry

        lax.fori_loop(1, count, hello, 0)
        waits += count - 1
    pl.semaphore_wait(barrier, waits)


def remote(source, target, send, receive, device):
    return pltpu.make_async_remote_copy(
        src_ref=source,
        dst_ref=target,
        send_sem=send,
        recv_sem=receive,
        device_id=device,
        device_id_type=MESH,
    )


class Line:
    def __init__(self, source, out, sems):
        self.source, self.out = source, out
        self.up, self.down, self.receive, self.side_send, self.side_receive, self.keep = sems
        self.me = lax.axis_index("seq")
        self.chips = lax.axis_size("seq") // 2
        self.chip, self.core = self.me // 2, lax.rem(self.me, 2)
        self.parts, self.rows = source.shape[:2]

    def at(self, owner, part):
        return self.out.at[part, pl.ds(pl.multiple_of(owner * self.rows, 8), self.rows)]

    def line(self, source, owner_chip, part, target_chip, sems):
        return remote(
            source,
            self.at(owner_chip * 2 + self.core, part),
            sems.at[owner_chip, part],
            self.receive.at[owner_chip, part],
            {"seq": target_chip * 2 + self.core},
        )

    def side(self, source, owner_chip, part, from_sibling):
        core = 1 - self.core if from_sibling else self.core
        return remote(
            source,
            self.at(owner_chip * 2 + core, part),
            self.side_send.at[owner_chip, part],
            self.side_receive.at[owner_chip, part],
            {"seq": self.chip * 2 + 1 - self.core},
        )

    def stay(self, part):
        return pltpu.make_async_copy(
            self.source.at[part], self.at(self.me, part), self.keep.at[part]
        )

    def start(self):
        for part in range(self.parts):
            here = self.source.at[part]

            @pl.when(self.chip + 1 < self.chips)
            def _():
                self.line(here, self.chip, part, self.chip + 1, self.up).start()

            @pl.when(self.chip >= 1)
            def _():
                self.line(here, self.chip, part, self.chip - 1, self.down).start()

            self.side(here, self.chip, part, False).start()
            self.stay(part).start()

    def events(self):
        return (self.chips - 1) * self.parts

    def hop(self, event):
        turn, part = event // self.parts + 1, lax.rem(event, self.parts)
        below, above = self.chip - turn, self.chip + turn

        @pl.when(below >= 0)
        def _():
            here = self.at(below * 2 + self.core, part)
            self.line(here, below, part, self.chip, self.up).wait_recv()

            @pl.when(self.chip + 1 < self.chips)
            def _():
                self.line(here, below, part, self.chip + 1, self.up).start()

            self.side(here, below, part, False).start()

        @pl.when(above < self.chips)
        def _():
            here = self.at(above * 2 + self.core, part)
            self.line(here, above, part, self.chip, self.down).wait_recv()

            @pl.when(self.chip >= 1)
            def _():
                self.line(here, above, part, self.chip - 1, self.down).start()

            self.side(here, above, part, False).start()

    def hops(self, first):
        def body(event, carry):
            self.hop(event)
            return carry

        lax.fori_loop(first, self.events(), body, 0)

    def finish(self):
        def body(owner_chip, carry):
            for part in range(self.parts):
                here = self.at(owner_chip * 2 + self.core, part)

                @pl.when((owner_chip <= self.chip) & (self.chip + 1 < self.chips))
                def _():
                    self.line(here, owner_chip, part, self.chip + 1, self.up).wait_send()

                @pl.when((owner_chip >= self.chip) & (self.chip >= 1))
                def _():
                    self.line(here, owner_chip, part, self.chip - 1, self.down).wait_send()

                self.side(here, owner_chip, part, False).wait_send()
                self.side(here, owner_chip, part, True).wait_recv()
            return carry

        lax.fori_loop(0, self.chips, body, 0)
        for part in range(self.parts):
            self.stay(part).wait()


def line_sems(chips, parts):
    return [pltpu.SemaphoreType.DMA((chips, parts))] * 5 + [pltpu.SemaphoreType.DMA((parts,))]


class Chunk:
    def __init__(self, starts_ref, micro, chunk, rows, raw_dt, head_ref, expand, tri):
        first = chunk * rows
        column = lax.broadcasted_iota(jnp.int32, (rows, 1), 0) + first
        line = lax.broadcasted_iota(jnp.int32, (1, rows), 1) + first
        doc_col = doc_number(starts_ref, micro, column)
        doc_row = doc_number(starts_ref, micro, line)
        self.same = [
            (doc_number(starts_ref, micro, column - offset) == doc_col).astype(F32)
            for offset in range(1, TAPS)
        ]
        before = jnp.int32(0)
        last = jnp.int32(0)
        for item in range(starts_ref.shape[1]):
            before = before + (starts_ref[micro, item] <= first - 1).astype(jnp.int32)
            last = last + (starts_ref[micro, item] <= first + rows - 1).astype(jnp.int32)
        carry = (doc_col == before).astype(F32)
        same_last = (doc_col == last).astype(F32)
        self.bias = jnp.where((column >= line) & (doc_col == doc_row), 0.0, NEG)
        self.shifted_dt = raw_dt + head_ref[0:1]
        self.step = jnp.maximum(self.shifted_dt, 0.0) + jnp.log1p(
            jnp.exp(-jnp.abs(self.shifted_dt))
        )
        self.log_keep = self.step * head_ref[1:2]
        self.cum = prefix_sum(tri, self.log_keep)
        self.cum_t = self.cum.T
        carried = jnp.exp(self.cum) * carry
        left = jnp.exp(self.cum[rows - 1 :] - self.cum) * same_last
        spread = mm(
            halves(jnp.concatenate([self.step, carried, left], axis=0), 1), expand
        )
        self.step_cols = spread[:rows]
        self.carry_cols = spread[rows : 2 * rows]
        self.left_cols = spread[2 * rows :]
        self.keep_all = self.carry_cols[rows - 1 :]

    def decay(self, head):
        return jnp.exp(self.cum[:, head : head + 1] - self.cum_t[head : head + 1] + self.bias)


def head_groups(heads):
    size = 2 if heads % 2 == 0 else 1
    return size, heads // size


def stacked(value, size):
    if size == 1:
        return value.astype(BF16)
    lane = lax.broadcasted_iota(jnp.int32, value.shape, 1)
    first = jnp.where(lane < HEAD_DIM, value, 0.0)
    second = jnp.where(lane < HEAD_DIM, 0.0, value)
    return jnp.concatenate([first, second], axis=0).astype(BF16)


def convolved(ext, micro, rows, taps_ref, same):
    current = ext[micro, 8 : 8 + rows, :]
    total = taps_ref[TAPS : TAPS + 1] + taps_ref[TAPS - 1 : TAPS] * current
    views = []
    for offset in range(1, TAPS):
        view = ext[micro, 8 - offset : 8 - offset + rows, :] * same[offset - 1]
        views.append(view)
        total = total + taps_ref[TAPS - 1 - offset : TAPS - offset] * view
    return current, views, total


def forward_kernel(
    micros,
    heads,
    starts_ref,
    x_ref,
    weight_ref,
    out_weight_ref,
    g_ref,
    table_ref,
    heads_ref,
    expand_ref,
    tri_ref,
    proj_ref,
    gg_ref,
    branch_ref,
    mixed_ref,
    states_ref,
    tails_ref,
    sums_ref,
    taps_ref,
    cols_ref,
    head_ref,
    g_out,
    ext,
    state,
    *sems,
):
    chunk, chunks = pl.program_id(0), pl.num_programs(0)
    rows = x_ref.shape[1]
    width = heads * HEAD_DIM
    conv_width = 2 * STATE + width
    size, groups = head_groups(heads)
    line = Line(g_ref, g_out, sems)
    early = min((g_out.shape[1] // g_ref.shape[1] - 1) // 2, line.events())

    @pl.when(chunk == 0)
    def _():
        greet(("seq",))
        line.start()

    @pl.when((lax.rem(chunk, 2) == 0) & (chunk >= 2) & (chunk // 2 - 1 < early))
    def _():
        line.hop(chunk // 2 - 1)

    @pl.when(chunk == 0)
    def _():
        ext[:, :8, :] = jnp.zeros((micros, 8, conv_width), F32)
        state[...] = jnp.zeros_like(state)
        me = lax.axis_index("seq")
        local = pltpu.roll(
            table_ref[:, :INNER], lax.rem(INNER - me * width, jnp.int32(INNER)), 1
        )[:, :width]
        taps_ref[:, : 2 * STATE] = table_ref[:, INNER:]
        taps_ref[:, 2 * STATE :] = local
        head_row = me * heads + (
            lax.broadcasted_iota(jnp.int32, (1, width), 1) // HEAD_DIM
        )
        limit = HEADS // 8 * jnp.left_shift(jnp.int32(1), lax.axis_index("width"))
        cols_ref[0:1] = local[6:7]
        cols_ref[1:2] = local[5:6]
        cols_ref[2:3] = (head_row < limit).astype(F32)
        cols_ref[3:8] = jnp.zeros((5, width), F32)
        head_ref[...] = pltpu.roll(
            heads_ref[...], lax.rem(LANES - me * heads, jnp.int32(LANES)), 1
        )

    skip, gain, mask = cols_ref[0:1], cols_ref[1:2], cols_ref[2:3]
    rows_in = x_ref[...].reshape(micros * rows, x_ref.shape[2])
    proj_ref[...] = mm(rows_in, weight_ref[...]).astype(BF16).reshape(proj_ref.shape)
    sums, gated_gains = [], []
    for micro in range(micros):
        tails_ref[micro] = ext[micro, :8, :]
        ext[micro, 8 : 8 + rows, :] = proj_ref[micro, :, :conv_width].astype(F32)
        raw_dt = proj_ref[micro, :, conv_width + width :].astype(F32)
        at = Chunk(
            starts_ref, micro, chunk, rows, raw_dt, head_ref, expand_ref[...], tri_ref[...]
        )
        conv = convolved(ext, micro, rows, taps_ref, at.same)[2]
        act = conv * sigmoid(conv)
        write = act[:, :STATE].astype(BF16)
        read = act[:, STATE : 2 * STATE].astype(BF16)
        x_heads = act[:, 2 * STATE :]
        scores = mm_nt(read, write)
        inputs = x_heads * at.step_cols
        state_in = state[micro]
        state_low = state_in.astype(BF16)
        states_ref[micro] = state_low
        outs = []
        for group in range(groups):
            matrices = [
                (at.decay(group * size + item) * scores).astype(BF16) for item in range(size)
            ]
            span = slice(group * size * HEAD_DIM, (group + 1) * size * HEAD_DIM)
            outs.append(mm(jnp.concatenate(matrices, axis=1), stacked(inputs[:, span], size)))
        mixed = jnp.concatenate(outs, axis=1) + at.carry_cols * mm(read, state_low)
        state[micro] = at.keep_all * state_in + mm_tn(
            write, (inputs * at.left_cols).astype(BF16)
        )
        mixed = mixed + skip * x_heads
        mixed_ref[micro] = mixed
        gate = proj_ref[micro, :, conv_width : conv_width + width].astype(F32)
        gated = mask * mixed * (gate * sigmoid(gate))
        gated_gain = (gated * gain).astype(BF16)
        gg_ref[micro] = gated_gain
        gated_gains.append(gated_gain)
        square = jnp.sum(gated * gated, axis=1, keepdims=True)
        lane = lax.broadcasted_iota(jnp.int32, (rows, LANES), 1)
        sums.append(jnp.where(lane == 0, square, 0.0).T[:2])
        ext[micro, :8, :] = ext[micro, rows : rows + 8, :]
    pad = sums_ref.shape[0] - 2 * micros
    if pad:
        sums.append(jnp.zeros((pad, rows), F32))
    sums_ref[...] = jnp.concatenate(sums, axis=0)
    branch_ref[...] = mm(jnp.concatenate(gated_gains, axis=0), out_weight_ref[...]).astype(BF16)

    @pl.when(chunk == chunks - 1)
    def _():
        line.hops(early)
        line.finish()


def cross_kernel(
    g_ref, out_weight_ref, gg_ref, sums_ref, dnorm_ref, total_ref, mine, slots, send, receive
):
    chunk, chunks = pl.program_id(0), pl.num_programs(0)
    micros, rows, model_width = g_ref.shape
    me = lax.axis_index("seq")

    @pl.when(chunk == 0)
    def _():
        greet(("seq",))

    grads = g_ref[...].reshape(micros * rows, model_width)
    dnorm = mm_nt(grads, out_weight_ref[...])
    gg = gg_ref[...].reshape(micros * rows, dnorm.shape[1])
    dnorm_ref[...] = dnorm.reshape(dnorm_ref.shape)
    cross = jnp.sum(dnorm * gg.astype(F32), axis=1, keepdims=True)
    lane = lax.broadcasted_iota(jnp.int32, (rows, LANES), 1)
    lines = []
    for micro in range(micros):
        part = cross[micro * rows : (micro + 1) * rows]
        lines.append(jnp.where(lane == 1, part, 0.0).T[:2])
    pad = sums_ref.shape[0] - 2 * micros
    if pad:
        lines.append(jnp.zeros((pad, rows), F32))
    mine[chunk] = sums_ref[...] + jnp.concatenate(lines, axis=0)

    @pl.when(chunk == chunks - 1)
    def _():
        def copy(turn, owner):
            peer = lax.rem(me + turn, chunks)
            return remote(
                mine, slots.at[owner], send.at[peer], receive.at[owner], {"seq": peer}
            )

        def start(turn, carry):
            copy(turn, me).start()
            return carry

        def finish(turn, carry):
            copy(turn, me).wait_send()
            copy(turn, lax.rem(me + turn, chunks)).wait_recv()
            return carry

        lax.fori_loop(1, chunks, start, 0)
        slots[me] = mine[...]
        lax.fori_loop(1, chunks, finish, 0)

        def add(owner, total):
            return total + slots[owner]

        total_ref[...] = lax.fori_loop(1, chunks, add, slots[0])


def backward_kernel(
    micros,
    heads,
    starts_ref,
    active_ref,
    proj_ref,
    dnorm_ref,
    mixed_ref,
    states_ref,
    tails_ref,
    sums_ref,
    weight_ref,
    taps_ref,
    head_ref,
    cols_ref,
    expand_ref,
    gather_ref,
    tri_ref,
    dproj_ref,
    partial_ref,
    gconv_ref,
    gcols_ref,
    ghead_ref,
    ext,
    heads_ext,
    dstate,
):
    chunks = pl.num_programs(0)
    step_index = pl.program_id(0)
    rows = proj_ref.shape[1]

    @pl.when(step_index == 0)
    def _():
        heads_ext[:, :, rows:, :] = jnp.zeros((micros, TAPS - 1, 8, ext.shape[2]), F32)
        dstate[...] = jnp.zeros_like(dstate)
        gconv_ref[...] = jnp.zeros_like(gconv_ref)
        gcols_ref[...] = jnp.zeros_like(gcols_ref)
        ghead_ref[...] = jnp.zeros_like(ghead_ref)

    for micro in range(micros):
        backward_rows(
            micro,
            heads,
            chunks - 1 - step_index,
            starts_ref,
            active_ref,
            proj_ref.at[micro],
            dnorm_ref.at[micro],
            mixed_ref.at[micro],
            states_ref.at[micro],
            tails_ref.at[micro],
            sums_ref,
            taps_ref,
            head_ref,
            cols_ref,
            expand_ref,
            gather_ref,
            tri_ref,
            dproj_ref.at[micro],
            gconv_ref,
            gcols_ref,
            ghead_ref,
            ext,
            heads_ext.at[micro],
            dstate.at[micro],
        )
    d_rows = dproj_ref[...].reshape(micros * rows, dproj_ref.shape[2])
    partial_ref[...] = mm_nt(d_rows, weight_ref[...]).astype(BF16)

    @pl.when(step_index == chunks - 1)
    def _():
        ghead_ref[2:3] = mm(halves(gcols_ref[...], 1), gather_ref[...])[0:1]


def backward_rows(
    micro,
    heads,
    chunk,
    starts_ref,
    active_ref,
    proj_ref,
    dnorm_ref,
    mixed_ref,
    states_ref,
    tails_ref,
    sums_ref,
    taps_ref,
    head_ref,
    cols_ref,
    expand_ref,
    gather_ref,
    tri_ref,
    dproj_ref,
    gconv_ref,
    gcols_ref,
    ghead_ref,
    ext,
    heads_ext,
    dstate,
):
    rows = proj_ref.shape[0]
    width = heads * HEAD_DIM
    conv_width = 2 * STATE + width
    size, groups = head_groups(heads)
    skip, gain, mask = cols_ref[0:1], cols_ref[1:2], cols_ref[2:3]
    tri = tri_ref[...]
    gather = gather_ref[...]
    inverse_active = 1.0 / active_ref[0]
    sums = jnp.concatenate(
        [sums_ref[...], jnp.zeros((LANES - sums_ref.shape[0], rows), F32)], axis=0
    ).T
    ext[micro, :8, :] = tails_ref[...]
    ext[micro, 8 : 8 + rows, :] = proj_ref[:, :conv_width].astype(F32)
    raw_dt = proj_ref[:, conv_width + width :].astype(F32)
    at = Chunk(starts_ref, micro, chunk, rows, raw_dt, head_ref, expand_ref[...], tri)
    current, views, conv = convolved(ext, micro, rows, taps_ref, at.same)
    conv_sig = sigmoid(conv)
    act = conv * conv_sig
    write = act[:, :STATE].astype(BF16)
    read = act[:, STATE : 2 * STATE].astype(BF16)
    x_heads = act[:, 2 * STATE :]
    scores = mm_nt(read, write)
    inputs = x_heads * at.step_cols

    gate = proj_ref[:, conv_width : conv_width + width].astype(F32)
    gate_sig = sigmoid(gate)
    gate_act = gate * gate_sig
    masked = mask * mixed_ref[...]
    gated = masked * gate_act
    root = lax.rsqrt(sums[:, 2 * micro : 2 * micro + 1] * inverse_active + EPSILON)
    pull = root * root * root * sums[:, 2 * micro + 1 : 2 * micro + 2] * inverse_active
    dnorm = dnorm_ref[...]
    scaled = gated * root
    d_gated = root * dnorm * gain - gated * pull
    d_gate = d_gated * masked * (gate_sig * (1.0 + gate * (1.0 - gate_sig)))
    d_mixed = mask * d_gated * gate_act
    gcols_ref[0:1] += jnp.sum(d_mixed * x_heads, axis=0, keepdims=True)
    gcols_ref[1:2] += jnp.sum(dnorm * scaled, axis=0, keepdims=True)

    state_low = states_ref[...]
    d_state = dstate[...]
    d_state_low = d_state.astype(BF16)
    from_state = (d_mixed * at.carry_cols).astype(BF16)
    left = inputs * at.left_cols
    left_low = left.astype(BF16)
    d_left = mm(write, d_state_low)
    state_out = mm(read, state_low)
    d_read = mm_nt(from_state, state_low)
    d_write = mm_nt(left_low, d_state_low)
    d_mixed_low = d_mixed.astype(BF16).astype(F32)
    inputs_low = inputs.astype(BF16).astype(F32)
    d_scores = jnp.zeros((rows, rows), F32)
    locals_out, d_locals = [], []
    for group in range(groups):
        span = slice(group * size * HEAD_DIM, (group + 1) * size * HEAD_DIM)
        decays = [at.decay(group * size + item) for item in range(size)]
        matrices = [(decay * scores).astype(BF16) for decay in decays]
        in_stack = stacked(inputs[:, span], size)
        out_stack = stacked(d_mixed[:, span], size)
        locals_out.append(mm(jnp.concatenate(matrices, axis=1), in_stack))
        d_locals.append(mm_tn(jnp.concatenate(matrices, axis=0), out_stack))
        d_matrices = mm_nt(out_stack, inputs[:, span].astype(BF16))
        for item in range(size):
            d_scores = (
                d_scores + d_matrices[item * rows : (item + 1) * rows] * decays[item]
            )
    local_out = jnp.concatenate(locals_out, axis=1)
    d_local = jnp.concatenate(d_locals, axis=1)
    d_scores_low = d_scores.astype(BF16)
    d_read = d_read + mm(d_scores_low, write)
    d_write = d_write + mm_tn(d_scores_low, read)
    d_inputs = d_local + at.left_cols * d_left
    d_x = skip * d_mixed + d_inputs * at.step_cols

    passed = left * d_left
    cum_terms = (
        d_mixed_low * local_out
        + d_mixed * at.carry_cols * state_out
        - inputs_low * d_local
        - passed
    )
    kept = jnp.sum(d_state * at.keep_all * state_low.astype(F32), axis=0, keepdims=True)
    final = jnp.sum(passed, axis=0, keepdims=True) + kept
    stack = jnp.concatenate(
        [cum_terms, d_inputs * x_heads, jnp.broadcast_to(final, (8, width))], axis=0
    )
    reduced = mm(halves(stack, 1), gather)
    d_cum = reduced[:rows]
    d_step = reduced[rows : 2 * rows]
    final_row = reduced[2 * rows : 2 * rows + 1]
    total = jnp.sum(d_cum, axis=0, keepdims=True) + final_row
    d_log = total - prefix_sum(tri, d_cum) + d_cum
    d_step = d_step + d_log * head_ref[1:2]
    d_dt = d_step * sigmoid(at.shifted_dt)
    ghead_ref[0:1] += jnp.sum(d_log * at.log_keep, axis=0, keepdims=True)
    ghead_ref[1:2] += jnp.sum(d_dt, axis=0, keepdims=True)
    dstate[...] = at.keep_all * d_state + mm_tn(read, from_state)

    d_conv = jnp.concatenate([d_write, d_read, d_x], axis=1) * (
        conv_sig * (1.0 + conv * (1.0 - conv_sig))
    )
    gconv_ref[TAPS : TAPS + 1] += jnp.sum(d_conv, axis=0, keepdims=True)
    gconv_ref[TAPS - 1 : TAPS] += jnp.sum(d_conv * current, axis=0, keepdims=True)
    d_raw = taps_ref[TAPS - 1 : TAPS] * d_conv
    for offset in range(1, TAPS):
        tap = TAPS - 1 - offset
        gconv_ref[tap : tap + 1] += jnp.sum(
            d_conv * views[offset - 1], axis=0, keepdims=True
        )
        heads_ext[offset - 1, :rows, :] = d_conv * at.same[offset - 1]
        d_raw = d_raw + taps_ref[tap : tap + 1] * (
            heads_ext[offset - 1, offset : offset + rows, :]
        )
        heads_ext[offset - 1, rows:, :] = heads_ext[offset - 1, :8, :]
    dproj_ref[:, :conv_width] = d_raw.astype(BF16)
    dproj_ref[:, conv_width : conv_width + width] = d_gate.astype(BF16)
    dproj_ref[:, conv_width + width :] = d_dt.astype(BF16)


def constant(shape):
    return pl.BlockSpec(shape, lambda index: (0,) * len(shape))


def run_forward(
    heads, starts, x, weight, out_weight, g, table, head_table, expand, tri, collective_id
):
    micros, rows, model_width = g.shape
    chunks = x.shape[1] // rows
    width = heads * HEAD_DIM
    conv_width = 2 * STATE + width
    block = micros * rows
    sum_rows = -(-2 * micros // 8) * 8
    columns = weight.shape[1]

    def whole(value):
        return pl.BlockSpec(
            value.shape, lambda index: (0,) * value.ndim, pipeline_mode=pl.Buffered(1)
        )

    def row_block(size):
        return pl.BlockSpec((micros, rows, size), lambda index: (0, index, 0))

    return pl.pallas_call(
        partial(forward_kernel, micros, heads),
        grid=(chunks,),
        in_specs=[
            pl.BlockSpec(memory_space=pltpu.SMEM),
            row_block(model_width),
            whole(weight),
            whole(out_weight),
            ANY,
            whole(table),
            whole(head_table),
            whole(expand),
            whole(tri),
        ],
        out_specs=[
            row_block(columns),
            row_block(width),
            pl.BlockSpec((block, model_width), lambda index: (index, 0)),
            row_block(width),
            pl.BlockSpec((None, micros, STATE, width), lambda index: (index, 0, 0, 0)),
            pl.BlockSpec((None, micros, 8, conv_width), lambda index: (index, 0, 0, 0)),
            pl.BlockSpec((None, sum_rows, rows), lambda index: (index, 0, 0)),
            constant((8, conv_width)),
            constant((8, width)),
            constant((8, LANES)),
            ANY,
        ],
        out_shape=[
            jax.ShapeDtypeStruct((micros, chunks * rows, columns), BF16),
            jax.ShapeDtypeStruct((micros, chunks * rows, width), BF16),
            jax.ShapeDtypeStruct((chunks * block, model_width), BF16),
            jax.ShapeDtypeStruct((micros, chunks * rows, width), F32),
            jax.ShapeDtypeStruct((chunks, micros, STATE, width), BF16),
            jax.ShapeDtypeStruct((chunks, micros, 8, conv_width), F32),
            jax.ShapeDtypeStruct((chunks, sum_rows, rows), F32),
            jax.ShapeDtypeStruct((8, conv_width), F32),
            jax.ShapeDtypeStruct((8, width), F32),
            jax.ShapeDtypeStruct((8, LANES), F32),
            jax.ShapeDtypeStruct((micros, chunks * rows, model_width), BF16),
        ],
        scratch_shapes=[
            pltpu.VMEM((micros, rows + 8, conv_width), F32),
            pltpu.VMEM((micros, STATE, width), F32),
        ]
        + line_sems(chunks // 2, micros),
        compiler_params=pltpu.CompilerParams(
            collective_id=collective_id, has_side_effects=True, vmem_limit_bytes=56 << 20
        ),
        cost_estimate=pl.CostEstimate(
            flops=60 * 10**9, bytes_accessed=150 * 10**6, transcendentals=0
        ),
        name="mixer_forward",
    )(starts, x, weight, out_weight, g, table, head_table, expand, tri)


def run_cross(g, out_weight, gg, sums, collective_id):
    chunks = sums.shape[0]
    micros, all_rows, model_width = g.shape
    rows, width = all_rows // chunks, gg.shape[2]

    def row_block(size):
        return pl.BlockSpec((micros, rows, size), lambda index: (0, index, 0))

    return pl.pallas_call(
        cross_kernel,
        grid=(chunks,),
        in_specs=[
            row_block(model_width),
            pl.BlockSpec(out_weight.shape, lambda index: (0, 0), pipeline_mode=pl.Buffered(1)),
            row_block(width),
            pl.BlockSpec((None,) + sums.shape[1:], lambda index: (index, 0, 0)),
        ],
        out_specs=[row_block(width), constant(sums.shape)],
        out_shape=[
            jax.ShapeDtypeStruct((micros, all_rows, width), F32),
            jax.ShapeDtypeStruct(sums.shape, F32),
        ],
        scratch_shapes=[
            pltpu.VMEM(sums.shape, F32),
            pltpu.VMEM((chunks,) + sums.shape, F32),
            pltpu.SemaphoreType.DMA((chunks,)),
            pltpu.SemaphoreType.DMA((chunks,)),
        ],
        compiler_params=pltpu.CompilerParams(
            collective_id=collective_id, has_side_effects=True, vmem_limit_bytes=60 << 20
        ),
        cost_estimate=pl.CostEstimate(
            flops=12 * 10**9, bytes_accessed=16 * 10**6, transcendentals=0
        ),
        name="cross_sums",
    )(g, out_weight, gg, sums)


def run_backward(
    heads, starts, active, proj, dnorm, mixed, states, tails, sums, weight, shared
):
    micros, all_rows, columns = proj.shape
    chunks = sums.shape[0]
    rows = all_rows // chunks
    width = heads * HEAD_DIM
    conv_width = 2 * STATE + width
    model_width = weight.shape[0]

    def row_block(size):
        return pl.BlockSpec((micros, rows, size), lambda index: (0, chunks - 1 - index, 0))

    def chunk_block(shape):
        return pl.BlockSpec((None, micros) + shape, lambda index: (chunks - 1 - index, 0, 0, 0))

    return pl.pallas_call(
        partial(backward_kernel, micros, heads),
        grid=(chunks,),
        in_specs=[
            pl.BlockSpec(memory_space=pltpu.SMEM),
            pl.BlockSpec(memory_space=pltpu.SMEM),
            row_block(columns),
            row_block(width),
            row_block(width),
            chunk_block((STATE, width)),
            chunk_block((8, conv_width)),
            pl.BlockSpec((None, sums.shape[1], rows), lambda index: (chunks - 1 - index, 0, 0)),
            pl.BlockSpec(weight.shape, lambda index: (0, 0), pipeline_mode=pl.Buffered(1)),
        ]
        + [constant(item.shape) for item in shared],
        out_specs=[
            row_block(columns),
            pl.BlockSpec((micros * rows, model_width), lambda index: (chunks - 1 - index, 0)),
            constant((8, conv_width)),
            constant((8, width)),
            constant((8, LANES)),
        ],
        out_shape=[
            jax.ShapeDtypeStruct((micros, all_rows, columns), BF16),
            jax.ShapeDtypeStruct((micros * all_rows, model_width), BF16),
            jax.ShapeDtypeStruct((8, conv_width), F32),
            jax.ShapeDtypeStruct((8, width), F32),
            jax.ShapeDtypeStruct((8, LANES), F32),
        ],
        scratch_shapes=[
            pltpu.VMEM((micros, rows + 8, conv_width), F32),
            pltpu.VMEM((micros, TAPS - 1, rows + 8, conv_width), F32),
            pltpu.VMEM((micros, STATE, width), F32),
        ],
        compiler_params=pltpu.CompilerParams(vmem_limit_bytes=56 << 20),
        cost_estimate=pl.CostEstimate(
            flops=60 * 10**9, bytes_accessed=60 * 10**6, transcendentals=0
        ),
        name="mixer_backward",
    )(starts, active, proj, dnorm, mixed, states, tails, sums, weight, *shared)


def tables(heads, rows):
    width = heads * HEAD_DIM
    expand = (
        jnp.arange(LANES)[:, None] == jnp.arange(width)[None, :] // HEAD_DIM
    ).astype(BF16)
    tri = (jnp.arange(rows)[:, None] >= jnp.arange(rows)[None, :]).astype(BF16)
    return (
        jnp.concatenate([expand, expand], axis=0),
        jnp.concatenate([expand.T, expand.T], axis=0),
        tri,
    )


def gather_kernel(
    x_ref,
    w_ref,
    x_out,
    w_out,
    w_send,
    w_receive,
    f_send,
    f_receive,
    keep,
    *sems,
):
    seq_total, width_total = lax.axis_size("seq"), lax.axis_size("width")
    me, mine = lax.axis_index("seq"), lax.axis_index("width")
    quarter = w_ref.shape[1]
    depth = quarter * width_total
    line = Line(x_ref, x_out, sems)
    greet(("seq", "width"))

    def rows(source, group):
        return pl.ds(pl.multiple_of(source * depth + group * quarter, 8), quarter)

    def deal(turn, from_peer):
        peer = lax.rem(me + turn, seq_total)
        owner = peer if from_peer else me
        return remote(
            w_ref.at[peer],
            w_out.at[rows(owner, mine)],
            w_send.at[peer],
            w_receive.at[owner],
            {"seq": peer},
        )

    def deal_start(turn, carry):
        deal(turn, False).start()
        return carry

    lax.fori_loop(1, seq_total, deal_start, 0)
    w_own = pltpu.make_async_copy(w_ref.at[me], w_out.at[rows(me, mine)], keep.at[0])
    w_own.start()
    line.start()

    def forward(source, turn, from_peer):
        peer = lax.rem(mine + turn, width_total)
        group = peer if from_peer else mine
        where = w_out.at[rows(source, group)]
        return remote(
            where, where, f_send.at[peer, source], f_receive.at[group, source], {"width": peer}
        )

    def forward_start(source):
        for turn in range(1, width_total):
            forward(source, turn, False).start()

    def deal_pass(turn, carry):
        deal(turn, True).wait_recv()
        forward_start(lax.rem(me + turn, seq_total))
        return carry

    w_own.wait()
    forward_start(me)
    lax.fori_loop(1, seq_total, deal_pass, 0)
    line.hops(0)

    def deal_end(turn, carry):
        deal(turn, False).wait_send()
        return carry

    lax.fori_loop(1, seq_total, deal_end, 0)

    def forward_end(source, carry):
        for turn in range(1, width_total):
            forward(source, turn, False).wait_send()
            forward(source, turn, True).wait_recv()
        return carry

    lax.fori_loop(0, seq_total, forward_end, 0)
    line.finish()


def gather_rows(x, pieces, collective_id):
    seq_total, width_total = lax.axis_size("seq"), lax.axis_size("width")
    parts, rows, model_width = x.shape
    whole = (parts, rows * seq_total, model_width)
    weight = (seq_total * width_total * pieces.shape[1], pieces.shape[2])
    dma = pltpu.SemaphoreType.DMA
    return pl.pallas_call(
        gather_kernel,
        in_specs=[ANY] * 2,
        out_specs=[ANY] * 2,
        out_shape=[
            jax.ShapeDtypeStruct(whole, x.dtype),
            jax.ShapeDtypeStruct(weight, pieces.dtype),
        ],
        scratch_shapes=[
            dma((seq_total,)),
            dma((seq_total,)),
            dma((width_total, seq_total)),
            dma((width_total, seq_total)),
            dma((1,)),
        ]
        + line_sems(seq_total // 2, parts),
        compiler_params=pltpu.CompilerParams(
            collective_id=collective_id, has_side_effects=True
        ),
        cost_estimate=pl.CostEstimate(
            flops=80 * 10**9, bytes_accessed=200 * 10**6, transcendentals=0
        ),
        name="gather_rows",
    )(x, pieces)


TILE = 256
MIDDLE = 2
LAST = 4


def home_kernel(
    layout,
    normed_ref,
    columns_ref,
    gconv_ref,
    gcols_ref,
    ghead_ref,
    in_gain_ref,
    grad_ref,
    gnorm_ref,
    dproj_ref,
    shard_in_ref,
    shard_out_ref,
    taps_out,
    bias_out,
    gain_out,
    head_out,
    in_gain_out,
    zx_ref,
    bc_ref,
    go_ref,
    small_out,
    line_buffer,
    blocks_in,
    acc,
    out_acc,
    stage,
    arrived,
    last_arrived,
    sum_x,
    sum_z,
    sum_b,
    out_stage,
    out_arrived,
    out_last,
    sum_out,
    small_stage,
    small_slots,
    fetch,
    in_sems,
    zx_send,
    zx_receive,
    bc_send,
    bc_receive,
    out_sems,
    go_send,
    go_receive,
    small_send,
    small_receive,
    last_send,
    last_receive,
):
    seq_total, width_total, quarter, width, slots, shard, heads = layout
    micros = normed_ref.shape[0]
    me, mine = lax.axis_index("seq"), lax.axis_index("width")
    depth = quarter * width_total
    conv_width = 2 * STATE + width
    per_tile = TILE // depth
    tiles = seq_total // per_tile
    chunk_rows = blocks_in.shape[1]
    pieces = normed_ref.shape[1] // chunk_rows
    chunks = micros * pieces
    owners = seq_total // width_total
    barrier = pltpu.get_barrier_semaphore()
    count = seq_total * width_total
    place = mine * seq_total + me

    def turned(turn):
        return lax.rem(turn + me // per_tile, tiles)

    def fetch_copy(source, turn, chunk):
        tile = turned(turn)
        first = chunk % pieces * chunk_rows
        return pltpu.make_async_copy(
            source.at[
                chunk // pieces,
                pl.ds(first, chunk_rows),
                pl.ds(pl.multiple_of(tile * TILE, TILE), TILE),
            ],
            blocks_in.at[chunk % 2],
            fetch.at[chunk % 2],
        )

    def fetched(source, following, turn, chunk):
        fetch_copy(source, turn, chunk).wait()
        if chunk + 1 < chunks:
            fetch_copy(source, turn, chunk + 1).start()
        else:

            @pl.when(turn + 1 < tiles)
            def _():
                fetch_copy(source, turn + 1, 0).start()

            if following is not None:

                @pl.when(turn + 1 == tiles)
                def _():
                    fetch_copy(following, 0, 0).start()

        return blocks_in[chunk % 2]

    fetch_copy(grad_ref, 0, 0).start()

    def hello(turn, carry):
        peer = lax.rem(place + turn, count)
        pl.semaphore_signal(
            barrier,
            inc=1,
            device_id={"width": peer // seq_total, "seq": lax.rem(peer, seq_total)},
            device_id_type=MESH,
        )
        return carry

    lax.fori_loop(1, count, hello, 0)
    pl.semaphore_wait(barrier, count - 1)

    def both(is_here, source, target, send, receive, device, action):
        if action != "send":

            @pl.when(is_here)
            def _():
                stay = pltpu.make_async_copy(source, target, receive)
                if action == "start":
                    stay.start()
                else:
                    stay.wait()

        @pl.when(jnp.logical_not(is_here))
        def _():
            away = remote(source, target, send, receive, device)
            if action == "start":
                away.start()
            elif action == "receive":
                away.wait_recv()
            else:
                away.wait_send()

    sub, cols = out_stage.shape[2:]
    per_out = TILE // cols

    upper, lower = mine // 2, lax.rem(mine, 2)

    def order(block):
        odd = lax.rem(block, 2)
        even = 1 - odd
        first = odd * upper + even * lower
        second = odd * lower + even * upper
        across = 2 * (1 - upper) + lower
        beside = 2 * upper + 1 - lower
        return first, second, odd * across + even * beside, odd * beside + even * across

    def slot_of(block, group):
        odd = lax.rem(block, 2)
        return odd * group + (1 - odd) * (group % 2 * 2 + group // 2)

    class Meeting:
        def __init__(self, parts, come, last, sems):
            self.parts, self.come, self.last, self.sems = parts, come, last, sems

        def first(self, block):
            side, _, partner, _ = order(block)
            return remote(
                self.parts.at[block, pl.ds(2 * (1 - side), 2)],
                self.come.at[block],
                self.sems.at[0, block],
                self.sems.at[1, block],
                {"width": partner},
            )

        def second(self, block):
            side, place, _, partner = order(block)
            return remote(
                self.parts.at[block, 2 * side + 1 - place],
                self.last.at[block],
                self.sems.at[2, block],
                self.sems.at[3, block],
                {"width": partner},
            )

        def middle(self, block):
            self.first(block).wait_recv()
            side = order(block)[0]
            for item in range(2):
                slot = 2 * side + item
                total = self.parts[block, slot].astype(F32) + self.come[block, item].astype(F32)
                self.parts[block, slot] = total.astype(BF16)
            self.second(block).start()

        def total(self, block):
            self.second(block).wait_recv()
            side, place = order(block)[:2]
            return self.parts[block, 2 * side + place].astype(F32) + self.last[block].astype(F32)

        def sent(self, block):
            self.first(block).wait_send()
            self.second(block).wait_send()

    out_meeting = Meeting(out_stage, out_arrived, out_last, out_sems)
    in_meeting = Meeting(stage, arrived, last_arrived, in_sems)

    def each(turn, per, act):
        for item in range(per):
            act(turned(turn) * per + item)

    go_owner = me // owners

    def go_copy(target, action):
        both(
            (go_owner == mine) & (target == me),
            sum_out.at[target],
            go_ref.at[lax.rem(me, owners), mine],
            go_send.at[target],
            go_receive.at[lax.rem(me, owners), mine],
            {"width": go_owner, "seq": target},
            action,
        )

    def out_combine(block):
        sum_out[block] = out_meeting.total(block).astype(BF16)
        go_copy(block, "start")

    def out_multiply(turn, carry):
        tile = turned(turn)
        for chunk in range(chunks):
            block = fetched(grad_ref, normed_ref, turn, chunk)
            first = chunk % pieces * chunk_rows
            part = mm_tn(gnorm_ref[chunk // pieces, first : first + chunk_rows, :], block)
            out_acc[...] = part if chunk == 0 else out_acc[...] + part
        for item in range(per_out):
            block = tile * per_out + item
            for group in range(width_total):
                out_stage[block, slot_of(block, group)] = out_acc[
                    group * sub : (group + 1) * sub, item * cols : (item + 1) * cols
                ].astype(BF16)
            out_meeting.first(block).start()

        @pl.when(turn >= MIDDLE)
        def _():
            each(turn - MIDDLE, per_out, out_meeting.middle)

        @pl.when(turn >= LAST)
        def _():
            each(turn - LAST, per_out, out_combine)

        return carry

    lax.fori_loop(0, tiles, out_multiply, 0)
    conv_end = conv_width + width
    small_stage[:, :conv_width] = gconv_ref[...]
    small_stage[:, conv_width:conv_end] = gcols_ref[...]
    small_stage[:, conv_end : conv_end + LANES] = ghead_ref[...]

    def block_copy(sums, sem_row, number, block, second, action):
        low = (number * width) // shard
        high = ((number + 1) * width - 1) // shard
        owner = high if second else low
        slot = number - (owner * shard) // width

        def act():
            both(
                (owner == mine) & (block == me),
                sums.at[block],
                zx_ref.at[slot, mine],
                zx_send.at[sem_row, block],
                zx_receive.at[slot, mine],
                {"width": owner, "seq": block},
                action,
            )

        if second:
            pl.when(high != low)(act)
        else:
            act()

    def bc_copy(block, action):
        both(
            (mine == width_total - 1) & (block == me),
            sum_b.at[block],
            bc_ref.at[me, mine],
            bc_send.at[block],
            bc_receive.at[me, mine],
            {"width": width_total - 1, "seq": block},
            action,
        )

    def pieces_of(block, action):
        for second in (False, True):
            block_copy(sum_z, int(second), me, block, second, action)
            block_copy(sum_x, 2 + int(second), seq_total + me, block, second, action)
        bc_copy(block, action)

    def combine(block):
        low = in_meeting.total(block).astype(BF16)
        sum_b[block, :, : 2 * STATE] = low[:, : 2 * STATE]
        sum_x[block] = low[:, 2 * STATE : conv_width]
        sum_z[block] = low[:, conv_width : conv_width + width]
        sum_b[block, :, 2 * STATE :] = low[:, conv_width + width :]
        pieces_of(block, "start")

    def multiply(turn, carry):
        tile = turned(turn)
        for chunk in range(chunks):
            block = fetched(normed_ref, None, turn, chunk)
            first = chunk % pieces * chunk_rows
            part = mm_tn(
                block, dproj_ref[chunk // pieces, first : first + chunk_rows, :]
            )
            acc[...] = part if chunk == 0 else acc[...] + part
        for item in range(per_tile):
            block = tile * per_tile + item
            for group in range(width_total):
                row = item * depth + group * quarter
                stage[block, slot_of(block, group)] = acc[row : row + quarter].astype(BF16)
            in_meeting.first(block).start()
        weights = columns_ref[pl.ds(pl.multiple_of(tile * TILE, TILE), TILE), :]
        product = (acc[...] * weights.astype(F32)).astype(BF16)
        line = mm_nt(jnp.ones((8, product.shape[1]), BF16), product)
        small_stage[pl.ds(tile, 1), conv_end + LANES :] = line[:1]

        @pl.when(turn < MIDDLE)
        def _():
            each(tiles - MIDDLE + turn, per_out, out_meeting.middle)

        @pl.when(turn >= MIDDLE)
        def _():
            each(turn - MIDDLE, per_tile, in_meeting.middle)

        @pl.when(turn < LAST)
        def _():
            each(tiles - LAST + turn, per_out, out_combine)

        @pl.when(turn >= LAST)
        def _():
            each(turn - LAST, per_tile, combine)

        return carry

    lax.fori_loop(0, tiles, multiply, 0)

    def small_hop(turn, from_peer):
        peer = lax.rem(mine + turn, width_total)
        group = peer if from_peer else mine
        return remote(
            small_stage,
            small_slots.at[group],
            small_send.at[peer],
            small_receive.at[group],
            {"width": peer},
        )

    for turn in range(1, width_total):
        small_hop(turn, False).start()
    small_slots[mine] = small_stage[...]

    for tile in range(tiles - LAST, tiles):
        if tile >= tiles - MIDDLE:
            each(tile, per_tile, in_meeting.middle)
    for tile in range(tiles - LAST, tiles):
        each(tile, per_tile, combine)

    for turn in range(1, width_total):
        small_hop(turn, True).wait_recv()
        small_hop(turn, False).wait_send()
    total = small_slots[0]
    for group in range(1, width_total):
        total = total + small_slots[group]
    small_stage[...] = total

    def last_hop(turn, from_peer):
        peer = lax.rem(me + turn, seq_total)
        owner = peer if from_peer else me
        return remote(
            small_stage,
            small_out.at[owner],
            last_send.at[peer],
            last_receive.at[owner],
            {"seq": peer},
        )

    def last_start(turn, carry):
        last_hop(turn, False).start()
        return carry

    lax.fori_loop(1, seq_total, last_start, 0)
    small_out[me] = small_stage[...]

    def sent(block, carry):
        in_meeting.sent(block)
        out_meeting.sent(block)
        pieces_of(block, "send")
        go_copy(block, "send")
        return carry

    lax.fori_loop(0, seq_total, sent, 0)

    first = (mine * shard) // width

    def landed(slot, carry):
        number = first + slot
        source = lax.rem(number, seq_total)

        @pl.when((number < 2 * seq_total) & (number * width < (mine + 1) * shard))
        def _():
            for group in range(width_total):
                both(
                    (source == me) & (mine == group),
                    sum_z.at[me],
                    zx_ref.at[slot, group],
                    zx_send.at[0, me],
                    zx_receive.at[slot, group],
                    {"width": group, "seq": source},
                    "receive",
                )

        return carry

    lax.fori_loop(0, slots, landed, 0)

    @pl.when(mine == width_total - 1)
    def _():
        def bc_landed(source, carry):
            for group in range(width_total):
                both(
                    (source == me) & (mine == group),
                    sum_b.at[me],
                    bc_ref.at[source, group],
                    bc_send.at[me],
                    bc_receive.at[source, group],
                    {"width": group, "seq": source},
                    "receive",
                )
            return carry

        lax.fori_loop(0, seq_total, bc_landed, 0)

    for item in range(owners):
        for group in range(width_total):
            source = mine * owners + item
            both(
                (source == me) & (mine == group),
                sum_out.at[me],
                go_ref.at[item, group],
                go_send.at[me],
                go_receive.at[item, group],
                {"width": group, "seq": source},
                "receive",
            )

    def last_end(turn, carry):
        last_hop(turn, False).wait_send()
        last_hop(turn, True).wait_recv()
        return carry

    lax.fori_loop(1, seq_total, last_end, 0)

    edge = (slots - -(-(2 * STATE + HEADS) // width)) * width
    for group in range(width_total):
        for slot in range(slots):
            line_buffer[:, slot * width : (slot + 1) * width] = zx_ref[slot, group].astype(F32)

        @pl.when(mine == width_total - 1)
        def _():
            def bc_add(source, total):
                return total + bc_ref[source, group, :, : 2 * STATE].astype(F32)

            first_sum = bc_ref[0, group, :, : 2 * STATE].astype(F32)
            line_buffer[:, edge : edge + 2 * STATE] = lax.fori_loop(
                1, seq_total, bc_add, first_sum
            )
            for source in range(seq_total):
                at = edge + 2 * STATE + source * heads
                line_buffer[:, at : at + heads] = bc_ref[
                    source, group, :, 2 * STATE : 2 * STATE + heads
                ].astype(F32)

        total_lanes = line_buffer.shape[1]
        start = lax.rem(mine * shard, jnp.int32(width))
        rolled = pltpu.roll(
            line_buffer[...], lax.rem(total_lanes - start, jnp.int32(total_lanes)), 1
        )
        shard_in_ref[group * quarter : (group + 1) * quarter, :] = rolled[:, :shard]
    for item in range(owners):
        for group in range(width_total):
            row = item * width + group * sub
            shard_out_ref[row : row + sub, :] = go_ref[item, group].astype(F32)

    def small_add(source, total):
        return total + small_out[source]

    total = lax.fori_loop(1, seq_total, small_add, small_out[0])
    taps_out[:, INNER:] = total[:TAPS, : 2 * STATE]
    bias_out[:, INNER:] = total[TAPS : TAPS + 1, : 2 * STATE]
    in_gain_out[...] = total[:, conv_end + LANES :] / in_gain_ref[...]
    for source in range(seq_total):
        first = source * width
        taps_out[:, first : first + width] = small_out[source, :TAPS, 2 * STATE : conv_width]
        bias_out[:, first : first + width] = small_out[
            source, TAPS : TAPS + 1, 2 * STATE : conv_width
        ]
        gain_out[:, first : first + width] = small_out[source, 1:2, conv_width:conv_end]
        head_out[:, source * heads : (source + 1) * heads] = small_out[
            source, :, conv_end : conv_end + heads
        ]


def bring_home(normed, dproj, columns, smalls, in_gain, grad, gnorm, heads, collective_id):
    seq_total, width_total = lax.axis_size("seq"), lax.axis_size("width")
    width = heads * HEAD_DIM
    micros, group_rows, model_width = normed.shape
    depth = model_width // seq_total
    quarter = depth // width_total
    shard = (INNER + CONV + HEADS) // width_total
    slots = max(
        ((group + 1) * shard - 1) // width - group * shard // width + 1
        for group in range(width_total)
    )
    all_columns = dproj.shape[2]
    layout = (seq_total, width_total, quarter, width, slots, shard, heads)
    rest = all_columns - 2 * width
    sub, cols = width // width_total, model_width // seq_total
    owners = seq_total // width_total
    small = (8, 2 * STATE + 2 * width + LANES + TILE)
    lanes = -(-slots * width // LANES) * LANES
    dma = pltpu.SemaphoreType.DMA
    vmem = pl.BlockSpec(memory_space=pltpu.VMEM)
    return pl.pallas_call(
        partial(home_kernel, layout),
        in_specs=[ANY, vmem, vmem, vmem, vmem, vmem, ANY, vmem, vmem],
        out_specs=[vmem] * 7,
        out_shape=[
            jax.ShapeDtypeStruct((depth, shard), F32),
            jax.ShapeDtypeStruct((owners * width, cols), F32),
            jax.ShapeDtypeStruct((TAPS, CONV), F32),
            jax.ShapeDtypeStruct((1, CONV), F32),
            jax.ShapeDtypeStruct((1, INNER), F32),
            jax.ShapeDtypeStruct((8, HEADS), F32),
            jax.ShapeDtypeStruct(in_gain.shape, F32),
        ],
        scratch_shapes=[
            pltpu.VMEM((slots, width_total, quarter, width), BF16),
            pltpu.VMEM((seq_total, width_total, quarter, rest), BF16),
            pltpu.VMEM((owners, width_total, sub, cols), BF16),
            pltpu.VMEM((seq_total,) + small, F32),
            pltpu.VMEM((quarter, lanes), F32),
            pltpu.VMEM((2, min(group_rows, 1024), TILE), BF16),
            pltpu.VMEM((TILE, all_columns), F32),
            pltpu.VMEM((width, TILE), F32),
            pltpu.VMEM((seq_total, width_total, quarter, all_columns), BF16),
            pltpu.VMEM((seq_total, 2, quarter, all_columns), BF16),
            pltpu.VMEM((seq_total, quarter, all_columns), BF16),
            pltpu.VMEM((seq_total, quarter, width), BF16),
            pltpu.VMEM((seq_total, quarter, width), BF16),
            pltpu.VMEM((seq_total, quarter, rest), BF16),
            pltpu.VMEM((seq_total, width_total, sub, cols), BF16),
            pltpu.VMEM((seq_total, 2, sub, cols), BF16),
            pltpu.VMEM((seq_total, sub, cols), BF16),
            pltpu.VMEM((seq_total, sub, cols), BF16),
            pltpu.VMEM(small, F32),
            pltpu.VMEM((width_total,) + small, F32),
            dma((2,)),
            dma((4, seq_total)),
            dma((4, seq_total)),
            dma((slots, width_total)),
            dma((seq_total,)),
            dma((seq_total, width_total)),
            dma((4, seq_total)),
            dma((seq_total,)),
            dma((owners, width_total)),
            dma((width_total,)),
            dma((width_total,)),
            dma((seq_total,)),
            dma((seq_total,)),
        ],
        compiler_params=pltpu.CompilerParams(
            collective_id=collective_id, has_side_effects=True, vmem_limit_bytes=60 << 20
        ),
        cost_estimate=pl.CostEstimate(
            flops=150 * 10**9, bytes_accessed=8 * normed.size, transcendentals=0
        ),
        name="bring_home",
    )(normed, columns, *smalls, in_gain, grad, gnorm, dproj)


def own(value, start, count, axis=0):
    return lax.dynamic_slice_in_dim(value, start, count, axis)


def per_device(
    hidden_in,
    starts,
    in_gain,
    in_weight,
    conv_weight,
    conv_bias,
    step_bias,
    decay_log,
    skip_gain,
    gate_gain,
    out_weight,
    cotangent,
):
    seq_total = lax.axis_size("seq")
    seq_index = lax.axis_index("seq")
    group_index = lax.axis_index("width")
    micros, rows, model_width = hidden_in.shape[1:]
    heads = HEADS // seq_total
    width = heads * HEAD_DIM
    depth = in_weight.shape[0]
    head_count = HEADS // 8 * jnp.left_shift(jnp.int32(1), group_index)
    active = head_count.astype(F32) * HEAD_DIM

    hidden = hidden_in[0].astype(F32)
    grads = cotangent[0]
    root_in = lax.rsqrt(jnp.mean(hidden * hidden, axis=2, keepdims=True) + EPSILON)
    normed = (hidden * root_in * in_gain).astype(BF16)

    dt_pad = LANES
    width_total = lax.axis_size("width")
    quarter = depth // width_total
    in_quarter = own(in_weight, group_index * quarter, quarter)
    gates = in_quarter[:, :INNER].reshape(quarter, seq_total, width)
    xs = in_quarter[:, INNER : 2 * INNER].reshape(quarter, seq_total, width)
    bc = jnp.broadcast_to(
        in_quarter[:, None, 2 * INNER : INNER + CONV], (quarter, seq_total, 2 * STATE)
    )
    dts = in_quarter[:, INNER + CONV :].reshape(quarter, seq_total, heads)
    dts = jnp.pad(dts, ((0, 0), (0, 0), (0, dt_pad - heads)))
    pieces = jnp.concatenate([bc, xs, gates, dts], axis=2).transpose(1, 0, 2)
    all_normed, columns = gather_rows(normed, pieces, 0)

    def lane_pad(value):
        return jnp.pad(value, (0, CONV - INNER))[None]

    table = jnp.concatenate(
        [
            conv_weight,
            conv_bias[None],
            lane_pad(gate_gain),
            lane_pad(jnp.repeat(skip_gain, HEAD_DIM)),
            jnp.zeros((1, CONV), F32),
        ],
        axis=0,
    )
    head_table = jnp.pad(
        jnp.stack([step_bias, -jnp.exp(decay_log)]), ((0, 6), (0, LANES - HEADS))
    )
    expand, gather, tri = tables(heads, rows)

    proj, gg, branch, mixed, states, tails, sums, taps, cols, head, all_grad = run_forward(
        heads,
        starts[0],
        all_normed,
        columns,
        out_weight,
        grads,
        table,
        head_table,
        expand,
        tri,
        3,
    )
    branch = lax.psum_scatter(branch, "seq", scatter_dimension=0, tiled=True)
    dnorm, sums = run_cross(all_grad, out_weight, gg, sums, 1)
    roots = lax.rsqrt(sums[:, : 2 * micros : 2] / active + EPSILON)
    own_roots = own(roots, seq_index, 1).reshape(micros, rows, 1)
    all_roots = roots.transpose(1, 0, 2).reshape(micros, seq_total * rows, 1)
    gnorm = (gg.astype(F32) * all_roots).astype(BF16)

    dproj, partial_rows, *smalls = run_backward(
        heads,
        starts[0],
        active[None],
        proj,
        dnorm,
        mixed,
        states,
        tails,
        sums,
        columns,
        [taps, head, cols, expand, gather, tri],
    )
    scattered = lax.psum_scatter(partial_rows, "seq", scatter_dimension=0, tiled=True)
    head_sums, branch = lax.optimization_barrier((smalls[2], branch))
    home = bring_home(
        all_normed,
        dproj,
        columns,
        [smalls[0], smalls[1], head_sums],
        in_gain.reshape(-1, TILE),
        all_grad,
        gnorm,
        heads,
        2,
    )
    shard_in, shard_out, taps_sum, bias_sum, gain_sum, head_sums, in_gain_sum = home
    output = hidden + branch.reshape(hidden.shape).astype(F32) * own_roots
    scattered, in_gain_sum = lax.optimization_barrier((scattered, in_gain_sum))
    gained = scattered.reshape(hidden.shape).astype(F32) * in_gain
    pull = jnp.mean(gained * hidden, axis=2, keepdims=True) * (root_in * root_in * root_in)
    hidden_grads = grads.astype(F32) + root_in * gained - hidden * pull
    shape = hidden_in.shape
    return (
        output.astype(BF16).reshape(shape),
        hidden_grads.astype(BF16).reshape(shape),
        in_gain_sum.reshape(-1),
        shard_in,
        taps_sum,
        bias_sum[0],
        head_sums[1],
        head_sums[0],
        head_sums[2],
        gain_sum[0],
        shard_out,
    )


def solution(mesh):
    in_specs = (
        P("width", None, "seq", None),
        P("width", None, None),
        P(),
        P("seq", None),
        P(),
        P(),
        P(),
        P(),
        P(),
        P(),
        P("seq", None),
        P("width", None, "seq", None),
    )
    out_specs = (
        P("width", None, "seq", None),
        P("width", None, "seq", None),
        P(),
        P("seq", "width"),
        P(),
        P(),
        P(),
        P(),
        P(),
        P(),
        P("width", "seq"),
    )
    return jax.shard_map(
        per_device, mesh=mesh, in_specs=in_specs, out_specs=out_specs, check_vma=False
    )
```

time: 491 us -> 468 us (0.953)
  the two profiles are of different devices: /device:TPU:31 before, /device:TPU:0 now
where the time goes in v4:
time: 468 us; the launch traced here: 466 us
  Pallas kernels  409 us (87%)
  local copies, waits for them, and re-layouts  19.8 us (4%)
  other arithmetic  15.3 us (3%)
  between operations  14.4 us (3%)
  waiting for transfers between devices  7.8 us (2%)
    pallas_call x1, Pallas kernels, bring_home(): pl.pallas_call(partial(home_kernel, layout), in_specs=[ANY, vmem, vmem, v...  150 us
    pallas_call x1, Pallas kernels, gather_rows(): pl.pallas_call(gather_kernel, in_specs=[ANY] * 2, out_specs=[ANY] * 2, ou...  100 us
    pallas_call x1, Pallas kernels, run_forward(): pl.pallas_call(partial(forward_kernel, micros, heads), grid=(chunks,), in...  78.8 us
    pallas_call x1, Pallas kernels, run_backward(): pl.pallas_call(partial(backward_kernel, micros, heads), grid=(chunks,), i...  56.4 us
    pallas_call x1, Pallas kernels, run_cross(): pl.pallas_call(cross_kernel, grid=(chunks,), in_specs=[row_block(model_wi...  23.4 us
  transfers between devices with their start and end apart: 2, of which 1 were waited for; matrix products, arithmetic and copies ran while one was open for 1% of the time, Pallas kernels for 49%

profile of v4, /device:TPU:0, one launch (start us, length us, event | category | flops | bytes accessed | tf_op | source)
XLA Modules:
  0.0 466.1 jit_solution(3412208385651265635)
XLA Ops:
  7.2 0.0 reduce-scatter.3.cloned.1.call-start
  7.2 0.6 fusion.11.tri_ref
  7.9 0.7 negate_bitcast_fusion
  8.5 1.5 fusion.6
  10.1 0.7 broadcast_in_dim.16
  10.8 0.7 pad.16
  11.6 0.7 broadcast_in_dim.36
  12.3 0.1 reshape.154
  12.4 0.8 dynamic-slice_bitcast_fusion
  13.2 0.9 dynamic-slice
  14.1 0.1 copy.25
  14.3 0.1 copy.28
  14.4 0.7 add_convert_fusion.expand_ref
  15.1 2.3 fusion.16
  17.4 0.0 copy-start.21
  17.4 1.1 copy.29
  18.6 0.3 copy.30
  18.9 0.6 select_maximum_fusion.heads_ref
  19.5 1.3 fusion.8.x_ref
  20.8 1.2 fusion.10.w_ref
  22.1 100.5 %gather_rows.1 = (bf16[2,1024,2048]{2,1,0:T(8,128)(2,1)}, bf16[2048,1408]{1,0:T(8,128)(2,1)}) custom-call(bf16[2,128,2048]{2,1,0:T(8,128)(2,1)} %fusion.8.x_ref, bf16[8,64,1408]{2,1,0:T(8,128)(2,1)} %fusion.10.w_ref), custom_call_target="tpu_custom_call" | custom-call | flops 80000000000 | bytes 200000000 | tf_op jit(solution)/shard_map/gather_rows/pallas_call | solution.py:941
  122.6 0.8 concatenate.17.table_ref
  123.4 78.8 %mixer_forward.1 = (bf16[2,1024,1408]{2,1,0:T(8,128)(2,1)}, bf16[2,1024,512]{2,1,0:T(8,128)(2,1)}, bf16[2048,2048]{1,0:T(8,128)(2,1)}, f32[2,1024,512]{2,1,0:T(8...) custom-call(s32[2,4]{1,0:T(2,128)} %bitcast.55, ...), custom_call_target="tpu_custom_call" | custom-call | flops 60000002048 | bytes 150000000 | tf_op jit(solution)/shard_map/mixer_forward/pallas_call | solution.py:691
  202.2 0.0 reduce-scatter.3.cloned.1.call-update
  202.2 0.2 reduce-scatter.5.cloned.1.call-start
  202.4 0.4 copy-done.13
  202.9 0.1 iota_compare_fusion.1
  203.0 0.7 add_convert_fusion.1.gather_ref
  203.7 23.4 %cross_sums.1 = (f32[2,1024,512]{2,1,0:T(8,128)}, f32[8,8,128]{2,1,0:T(8,128)}) custom-call(bf16[2,1024,2048]{2,1,0:T(8,128)(2,1)} %get-tuple-element.45.g_ref.grad_ref, bf16[512,2048]{1,0:T(8,128)(2,1)} %out_weight_ref.3, bf16[2,1024,512]{2,1,0:T(8,128)(2,1)} %get-tuple-element.46.gg_ref, f32[8,8,128]{2,1,0:T(8,128)} %get-tuple-element.47.sums_ref), custom_call_target="tpu_custom_call" | custom-call | flops 12000000000 | bytes 16000000 | tf_op jit(solution)/shard_map/cross_sums/pallas_call | solution.py:754
  227.1 56.4 %mixer_backward.1 = (bf16[2,1024,1408]{2,1,0:T(8,128)(2,1)}, bf16[2048,2048]{1,0:T(8,128)(2,1)}, f32[8,768]{1,0:T(8,128)}, f32[8,512]{1,0:T(8,128)}, f32[8,128]{1,0:T(8,128)}) custom-call(s32[2,4]{1,0:T(2,128)} %bitcast.56, f32[1]{0:T(128)} %bitcast.1.active_ref, bf16[2,1024,1408]{2,1,0:T(8,128)(2,1)} %get-tuple-element.44.proj_ref, ...), custom_call_target="tpu_custom_call" | custom-call | flops 60000002048 | bytes 60000000 | tf_op jit(solution)/shard_map/mixer_backward/pallas_call | solution.py:800
  283.6 0.0 reduce-scatter.5.cloned.1.call-update
  283.6 0.7 copy-done.8
  284.3 0.6 reshape.155.in_gain_ref
  284.9 0.8 slice.28
  285.7 0.6 dynamic-slice_bitcast_fusion.1
  286.3 1.8 multiply_convert_fusion.gnorm_ref
  288.1 7.7 %reduce-scatter.3.cloned.1.call-done = bf16[256,2048]{1,0:T(8,128)(2,1)} async-done(((bf16[2048,2048]{1,0:T(8,128)(2,1)}), bf16[256,2048]{1,0:T(8,128)(2,1)}) %reduce-scatter.3.cloned.1.call-update) | async-done | bytes 1048592 | tf_op jit(solution)/shard_map/reduce_scatter | solution.py:1633
  295.8 149.5 %bring_home.1 = (f32[256,2128]{1,0:T(8,128)}, f32[1024,256]{1,0:T(8,128)}, f32[4,4352]{1,0:T(4,128)}, f32[1,4352]{1,0:T(1,128)}, f32[1,4096]{1,0:T(1,128)}, /*index=5*/f32[8,64]{1,0:T(8,128)}, f32[8,256]{1,0:T(8,128)}) custom-call(bf16[2,1024,2048]{2,1,0:T(8,128)(2,1)} %get-tuple-element.42.x_ref.normed_ref, ...), custom_call_target="tpu_custom_call" | custom-call | flops 149999992832 | bytes 33554432 | tf_op jit(solution)/shard_map/bring_home/pallas_call | solution.py:1497
  445.3 0.0 reduce-scatter.5.cloned.1.call-done
  445.4 1.3 copy.36
  446.7 1.6 fusion.3
  448.3 1.3 slice_bitcast_fusion
  449.7 3.1 copy.31
  452.8 0.7 reduce.1
  453.5 3.6 fusion.5
  457.1 0.6 copy.40
  457.7 0.6 copy.41
  458.3 1.0 copy.42
  (52 shorter events, 0.3 us)
Async XLA Ops:
  7.2 288.6 %reduce-scatter.3.cloned.1.call-start = ((), (), s32[]{:S(2)}) async-start(), calls=%async_computation.2 | async-start | bytes 9437184 | tf_op jit(solution)/shard_map/reduce_scatter | solution.py:1633
  7.2 7.9 %copy-start.12 = (s32[512]{0:T(512)}, s32[512]{0:T(512)S(1)}, u32[]{:S(2)}) copy-start(s32[512]{0:T(512)S(1)} %add_select_fusion) | copy-start | bytes 6148
  10.0 5.1 %copy-start.18 = (f32[2,128]{1,0:T(2,128)}, f32[2,128]{1,0:T(2,128)S(1)}, u32[]{:S(2)}) copy-start(f32[2,128]{1,0:T(2,128)S(1)} %fusion.6) | copy-start | bytes 3076
  10.1 9.5 %copy-start.16 = (f32[2,128]{1,0:T(2,128)}, f32[2,128]{1,0:T(2,128)S(1)}, u32[]{:S(2)}) copy-start(f32[2,128]{1,0:T(2,128)S(1)} %add_rsqrt_fusion.1) | copy-start | bytes 3076
  17.4 1.5 copy-start.21
  17.4 2.1 copy-start
  17.4 2.1 copy-start.7
  18.6 2.3 copy-start.4
  22.1 100.5 %copy-start.10 = (f32[4,4352]{1,0:T(4,128)S(1)}, f32[4,4352]{1,0:T(4,128)}, u32[]{:S(2)}) copy-start(f32[4,4352]{1,0:T(4,128)} %param.16) | copy-start | bytes 208900
  202.2 0.7 copy-start.13
  202.2 243.1 %reduce-scatter.5.cloned.1.call-start = ((), (), s32[]{:S(2)}) async-start(), calls=%async_computation.3 | async-start | bytes 9437184 | tf_op jit(solution)/shard_map/reduce_scatter | solution.py:1653
  283.6 0.7 copy-start.8
  283.6 2.7 copy-start.3
  295.8 150.9 %copy-start.1 = (bf16[1,2,128,2048]{3,2,1,0:T(8,128)(2,1)S(1)}, bf16[1,2,128,2048]{3,2,1,0:T(8,128)(2,1)}, u32[]{:S(2)}) copy-start(bf16[1,2,128,2048]{3,2,1,0:T(8,128)(2,1)} %param.12) | copy-start | bytes 3145732
  295.8 150.9 %copy-start.9 = (f32[2048]{0:T(1024)S(1)}, f32[2048]{0:T(1024)}, u32[]{:S(2)}) copy-start(f32[2048]{0:T(1024)} %param.14) | copy-start | bytes 24580
  445.3 3.0 copy-start.19
  449.6 3.1 copy-start.14
  449.7 3.8 copy-start.2
  449.7 3.8 copy-start.5
  449.7 3.8 copy-start.17
  449.7 3.8 copy-start.20
  453.4 3.6 copy-start.11
  453.5 4.2 copy-start.15
  453.5 4.8 %copy-start.6 = (f32[1024,256]{1,0:T(8,128)S(1)}, f32[1024,256]{1,0:T(8,128)}, u32[]{:S(2)}) copy-start(f32[1024,256]{1,0:T(8,128)} %get-tuple-element.123) | copy-start | bytes 3145732
Sparse Core Ops, SparseCore 0:
  202.3 93.4 reduce-scatter.2
  298.1 124.3 reduce-scatter.4

commit v5 on v4

--- a/solution.py
+++ b/solution.py
@@ -205,6 +205,333 @@
 
 def line_sems(chips, parts):
     return [pltpu.SemaphoreType.DMA((chips, parts))] * 5 + [pltpu.SemaphoreType.DMA((parts,))]
+
+
+TILE = 256
+MIDDLE = 2
+LAST = 4
+
+
+def greet_all():
+    seq_total, width_total = lax.axis_size("seq"), lax.axis_size("width")
+    count = seq_total * width_total
+    place = lax.axis_index("width") * seq_total + lax.axis_index("seq")
+    barrier = pltpu.get_barrier_semaphore()
+
+    def hello(turn, carry):
+        peer = lax.rem(place + turn, count)
+        pl.semaphore_signal(
+            barrier,
+            inc=1,
+            device_id={"width": peer // seq_total, "seq": lax.rem(peer, seq_total)},
+            device_id_type=MESH,
+        )
+        return carry
+
+    lax.fori_loop(1, count, hello, 0)
+    pl.semaphore_wait(barrier, count - 1)
+
+
+def both(is_here, source, target, send, receive, device, action):
+    if action != "send":
+
+        @pl.when(is_here)
+        def _():
+            stay = pltpu.make_async_copy(source, target, receive)
+            if action == "start":
+                stay.start()
+            else:
+                stay.wait()
+
+    @pl.when(jnp.logical_not(is_here))
+    def _():
+        away = remote(source, target, send, receive, device)
+        if action == "start":
+            away.start()
+        elif action == "receive":
+            away.wait_recv()
+        else:
+            away.wait_send()
+
+
+class Meeting:
+    def __init__(self, parts, come, last, sems):
+        self.parts, self.come, self.last, self.sems = parts, come, last, sems
+        mine = lax.axis_index("width")
+        self.upper, self.lower = mine // 2, lax.rem(mine, 2)
+
+    def order(self, block):
+        odd = lax.rem(block, 2)
+        even = 1 - odd
+        first = odd * self.upper + even * self.lower
+        second = odd * self.lower + even * self.upper
+        across = 2 * (1 - self.upper) + self.lower
+        beside = 2 * self.upper + 1 - self.lower
+        return first, second, odd * across + even * beside, odd * beside + even * across
+
+    def slot(self, block, group):
+        odd = lax.rem(block, 2)
+        return odd * group + (1 - odd) * (group % 2 * 2 + group // 2)
+
+    def first(self, block):
+        side, _, partner, _ = self.order(block)
+        return remote(
+            self.parts.at[block, pl.ds(2 * (1 - side), 2)],
+            self.come.at[block],
+            self.sems.at[0, block],
+            self.sems.at[1, block],
+            {"width": partner},
+        )
+
+    def second(self, block):
+        side, place, _, partner = self.order(block)
+        return remote(
+            self.parts.at[block, 2 * side + 1 - place],
+            self.last.at[block],
+            self.sems.at[2, block],
+            self.sems.at[3, block],
+            {"width": partner},
+        )
+
+    def middle(self, block):
+        self.first(block).wait_recv()
+        side = self.order(block)[0]
+        for item in range(2):
+            slot = 2 * side + item
+            total = self.parts[block, slot].astype(F32) + self.come[block, item].astype(F32)
+            self.parts[block, slot] = total.astype(BF16)
+        self.second(block).start()
+
+    def total(self, block):
+        self.second(block).wait_recv()
+        side, place = self.order(block)[:2]
+        return self.parts[block, 2 * side + place].astype(F32) + self.last[block].astype(F32)
+
+    def sent(self, block):
+        self.first(block).wait_send()
+        self.second(block).wait_send()
+
+
+class Tiles:
+    def __init__(self, source, blocks, sems, per_tile):
+        self.source, self.blocks, self.sems, self.per_tile = source, blocks, sems, per_tile
+        self.total = source.shape[2] // TILE
+        self.chunk_rows = blocks.shape[1]
+        self.pieces = source.shape[1] // self.chunk_rows
+        self.chunks = source.shape[0] * self.pieces
+
+    def turned(self, turn):
+        return lax.rem(turn + lax.axis_index("seq") // self.per_tile, self.total)
+
+    def fetch(self, turn, chunk):
+        first = chunk % self.pieces * self.chunk_rows
+        return pltpu.make_async_copy(
+            self.source.at[
+                chunk // self.pieces,
+                pl.ds(first, self.chunk_rows),
+                pl.ds(pl.multiple_of(self.turned(turn) * TILE, TILE), TILE),
+            ],
+            self.blocks.at[chunk % 2],
+            self.sems.at[chunk % 2],
+        )
+
+    def begin(self):
+        self.fetch(0, 0).start()
+        self.fetch(0, 1).start()
+
+    def block(self, turn, chunk):
+        self.fetch(turn, chunk).wait()
+        first = chunk % self.pieces * self.chunk_rows
+        return chunk // self.pieces, slice(first, first + self.chunk_rows), self.blocks[chunk % 2]
+
+    def used(self, turn, chunk):
+        if chunk + 2 < self.chunks:
+            self.fetch(turn, chunk + 2).start()
+        else:
+
+            @pl.when(turn + 1 < self.total)
+            def _():
+                self.fetch(turn + 1, chunk + 2 - self.chunks).start()
+
+    def each(self, turn, act):
+        for item in range(self.per_tile):
+            act(self.turned(turn) * self.per_tile + item)
+
+
+class OutGrad:
+    def __init__(self, grad, gnorm, refs):
+        (
+            blocks,
+            self.acc,
+            self.stage,
+            come,
+            last,
+            self.sums,
+            self.landing,
+            fetch,
+            sems,
+            self.send,
+            self.receive,
+        ) = refs
+        self.gnorm = gnorm
+        self.sub, self.cols = self.stage.shape[2:]
+        self.meeting = Meeting(self.stage, come, last, sems)
+        self.tiles = Tiles(grad, blocks, fetch, TILE // self.cols)
+        self.width_total = lax.axis_size("width")
+        self.seq_total = lax.axis_size("seq")
+        self.owners = self.seq_total // self.width_total
+        self.me, self.mine = lax.axis_index("seq"), lax.axis_index("width")
+
+    def copy(self, target, action):
+        owner = self.me // self.owners
+        place = self.landing.at[lax.rem(self.me, self.owners), self.mine]
+        receive = self.receive.at[lax.rem(self.me, self.owners), self.mine]
+        both(
+            (owner == self.mine) & (target == self.me),
+            self.sums.at[target],
+            place,
+            self.send.at[target],
+            receive,
+            {"width": owner, "seq": target},
+            action,
+        )
+
+    def combine(self, block):
+        self.sums[block] = self.meeting.total(block).astype(BF16)
+        self.copy(block, "start")
+
+    def multiply(self, turn):
+        for chunk in range(self.tiles.chunks):
+            micro, rows, block = self.tiles.block(turn, chunk)
+            part = mm_tn(self.gnorm[micro, rows, :], block)
+            self.acc[...] = part if chunk == 0 else self.acc[...] + part
+            self.tiles.used(turn, chunk)
+        for item in range(self.tiles.per_tile):
+            block = self.tiles.turned(turn) * self.tiles.per_tile + item
+            for group in range(self.width_total):
+                self.stage[block, self.meeting.slot(block, group)] = self.acc[
+                    group * self.sub : (group + 1) * self.sub,
+                    item * self.cols : (item + 1) * self.cols,
+                ].astype(BF16)
+            self.meeting.first(block).start()
+
+    def finish(self, out_ref):
+        def sent(block, carry):
+            self.meeting.sent(block)
+            self.copy(block, "send")
+            return carry
+
+        lax.fori_loop(0, self.seq_total, sent, 0)
+        for item in range(self.owners):
+            for group in range(self.width_total):
+                source = self.mine * self.owners + item
+                both(
+                    (source == self.me) & (self.mine == group),
+                    self.sums.at[self.me],
+                    self.landing.at[item, group],
+                    self.send.at[self.me],
+                    self.receive.at[item, group],
+                    {"width": group, "seq": source},
+                    "receive",
+                )
+                row = (item * self.width_total + group) * self.sub
+                out_ref[row : row + self.sub, :] = self.landing[item, group].astype(F32)
+
+
+def out_grad_scratch(heads, group_rows, model_width):
+    seq_total, width_total = lax.axis_size("seq"), lax.axis_size("width")
+    sub, cols = heads * HEAD_DIM // width_total, model_width // seq_total
+    owners = seq_total // width_total
+    dma = pltpu.SemaphoreType.DMA
+    return [
+        pltpu.VMEM((2, min(group_rows, 1024), TILE), BF16),
+        pltpu.VMEM((heads * HEAD_DIM, TILE), F32),
+        pltpu.VMEM((seq_total, width_total, sub, cols), BF16),
+        pltpu.VMEM((seq_total, 2, sub, cols), BF16),
+        pltpu.VMEM((seq_total, sub, cols), BF16),
+        pltpu.VMEM((seq_total, sub, cols), BF16),
+        pltpu.VMEM((owners, width_total, sub, cols), BF16),
+        dma((2,)),
+        dma((4, seq_total)),
+        dma((seq_total,)),
+        dma((owners, width_total)),
+    ]
+
+
+class PairSum:
+    def __init__(self, out, come, refs):
+        self.out, self.come = out, come
+        self.hold, self.leave, self.load, self.send, self.receive, self.local = refs
+        me = lax.axis_index("seq")
+        self.core, self.sibling = lax.rem(me, 2), me + 1 - 2 * lax.rem(me, 2)
+        self.pairs = out.shape[0]
+
+    def copy(self, pair):
+        return remote(
+            self.leave.at[lax.rem(pair, 2)],
+            self.come.at[pair],
+            self.send.at[pair],
+            self.receive.at[pair],
+            {"seq": self.sibling},
+        )
+
+    def put(self, position, earlier, block):
+        pair = position // 2
+        here = lax.rem(position, 2) == self.core
+
+        @pl.when(here)
+        def _():
+            self.hold[lax.rem(pair, 2)] = block
+
+        @pl.when(jnp.logical_not(here))
+        def _():
+            @pl.when((earlier >= 0) & (earlier < self.pairs))
+            def _():
+                self.copy(earlier).wait_send()
+
+            self.leave[lax.rem(pair, 2)] = block
+            self.copy(pair).start()
+
+    def fetch(self, pair):
+        return pltpu.make_async_copy(self.come.at[pair], self.load, self.local.at[0])
+
+    def store(self, pair):
+        return pltpu.make_async_copy(self.load, self.out.at[pair], self.local.at[1])
+
+    def begin(self, pair, earlier):
+        self.copy(pair).wait_recv()
+
+        @pl.when((earlier >= 0) & (earlier < self.pairs))
+        def _():
+            self.store(earlier).wait()
+
+        self.fetch(pair).start()
+
+    def settle(self, pair):
+        self.fetch(pair).wait()
+        total = self.hold[lax.rem(pair, 2)].astype(F32) + self.load[...].astype(F32)
+        self.load[...] = total.astype(BF16)
+        self.store(pair).start()
+
+    def finish(self, last):
+        for pair in last:
+            self.copy(pair).wait_send()
+
+
+def pair_scratch(pairs, block, columns):
+    dma = pltpu.SemaphoreType.DMA
+    return [
+        pltpu.VMEM((2, block, columns), BF16),
+        pltpu.VMEM((2, block, columns), BF16),
+        pltpu.VMEM((block, columns), BF16),
+        dma((pairs,)),
+        dma((pairs,)),
+        dma((2,)),
+    ]
+
+
+def chip_groups(seq_total):
+    return [list(range(core, seq_total, 2)) for core in range(2)]
 
 
 class Chunk:
@@ -295,6 +622,7 @@
     cols_ref,
     head_ref,
     g_out,
+    come_ref,
     ext,
     state,
     *sems,
@@ -304,7 +632,8 @@
     width = heads * HEAD_DIM
     conv_width = 2 * STATE + width
     size, groups = head_groups(heads)
-    line = Line(g_ref, g_out, sems)
+    line = Line(g_ref, g_out, sems[:6])
+    pairs = PairSum(branch_ref, come_ref, sems[6:])
     early = min((g_out.shape[1] // g_ref.shape[1] - 1) // 2, line.events())
 
     @pl.when(chunk == 0)
@@ -315,6 +644,10 @@
     @pl.when((lax.rem(chunk, 2) == 0) & (chunk >= 2) & (chunk // 2 - 1 < early))
     def _():
         line.hop(chunk // 2 - 1)
+
+    @pl.when((lax.rem(chunk, 2) == 0) & (chunk >= 2))
+    def _():
+        pairs.begin(chunk // 2 - 1, chunk // 2 - 2)
 
     @pl.when(chunk == 0)
     def _():
@@ -385,12 +718,23 @@
     if pad:
         sums.append(jnp.zeros((pad, rows), F32))
     sums_ref[...] = jnp.concatenate(sums, axis=0)
-    branch_ref[...] = mm(jnp.concatenate(gated_gains, axis=0), out_weight_ref[...]).astype(BF16)
+    branch = mm(jnp.concatenate(gated_gains, axis=0), out_weight_ref[...]).astype(BF16)
+
+    @pl.when((lax.rem(chunk, 2) == 0) & (chunk >= 2))
+    def _():
+        pairs.settle(chunk // 2 - 1)
+
+    pairs.put(chunk, chunk // 2 - 2, branch)
 
     @pl.when(chunk == chunks - 1)
     def _():
+        pair_count = branch_ref.shape[0]
         line.hops(early)
+        pairs.begin(jnp.int32(pair_count - 1), jnp.int32(pair_count - 2))
+        pairs.settle(jnp.int32(pair_count - 1))
         line.finish()
+        pairs.store(pair_count - 1).wait()
+        pairs.finish(range(max(0, pair_count - 2), pair_count))
 
 
 def cross_kernel(
@@ -469,13 +813,16 @@
     gconv_ref,
     gcols_ref,
     ghead_ref,
+    come_ref,
     ext,
     heads_ext,
     dstate,
+    *pair_refs,
 ):
     chunks = pl.num_programs(0)
     step_index = pl.program_id(0)
     rows = proj_ref.shape[1]
+    pairs = PairSum(partial_ref, come_ref, pair_refs)
 
     @pl.when(step_index == 0)
     def _():
@@ -484,6 +831,17 @@
         gconv_ref[...] = jnp.zeros_like(gconv_ref)
         gcols_ref[...] = jnp.zeros_like(gcols_ref)
         ghead_ref[...] = jnp.zeros_like(ghead_ref)
+        barrier = pltpu.get_barrier_semaphore()
+        pl.semaphore_signal(
+            barrier, inc=1, device_id={"seq": pairs.sibling}, device_id_type=MESH
+        )
+        pl.semaphore_wait(barrier, 1)
+
+    position = chunks - 1 - step_index
+
+    @pl.when((lax.rem(position, 2) == 1) & (step_index >= 2))
+    def _():
+        pairs.begin((position + 1) // 2, (position + 1) // 2 + 1)
 
     for micro in range(micros):
         backward_rows(
@@ -513,11 +871,21 @@
             dstate.at[micro],
         )
     d_rows = dproj_ref[...].reshape(micros * rows, dproj_ref.shape[2])
-    partial_ref[...] = mm_nt(d_rows, weight_ref[...]).astype(BF16)
+    partial_rows = mm_nt(d_rows, weight_ref[...]).astype(BF16)
+
+    @pl.when((lax.rem(position, 2) == 1) & (step_index >= 2))
+    def _():
+        pairs.settle((position + 1) // 2)
+
+    pairs.put(position, position // 2 + 2, partial_rows)
 
     @pl.when(step_index == chunks - 1)
     def _():
         ghead_ref[2:3] = mm(halves(gcols_ref[...], 1), gather_ref[...])[0:1]
+        pairs.begin(jnp.int32(0), jnp.int32(1))
+        pairs.settle(jnp.int32(0))
+        pairs.store(0).wait()
+        pairs.finish(range(min(2, partial_ref.shape[0])))
 
 
 def backward_rows(
@@ -705,7 +1073,7 @@
         out_specs=[
             row_block(columns),
             row_block(width),
-            pl.BlockSpec((block, model_width), lambda index: (index, 0)),
+            ANY,
             row_block(width),
             pl.BlockSpec((None, micros, STATE, width), lambda index: (index, 0, 0, 0)),
             pl.BlockSpec((None, micros, 8, conv_width), lambda index: (index, 0, 0, 0)),
@@ -714,11 +1082,12 @@
             constant((8, width)),
             constant((8, LANES)),
             ANY,
+            ANY,
         ],
         out_shape=[
             jax.ShapeDtypeStruct((micros, chunks * rows, columns), BF16),
             jax.ShapeDtypeStruct((micros, chunks * rows, width), BF16),
-            jax.ShapeDtypeStruct((chunks * block, model_width), BF16),
+            jax.ShapeDtypeStruct((chunks // 2, block, model_width), BF16),
             jax.ShapeDtypeStruct((micros, chunks * rows, width), F32),
             jax.ShapeDtypeStruct((chunks, micros, STATE, width), BF16),
             jax.ShapeDtypeStruct((chunks, micros, 8, conv_width), F32),
@@ -727,12 +1096,14 @@
             jax.ShapeDtypeStruct((8, width), F32),
             jax.ShapeDtypeStruct((8, LANES), F32),
             jax.ShapeDtypeStruct((micros, chunks * rows, model_width), BF16),
+            jax.ShapeDtypeStruct((chunks // 2, block, model_width), BF16),
         ],
         scratch_shapes=[
             pltpu.VMEM((micros, rows + 8, conv_width), F32),
             pltpu.VMEM((micros, STATE, width), F32),
         ]
-        + line_sems(chunks // 2, micros),
+        + line_sems(chunks // 2, micros)
+        + pair_scratch(chunks // 2, block, model_width),
         compiler_params=pltpu.CompilerParams(
             collective_id=collective_id, has_side_effects=True, vmem_limit_bytes=56 << 20
         ),
@@ -782,7 +1153,18 @@
 
 
 def run_backward(
-    heads, starts, active, proj, dnorm, mixed, states, tails, sums, weight, shared
+    heads,
+    starts,
+    active,
+    proj,
+    dnorm,
+    mixed,
+    states,
+    tails,
+    sums,
+    weight,
+    shared,
+    collective_id,
 ):
     micros, all_rows, columns = proj.shape
     chunks = sums.shape[0]
@@ -814,24 +1196,29 @@
         + [constant(item.shape) for item in shared],
         out_specs=[
             row_block(columns),
-            pl.BlockSpec((micros * rows, model_width), lambda index: (chunks - 1 - index, 0)),
+            ANY,
             constant((8, conv_width)),
             constant((8, width)),
             constant((8, LANES)),
+            ANY,
         ],
         out_shape=[
             jax.ShapeDtypeStruct((micros, all_rows, columns), BF16),
-            jax.ShapeDtypeStruct((micros * all_rows, model_width), BF16),
+            jax.ShapeDtypeStruct((chunks // 2, micros * rows, model_width), BF16),
             jax.ShapeDtypeStruct((8, conv_width), F32),
             jax.ShapeDtypeStruct((8, width), F32),
             jax.ShapeDtypeStruct((8, LANES), F32),
+            jax.ShapeDtypeStruct((chunks // 2, micros * rows, model_width), BF16),
         ],
         scratch_shapes=[
             pltpu.VMEM((micros, rows + 8, conv_width), F32),
             pltpu.VMEM((micros, TAPS - 1, rows + 8, conv_width), F32),
             pltpu.VMEM((micros, STATE, width), F32),
-        ],
-        compiler_params=pltpu.CompilerParams(vmem_limit_bytes=56 << 20),
+        ]
+        + pair_scratch(chunks // 2, micros * rows, model_width),
+        compiler_params=pltpu.CompilerParams(
+            collective_id=collective_id, has_side_effects=True, vmem_limit_bytes=60 << 20
+        ),
         cost_estimate=pl.CostEstimate(
             flops=60 * 10**9, bytes_accessed=60 * 10**6, transcendentals=0
         ),
@@ -964,11 +1351,6 @@
     )(x, pieces)
 
 
-TILE = 256
-MIDDLE = 2
-LAST = 4
-
-
 def home_kernel(
     layout,
     normed_ref,
@@ -977,9 +1359,9 @@
     gcols_ref,
     ghead_ref,
     in_gain_ref,
+    dproj_ref,
     grad_ref,
     gnorm_ref,
-    dproj_ref,
     shard_in_ref,
     shard_out_ref,
     taps_out,
@@ -989,22 +1371,16 @@
     in_gain_out,
     zx_ref,
     bc_ref,
-    go_ref,
     small_out,
     line_buffer,
     blocks_in,
     acc,
-    out_acc,
     stage,
     arrived,
     last_arrived,
     sum_x,
     sum_z,
     sum_b,
-    out_stage,
-    out_arrived,
-    out_last,
-    sum_out,
     small_stage,
     small_slots,
     fetch,
@@ -1013,13 +1389,15 @@
     zx_receive,
     bc_send,
     bc_receive,
-    out_sems,
-    go_send,
-    go_receive,
     small_send,
     small_receive,
     last_send,
     last_receive,
+    bc_total,
+    bc_last,
+    bc_last_send,
+    bc_last_receive,
+    *out_refs,
 ):
     seq_total, width_total, quarter, width, slots, shard, heads = layout
     micros = normed_ref.shape[0]
@@ -1028,194 +1406,28 @@
     conv_width = 2 * STATE + width
     per_tile = TILE // depth
     tiles = seq_total // per_tile
-    chunk_rows = blocks_in.shape[1]
-    pieces = normed_ref.shape[1] // chunk_rows
-    chunks = micros * pieces
-    owners = seq_total // width_total
-    barrier = pltpu.get_barrier_semaphore()
-    count = seq_total * width_total
-    place = mine * seq_total + me
-
-    def turned(turn):
-        return lax.rem(turn + me // per_tile, tiles)
-
-    def fetch_copy(source, turn, chunk):
-        tile = turned(turn)
-        first = chunk % pieces * chunk_rows
-        return pltpu.make_async_copy(
-            source.at[
-                chunk // pieces,
-                pl.ds(first, chunk_rows),
-                pl.ds(pl.multiple_of(tile * TILE, TILE), TILE),
-            ],
-            blocks_in.at[chunk % 2],
-            fetch.at[chunk % 2],
-        )
-
-    def fetched(source, following, turn, chunk):
-        fetch_copy(source, turn, chunk).wait()
-        if chunk + 1 < chunks:
-            fetch_copy(source, turn, chunk + 1).start()
-        else:
-
-            @pl.when(turn + 1 < tiles)
-            def _():
-                fetch_copy(source, turn + 1, 0).start()
-
-            if following is not None:
-
-                @pl.when(turn + 1 == tiles)
-                def _():
-                    fetch_copy(following, 0, 0).start()
-
-        return blocks_in[chunk % 2]
-
-    fetch_copy(grad_ref, 0, 0).start()
-
-    def hello(turn, carry):
-        peer = lax.rem(place + turn, count)
-        pl.semaphore_signal(
-            barrier,
-            inc=1,
-            device_id={"width": peer // seq_total, "seq": lax.rem(peer, seq_total)},
-            device_id_type=MESH,
-        )
-        return carry
-
-    lax.fori_loop(1, count, hello, 0)
-    pl.semaphore_wait(barrier, count - 1)
-
-    def both(is_here, source, target, send, receive, device, action):
-        if action != "send":
-
-            @pl.when(is_here)
-            def _():
-                stay = pltpu.make_async_copy(source, target, receive)
-                if action == "start":
-                    stay.start()
-                else:
-                    stay.wait()
-
-        @pl.when(jnp.logical_not(is_here))
-        def _():
-            away = remote(source, target, send, receive, device)
-            if action == "start":
-                away.start()
-            elif action == "receive":
-                away.wait_recv()
-            else:
-                away.wait_send()
-
-    sub, cols = out_stage.shape[2:]
-    per_out = TILE // cols
-
-    upper, lower = mine // 2, lax.rem(mine, 2)
-
-    def order(block):
-        odd = lax.rem(block, 2)
-        even = 1 - odd
-        first = odd * upper + even * lower
-        second = odd * lower + even * upper
-        across = 2 * (1 - upper) + lower
-        beside = 2 * upper + 1 - lower
-        return first, second, odd * across + even * beside, odd * beside + even * across
-
-    def slot_of(block, group):
-        odd = lax.rem(block, 2)
-        return odd * group + (1 - odd) * (group % 2 * 2 + group // 2)
-
-    class Meeting:
-        def __init__(self, parts, come, last, sems):
-            self.parts, self.come, self.last, self.sems = parts, come, last, sems
-
-        def first(self, block):
-            side, _, partner, _ = order(block)
-            return remote(
-                self.parts.at[block, pl.ds(2 * (1 - side), 2)],
-                self.come.at[block],
-                self.sems.at[0, block],
-                self.sems.at[1, block],
-                {"width": partner},
-            )
-
-        def second(self, block):
-            side, place, _, partner = order(block)
-            return remote(
-                self.parts.at[block, 2 * side + 1 - place],
-                self.last.at[block],
-                self.sems.at[2, block],
-                self.sems.at[3, block],
-                {"width": partner},
-            )
-
-        def middle(self, block):
-            self.first(block).wait_recv()
-            side = order(block)[0]
-            for item in range(2):
-                slot = 2 * side + item
-                total = self.parts[block, slot].astype(F32) + self.come[block, item].astype(F32)
-                self.parts[block, slot] = total.astype(BF16)
-            self.second(block).start()
-
-        def total(self, block):
-            self.second(block).wait_recv()
-            side, place = order(block)[:2]
-            return self.parts[block, 2 * side + place].astype(F32) + self.last[block].astype(F32)
-
-        def sent(self, block):
-            self.first(block).wait_send()
-            self.second(block).wait_send()
-
-    out_meeting = Meeting(out_stage, out_arrived, out_last, out_sems)
-    in_meeting = Meeting(stage, arrived, last_arrived, in_sems)
-
-    def each(turn, per, act):
-        for item in range(per):
-            act(turned(turn) * per + item)
-
-    go_owner = me // owners
-
-    def go_copy(target, action):
-        both(
-            (go_owner == mine) & (target == me),
-            sum_out.at[target],
-            go_ref.at[lax.rem(me, owners), mine],
-            go_send.at[target],
-            go_receive.at[lax.rem(me, owners), mine],
-            {"width": go_owner, "seq": target},
-            action,
-        )
-
-    def out_combine(block):
-        sum_out[block] = out_meeting.total(block).astype(BF16)
-        go_copy(block, "start")
+    rows_in = Tiles(normed_ref, blocks_in, fetch, per_tile)
+    meeting = Meeting(stage, arrived, last_arrived, in_sems)
+    out_grad = OutGrad(grad_ref, gnorm_ref, out_refs)
+    out_grad.tiles.begin()
+    greet_all()
 
     def out_multiply(turn, carry):
-        tile = turned(turn)
-        for chunk in range(chunks):
-            block = fetched(grad_ref, normed_ref, turn, chunk)
-            first = chunk % pieces * chunk_rows
-            part = mm_tn(gnorm_ref[chunk // pieces, first : first + chunk_rows, :], block)
-            out_acc[...] = part if chunk == 0 else out_acc[...] + part
-        for item in range(per_out):
-            block = tile * per_out + item
-            for group in range(width_total):
-                out_stage[block, slot_of(block, group)] = out_acc[
-                    group * sub : (group + 1) * sub, item * cols : (item + 1) * cols
-                ].astype(BF16)
-            out_meeting.first(block).start()
+        out_grad.multiply(turn)
 
         @pl.when(turn >= MIDDLE)
         def _():
-            each(turn - MIDDLE, per_out, out_meeting.middle)
+            out_grad.tiles.each(turn - MIDDLE, out_grad.meeting.middle)
 
         @pl.when(turn >= LAST)
         def _():
-            each(turn - LAST, per_out, out_combine)
+            out_grad.tiles.each(turn - LAST, out_grad.combine)
 
         return carry
 
+    rows_in.begin()
     lax.fori_loop(0, tiles, out_multiply, 0)
+
     conv_end = conv_width + width
     small_stage[:, :conv_width] = gconv_ref[...]
     small_stage[:, conv_width:conv_end] = gcols_ref[...]
@@ -1245,12 +1457,23 @@
 
     def bc_copy(block, action):
         both(
-            (mine == width_total - 1) & (block == me),
+            block == me,
             sum_b.at[block],
-            bc_ref.at[me, mine],
+            bc_ref.at[me],
             bc_send.at[block],
-            bc_receive.at[me, mine],
-            {"width": width_total - 1, "seq": block},
+            bc_receive.at[me],
+            {"seq": block},
+            action,
+        )
+
+    def bc_home(source, action):
+        both(
+            (mine == width_total - 1) & (source == mine),
+            bc_total,
+            bc_last.at[source],
+            bc_last_send.at[0],
+            bc_last_receive.at[source],
+            {"width": width_total - 1},
             action,
         )
 
@@ -1261,7 +1484,7 @@
         bc_copy(block, action)
 
     def combine(block):
-        low = in_meeting.total(block).astype(BF16)
+        low = meeting.total(block).astype(BF16)
         sum_b[block, :, : 2 * STATE] = low[:, : 2 * STATE]
         sum_x[block] = low[:, 2 * STATE : conv_width]
         sum_z[block] = low[:, conv_width : conv_width + width]
@@ -1269,20 +1492,18 @@
         pieces_of(block, "start")
 
     def multiply(turn, carry):
-        tile = turned(turn)
-        for chunk in range(chunks):
-            block = fetched(normed_ref, None, turn, chunk)
-            first = chunk % pieces * chunk_rows
-            part = mm_tn(
-                block, dproj_ref[chunk // pieces, first : first + chunk_rows, :]
-            )
+        tile = rows_in.turned(turn)
+        for chunk in range(rows_in.chunks):
+            micro, rows, block = rows_in.block(turn, chunk)
+            part = mm_tn(block, dproj_ref[micro, rows, :])
             acc[...] = part if chunk == 0 else acc[...] + part
+            rows_in.used(turn, chunk)
         for item in range(per_tile):
             block = tile * per_tile + item
             for group in range(width_total):
                 row = item * depth + group * quarter
-                stage[block, slot_of(block, group)] = acc[row : row + quarter].astype(BF16)
-            in_meeting.first(block).start()
+                stage[block, meeting.slot(block, group)] = acc[row : row + quarter].astype(BF16)
+            meeting.first(block).start()
         weights = columns_ref[pl.ds(pl.multiple_of(tile * TILE, TILE), TILE), :]
         product = (acc[...] * weights.astype(F32)).astype(BF16)
         line = mm_nt(jnp.ones((8, product.shape[1]), BF16), product)
@@ -1290,19 +1511,19 @@
 
         @pl.when(turn < MIDDLE)
         def _():
-            each(tiles - MIDDLE + turn, per_out, out_meeting.middle)
+            out_grad.tiles.each(tiles - MIDDLE + turn, out_grad.meeting.middle)
 
         @pl.when(turn >= MIDDLE)
         def _():
-            each(turn - MIDDLE, per_tile, in_meeting.middle)
+            rows_in.each(turn - MIDDLE, meeting.middle)
 
         @pl.when(turn < LAST)
         def _():
-            each(tiles - LAST + turn, per_out, out_combine)
+            out_grad.tiles.each(tiles - LAST + turn, out_grad.combine)
 
         @pl.when(turn >= LAST)
         def _():
-            each(turn - LAST, per_tile, combine)
+            rows_in.each(turn - LAST, combine)
 
         return carry
 
@@ -1323,11 +1544,35 @@
         small_hop(turn, False).start()
     small_slots[mine] = small_stage[...]
 
-    for tile in range(tiles - LAST, tiles):
-        if tile >= tiles - MIDDLE:
-            each(tile, per_tile, in_meeting.middle)
-    for tile in range(tiles - LAST, tiles):
-        each(tile, per_tile, combine)
+    for turn in range(tiles - MIDDLE, tiles):
+        rows_in.each(turn, meeting.middle)
+    for turn in range(tiles - LAST, tiles):
+        rows_in.each(turn, combine)
+
+    def bc_arrive(turn, carry):
+        source = lax.rem(me + turn, seq_total)
+        both(
+            source == me,
+            sum_b.at[me],
+            bc_ref.at[source],
+            bc_send.at[me],
+            bc_receive.at[source],
+            {"seq": source},
+            "receive",
+        )
+        return carry
+
+    lax.fori_loop(0, seq_total, bc_arrive, 0)
+
+    def bc_add(source, total):
+        return total + bc_ref[source, :, : 2 * STATE].astype(F32)
+
+    bc_sum = lax.fori_loop(1, seq_total, bc_add, bc_ref[0, :, : 2 * STATE].astype(F32))
+    bc_total[:, : 2 * STATE] = bc_sum.astype(BF16)
+    for source in range(seq_total):
+        at = 2 * STATE + source * heads
+        bc_total[:, at : at + heads] = bc_ref[source, :, 2 * STATE : 2 * STATE + heads]
+    bc_home(mine, "start")
 
     for turn in range(1, width_total):
         small_hop(turn, True).wait_recv()
@@ -1356,10 +1601,8 @@
     small_out[me] = small_stage[...]
 
     def sent(block, carry):
-        in_meeting.sent(block)
-        out_meeting.sent(block)
+        meeting.sent(block)
         pieces_of(block, "send")
-        go_copy(block, "send")
         return carry
 
     lax.fori_loop(0, seq_total, sent, 0)
@@ -1387,35 +1630,14 @@
 
     lax.fori_loop(0, slots, landed, 0)
 
+    bc_home(mine, "send")
+
     @pl.when(mine == width_total - 1)
     def _():
-        def bc_landed(source, carry):
-            for group in range(width_total):
-                both(
-                    (source == me) & (mine == group),
-                    sum_b.at[me],
-                    bc_ref.at[source, group],
-                    bc_send.at[me],
-                    bc_receive.at[source, group],
-                    {"width": group, "seq": source},
-                    "receive",
-                )
-            return carry
-
-        lax.fori_loop(0, seq_total, bc_landed, 0)
-
-    for item in range(owners):
-        for group in range(width_total):
-            source = mine * owners + item
-            both(
-                (source == me) & (mine == group),
-                sum_out.at[me],
-                go_ref.at[item, group],
-                go_send.at[me],
-                go_receive.at[item, group],
-                {"width": group, "seq": source},
-                "receive",
-            )
+        for source in range(width_total):
+            bc_home(source, "receive")
+
+    out_grad.finish(shard_out_ref)
 
     def last_end(turn, carry):
         last_hop(turn, False).wait_send()
@@ -1431,18 +1653,9 @@
 
         @pl.when(mine == width_total - 1)
         def _():
-            def bc_add(source, total):
-                return total + bc_ref[source, group, :, : 2 * STATE].astype(F32)
-
-            first_sum = bc_ref[0, group, :, : 2 * STATE].astype(F32)
-            line_buffer[:, edge : edge + 2 * STATE] = lax.fori_loop(
-                1, seq_total, bc_add, first_sum
-            )
-            for source in range(seq_total):
-                at = edge + 2 * STATE + source * heads
-                line_buffer[:, at : at + heads] = bc_ref[
-                    source, group, :, 2 * STATE : 2 * STATE + heads
-                ].astype(F32)
+            line_buffer[:, edge : edge + 2 * STATE + HEADS] = bc_last[
+                group, :, : 2 * STATE + HEADS
+            ].astype(F32)
 
         total_lanes = line_buffer.shape[1]
         start = lax.rem(mine * shard, jnp.int32(width))
@@ -1450,11 +1663,6 @@
             line_buffer[...], lax.rem(total_lanes - start, jnp.int32(total_lanes)), 1
         )
         shard_in_ref[group * quarter : (group + 1) * quarter, :] = rolled[:, :shard]
-    for item in range(owners):
-        for group in range(width_total):
-            row = item * width + group * sub
-            shard_out_ref[row : row + sub, :] = go_ref[item, group].astype(F32)
-
     def small_add(source, total):
         return total + small_out[source]
 
@@ -1488,19 +1696,17 @@
     all_columns = dproj.shape[2]
     layout = (seq_total, width_total, quarter, width, slots, shard, heads)
     rest = all_columns - 2 * width
-    sub, cols = width // width_total, model_width // seq_total
-    owners = seq_total // width_total
     small = (8, 2 * STATE + 2 * width + LANES + TILE)
     lanes = -(-slots * width // LANES) * LANES
     dma = pltpu.SemaphoreType.DMA
     vmem = pl.BlockSpec(memory_space=pltpu.VMEM)
     return pl.pallas_call(
         partial(home_kernel, layout),
-        in_specs=[ANY, vmem, vmem, vmem, vmem, vmem, ANY, vmem, vmem],
+        in_specs=[ANY] + [vmem] * 6 + [ANY, vmem],
         out_specs=[vmem] * 7,
         out_shape=[
             jax.ShapeDtypeStruct((depth, shard), F32),
-            jax.ShapeDtypeStruct((owners * width, cols), F32),
+            jax.ShapeDtypeStruct((seq_total // width_total * width, model_width // seq_total), F32),
             jax.ShapeDtypeStruct((TAPS, CONV), F32),
             jax.ShapeDtypeStruct((1, CONV), F32),
             jax.ShapeDtypeStruct((1, INNER), F32),
@@ -1509,23 +1715,17 @@
         ],
         scratch_shapes=[
             pltpu.VMEM((slots, width_total, quarter, width), BF16),
-            pltpu.VMEM((seq_total, width_total, quarter, rest), BF16),
-            pltpu.VMEM((owners, width_total, sub, cols), BF16),
+            pltpu.VMEM((seq_total, quarter, rest), BF16),
             pltpu.VMEM((seq_total,) + small, F32),
             pltpu.VMEM((quarter, lanes), F32),
             pltpu.VMEM((2, min(group_rows, 1024), TILE), BF16),
             pltpu.VMEM((TILE, all_columns), F32),
-            pltpu.VMEM((width, TILE), F32),
             pltpu.VMEM((seq_total, width_total, quarter, all_columns), BF16),
             pltpu.VMEM((seq_total, 2, quarter, all_columns), BF16),
             pltpu.VMEM((seq_total, quarter, all_columns), BF16),
             pltpu.VMEM((seq_total, quarter, width), BF16),
             pltpu.VMEM((seq_total, quarter, width), BF16),
             pltpu.VMEM((seq_total, quarter, rest), BF16),
-            pltpu.VMEM((seq_total, width_total, sub, cols), BF16),
-            pltpu.VMEM((seq_total, 2, sub, cols), BF16),
-            pltpu.VMEM((seq_total, sub, cols), BF16),
-            pltpu.VMEM((seq_total, sub, cols), BF16),
             pltpu.VMEM(small, F32),
             pltpu.VMEM((width_total,) + small, F32),
             dma((2,)),
@@ -1533,23 +1733,25 @@
             dma((4, seq_total)),
             dma((slots, width_total)),
             dma((seq_total,)),
-            dma((seq_total, width_total)),
-            dma((4, seq_total)),
             dma((seq_total,)),
-            dma((owners, width_total)),
             dma((width_total,)),
             dma((width_total,)),
             dma((seq_total,)),
             dma((seq_total,)),
-        ],
+            pltpu.VMEM((quarter, rest), BF16),
+            pltpu.VMEM((width_total, quarter, rest), BF16),
+            dma((1,)),
+            dma((width_total,)),
+        ]
+        + out_grad_scratch(heads, group_rows, model_width),
         compiler_params=pltpu.CompilerParams(
-            collective_id=collective_id, has_side_effects=True, vmem_limit_bytes=60 << 20
+            collective_id=collective_id, has_side_effects=True, vmem_limit_bytes=62 << 20
         ),
         cost_estimate=pl.CostEstimate(
             flops=150 * 10**9, bytes_accessed=8 * normed.size, transcendentals=0
         ),
         name="bring_home",
-    )(normed, columns, *smalls, in_gain, grad, gnorm, dproj)
+    )(normed, columns, *smalls, in_gain, dproj, grad, gnorm)
 
 
 def own(value, start, count, axis=0):
@@ -1617,7 +1819,7 @@
     )
     expand, gather, tri = tables(heads, rows)
 
-    proj, gg, branch, mixed, states, tails, sums, taps, cols, head, all_grad = run_forward(
+    proj, gg, branch, mixed, states, tails, sums, taps, cols, head, all_grad, _ = run_forward(
         heads,
         starts[0],
         all_normed,
@@ -1630,7 +1832,8 @@
         tri,
         3,
     )
-    branch = lax.psum_scatter(branch, "seq", scatter_dimension=0, tiled=True)
+    chip_wise = dict(axis_index_groups=chip_groups(seq_total), scatter_dimension=0, tiled=True)
+    branch = lax.psum_scatter(branch, "seq", **chip_wise)
     dnorm, sums = run_cross(all_grad, out_weight, gg, sums, 1)
     roots = lax.rsqrt(sums[:, : 2 * micros : 2] / active + EPSILON)
     own_roots = own(roots, seq_index, 1).reshape(micros, rows, 1)
@@ -1649,8 +1852,10 @@
         sums,
         columns,
         [taps, head, cols, expand, gather, tri],
+        4,
     )
-    scattered = lax.psum_scatter(partial_rows, "seq", scatter_dimension=0, tiled=True)
+    smalls.pop()
+    scattered = lax.psum_scatter(partial_rows, "seq", **chip_wise)
     head_sums, branch = lax.optimization_barrier((smalls[2], branch))
     home = bring_home(
         all_normed,

time: 468 us -> 456 us (0.974)
  waiting for transfers between devices: 7.8 us -> 0.06 us
    pallas_call x1, Pallas kernels: 150 us -> 139 us  [bring_home(): pl.pallas_call(partial(home_kernel, layout), in_specs=[ANY] + [vmem] * 6...]
    reduce_scatter x2, waiting for transfers between devices: 7.77 us -> 0.02 us  [the longest x1 0.02 us: per_device(): scattered = lax.psum_scatter(partial_rows, 'seq', **chip_wise)]
    pallas_call x1, Pallas kernels: 56.4 us -> 63.3 us  [run_backward(): pl.pallas_call(partial(backward_kernel, micros, heads), grid=(chunks,), i...]
  transfers between devices with their start and end apart: 2 -> 2, of which waited for: 1 -> 0; matrix products, arithmetic and copies ran while one was open for 1% -> 1% of each run, Pallas kernels for 49% -> 50%
where the time goes in v5:
time: 456 us; the launch traced here: 455 us
  Pallas kernels  406 us (89%)
  local copies, waits for them, and re-layouts  19.3 us (4%)
  other arithmetic  15.6 us (3%)
  between operations  14.4 us (3%)
    pallas_call x1, Pallas kernels, bring_home(): pl.pallas_call(partial(home_kernel, layout), in_specs=[ANY] + [vmem] * 6...  139 us
    pallas_call x1, Pallas kernels, gather_rows(): pl.pallas_call(gather_kernel, in_specs=[ANY] * 2, out_specs=[ANY] * 2, ou...  100 us
    pallas_call x1, Pallas kernels, run_forward(): pl.pallas_call(partial(forward_kernel, micros, heads), grid=(chunks,), in...  79.1 us
    pallas_call x1, Pallas kernels, run_backward(): pl.pallas_call(partial(backward_kernel, micros, heads), grid=(chunks,), i...  63.3 us
    pallas_call x1, Pallas kernels, run_cross(): pl.pallas_call(cross_kernel, grid=(chunks,), in_specs=[row_block(model_wi...  23.3 us
  transfers between devices with their start and end apart: 2, of which 0 were waited for; matrix products, arithmetic and copies ran while one was open for 1% of the time, Pallas kernels for 50%

profile of v5, /device:TPU:0, one launch (start us, length us, event | category | flops | bytes accessed | tf_op | source)
XLA Modules:
  0.0 455.3 jit_solution(11692326130522362188)
XLA Ops:
  7.2 0.0 reduce-scatter.3.cloned.1.call-start
  7.2 0.6 fusion.11.tri_ref
  7.9 0.7 negate_bitcast_fusion
  8.5 1.5 fusion.6
  10.1 0.7 broadcast_in_dim.16
  10.8 0.7 pad.16
  11.6 0.7 broadcast_in_dim.36
  12.3 0.1 reshape.163
  12.4 0.8 dynamic-slice_bitcast_fusion
  13.2 0.9 dynamic-slice
  14.1 0.1 copy.25
  14.3 0.1 copy.28
  14.4 0.7 add_convert_fusion.expand_ref
  15.1 2.3 fusion.16
  17.4 0.0 copy-start.18
  17.4 0.0 copy-start.6
  17.4 1.1 copy.29
  18.6 0.3 copy.30
  18.9 0.6 select_maximum_fusion.heads_ref
  19.5 1.3 fusion.8.x_ref
  20.8 1.2 fusion.10.w_ref
  22.1 100.5 %gather_rows.1 = (bf16[2,1024,2048]{2,1,0:T(8,128)(2,1)}, bf16[2048,1408]{1,0:T(8,128)(2,1)}) custom-call(bf16[2,128,2048]{2,1,0:T(8,128)(2,1)} %fusion.8.x_ref, bf16[8,64,1408]{2,1,0:T(8,128)(2,1)} %fusion.10.w_ref), custom_call_target="tpu_custom_call" | custom-call | flops 80000000000 | bytes 200000000 | tf_op jit(solution)/shard_map/gather_rows/pallas_call | solution.py:1328
  122.6 0.8 concatenate.17.table_ref
  123.4 79.1 %mixer_forward.1 = (bf16[2,1024,1408]{2,1,0:T(8,128)(2,1)}, bf16[2,1024,512]{2,1,0:T(8,128)(2,1)}, bf16[4,256,2048]{2,1,0:T(8,128)(2,1)}, f32[2,1024,512]{2,1,0:...) custom-call(s32[2,4]{1,0:T(2,128)} %bitcast.55, ...), custom_call_target="tpu_custom_call" | custom-call | flops 60000002048 | bytes 150000000 | tf_op jit(solution)/shard_map/mixer_forward/pallas_call | solution.py:1059
  202.5 0.0 reduce-scatter.3.cloned.1.call-update
  202.5 0.2 reduce-scatter.5.cloned.1.call-start
  202.7 0.1 iota_compare_fusion.1
  202.9 0.7 add_convert_fusion.1.gather_ref
  203.6 23.3 %cross_sums.1 = (f32[2,1024,512]{2,1,0:T(8,128)}, f32[8,8,128]{2,1,0:T(8,128)}) custom-call(bf16[2,1024,2048]{2,1,0:T(8,128)(2,1)} %get-tuple-element.45.g_ref.grad_ref, bf16[512,2048]{1,0:T(8,128)(2,1)} %out_weight_ref.3, bf16[2,1024,512]{2,1,0:T(8,128)(2,1)} %get-tuple-element.46.gg_ref, f32[8,8,128]{2,1,0:T(8,128)} %get-tuple-element.47.sums_ref), custom_call_target="tpu_custom_call" | custom-call | flops 12000000000 | bytes 16000000 | tf_op jit(solution)/shard_map/cross_sums/pallas_call | solution.py:1125
  226.9 63.3 %mixer_backward.1 = (bf16[2,1024,1408]{2,1,0:T(8,128)(2,1)}, bf16[4,256,2048]{2,1,0:T(8,128)(2,1)}, f32[8,768]{1,0:T(8,128)}, f32[8,512]{1,0:T(8,128)}, f32[8,128]{1,0:T(8,128)}, /*index=5*/bf16[4,256,2048]{2,1,0:T(8,128)(2,1)}) custom-call(s32[2,4]{1,0:T(2,128)} %bitcast.56, f32[1]{0:T(128)} %bitcast.1.active_ref, ...), custom_call_target="tpu_custom_call" | custom-call | flops 60000002048 | bytes 60000000 | tf_op jit(solution)/shard_map/mixer_backward/pallas_call | solution.py:1182
  290.3 0.0 reduce-scatter.5.cloned.1.call-update
  290.3 0.7 copy-done.7
  291.0 0.6 reshape.164.in_gain_ref
  291.6 0.8 slice.28
  292.4 1.8 multiply_convert_fusion.gnorm_ref
  294.2 0.6 dynamic-slice_bitcast_fusion.1
  294.8 139.4 %bring_home.1 = (f32[256,2128]{1,0:T(8,128)}, f32[1024,256]{1,0:T(8,128)}, f32[4,4352]{1,0:T(4,128)}, f32[1,4352]{1,0:T(1,128)}, f32[1,4096]{1,0:T(1,128)}, /*index=5*/f32[8,64]{1,0:T(8,128)}, f32[8,256]{1,0:T(8,128)}) custom-call(bf16[2,1024,2048]{2,1,0:T(8,128)(2,1)} %get-tuple-element.42.x_ref.normed_ref, ...), custom_call_target="tpu_custom_call" | custom-call | flops 149999992832 | bytes 33554432 | tf_op jit(solution)/shard_map/bring_home/pallas_call | solution.py:1703
  434.2 0.0 copy-start.16
  434.2 0.0 reduce-scatter.5.cloned.1.call-done
  434.3 1.3 copy.36
  435.6 1.6 fusion.3
  437.2 1.3 slice_bitcast_fusion
  438.6 3.0 copy.31
  441.6 0.7 reduce.1
  442.3 3.9 fusion.5
  446.2 0.6 copy.40
  446.8 0.6 copy.41
  447.4 1.0 copy.42
  (46 shorter events, 0.2 us)
Async XLA Ops:
  7.2 287.6 %reduce-scatter.3.cloned.1.call-start = ((), (), s32[]{:S(2)}) async-start(), calls=%async_computation.2 | async-start | bytes 5242880 | tf_op jit(solution)/shard_map/reduce_scatter | solution.py:1836
  10.0 1.5 copy-start.15
  10.1 9.5 %copy-start.13 = (f32[2,128]{1,0:T(2,128)}, f32[2,128]{1,0:T(2,128)S(1)}, u32[]{:S(2)}) copy-start(f32[2,128]{1,0:T(2,128)S(1)} %add_rsqrt_fusion.1) | copy-start | bytes 3076
  17.4 1.5 copy-start.18
  17.4 2.1 copy-start
  17.4 2.1 copy-start.6
  18.6 2.3 copy-start.4
  22.1 100.5 %copy-start.9 = (f32[4,4352]{1,0:T(4,128)S(1)}, f32[4,4352]{1,0:T(4,128)}, u32[]{:S(2)}) copy-start(f32[4,4352]{1,0:T(4,128)} %param.16) | copy-start | bytes 208900
  202.5 231.7 %reduce-scatter.5.cloned.1.call-start = ((), (), s32[]{:S(2)}) async-start(), calls=%async_computation.3 | async-start | bytes 5242880 | tf_op jit(solution)/shard_map/reduce_scatter | solution.py:1858
  290.3 0.7 copy-start.7
  290.3 2.1 copy-start.3
  294.8 140.8 %copy-start.1 = (bf16[1,2,128,2048]{3,2,1,0:T(8,128)(2,1)S(1)}, bf16[1,2,128,2048]{3,2,1,0:T(8,128)(2,1)}, u32[]{:S(2)}) copy-start(bf16[1,2,128,2048]{3,2,1,0:T(8,128)(2,1)} %param.12) | copy-start | bytes 3145732
  294.8 140.8 %copy-start.8 = (f32[2048]{0:T(1024)S(1)}, f32[2048]{0:T(1024)}, u32[]{:S(2)}) copy-start(f32[2048]{0:T(1024)} %param.14) | copy-start | bytes 24580
  434.2 3.0 copy-start.16
  438.5 3.1 copy-start.11
  438.5 3.7 copy-start.2
  438.6 3.7 copy-start.14
  438.6 3.7 copy-start.17
  442.3 3.9 copy-start.10
  442.3 4.6 %copy-start.12 = (f32[1,4096]{1,0:T(1,128)S(1)}, f32[1,4096]{1,0:T(1,128)}, u32[]{:S(2)}) copy-start(f32[1,4096]{1,0:T(1,128)} %get-tuple-element.71) | copy-start | bytes 49156
  442.3 5.2 %copy-start.5 = (f32[1024,256]{1,0:T(8,128)S(1)}, f32[1024,256]{1,0:T(8,128)}, u32[]{:S(2)}) copy-start(f32[1024,256]{1,0:T(8,128)} %get-tuple-element.123) | copy-start | bytes 3145732
Sparse Core Ops, SparseCore 0:
  202.6 80.5 reduce-scatter.2
  290.4 105.5 reduce-scatter.4

commit v6 on v5

--- a/solution.py
+++ b/solution.py
@@ -607,10 +607,12 @@
     weight_ref,
     out_weight_ref,
     g_ref,
-    table_ref,
-    heads_ref,
-    expand_ref,
-    tri_ref,
+    conv_weight_ref,
+    conv_bias_ref,
+    gate_gain_ref,
+    skip_ref,
+    step_bias_ref,
+    decay_ref,
     proj_ref,
     gg_ref,
     branch_ref,
@@ -621,10 +623,14 @@
     taps_ref,
     cols_ref,
     head_ref,
+    expand_ref,
+    gather_ref,
+    tri_ref,
     g_out,
     come_ref,
     ext,
     state,
+    table,
     *sems,
 ):
     chunk, chunks = pl.program_id(0), pl.num_programs(0)
@@ -654,22 +660,47 @@
         ext[:, :8, :] = jnp.zeros((micros, 8, conv_width), F32)
         state[...] = jnp.zeros_like(state)
         me = lax.axis_index("seq")
-        local = pltpu.roll(
-            table_ref[:, :INNER], lax.rem(INNER - me * width, jnp.int32(INNER)), 1
-        )[:, :width]
-        taps_ref[:, : 2 * STATE] = table_ref[:, INNER:]
-        taps_ref[:, 2 * STATE :] = local
+        lane_of = lax.broadcasted_iota(jnp.int32, (LANES, width), 0)
+        head_of = lax.broadcasted_iota(jnp.int32, (LANES, width), 1) // HEAD_DIM
+        spread = (lane_of == head_of).astype(F32).astype(BF16)
+        expand_ref[:LANES] = spread
+        expand_ref[LANES:] = spread
+        lane_of = lax.broadcasted_iota(jnp.int32, (width, LANES), 1)
+        head_of = lax.broadcasted_iota(jnp.int32, (width, LANES), 0) // HEAD_DIM
+        folded = (lane_of == head_of).astype(F32).astype(BF16)
+        gather_ref[:width] = folded
+        gather_ref[width:] = folded
+        later = lax.broadcasted_iota(jnp.int32, (rows, rows), 0)
+        sooner = lax.broadcasted_iota(jnp.int32, (rows, rows), 1)
+        tri_ref[...] = (later >= sooner).astype(F32).astype(BF16)
+
+        table[...] = jnp.zeros_like(table)
+        table[0:TAPS] = conv_weight_ref[:, :INNER]
+        table[TAPS : TAPS + 1] = conv_bias_ref[:, :INNER]
+        table[TAPS + 1 : TAPS + 2] = gate_gain_ref[...]
+        local = pltpu.roll(table[...], lax.rem(INNER - me * width, jnp.int32(INNER)), 1)[
+            :, :width
+        ]
+        taps_ref[...] = jnp.zeros_like(taps_ref)
+        taps_ref[0:TAPS, : 2 * STATE] = conv_weight_ref[:, INNER:]
+        taps_ref[TAPS : TAPS + 1, : 2 * STATE] = conv_bias_ref[:, INNER:]
+        taps_ref[0 : TAPS + 1, 2 * STATE :] = local[: TAPS + 1]
+        head_ref[...] = jnp.zeros_like(head_ref)
+        head_ref[0:1, :HEADS] = step_bias_ref[...]
+        head_ref[1:2, :HEADS] = -jnp.exp(decay_ref[...])
+        head_ref[2:3, :HEADS] = skip_ref[...]
+        own_heads = pltpu.roll(
+            head_ref[...], lax.rem(LANES - me * heads, jnp.int32(LANES)), 1
+        )
+        head_ref[...] = own_heads
         head_row = me * heads + (
             lax.broadcasted_iota(jnp.int32, (1, width), 1) // HEAD_DIM
         )
         limit = HEADS // 8 * jnp.left_shift(jnp.int32(1), lax.axis_index("width"))
-        cols_ref[0:1] = local[6:7]
-        cols_ref[1:2] = local[5:6]
+        cols_ref[0:1] = mm(halves(own_heads, 1), expand_ref[...])[2:3]
+        cols_ref[1:2] = local[TAPS + 1 : TAPS + 2]
         cols_ref[2:3] = (head_row < limit).astype(F32)
         cols_ref[3:8] = jnp.zeros((5, width), F32)
-        head_ref[...] = pltpu.roll(
-            heads_ref[...], lax.rem(LANES - me * heads, jnp.int32(LANES)), 1
-        )
 
     skip, gain, mask = cols_ref[0:1], cols_ref[1:2], cols_ref[2:3]
     rows_in = x_ref[...].reshape(micros * rows, x_ref.shape[2])
@@ -1038,7 +1069,7 @@
 
 
 def run_forward(
-    heads, starts, x, weight, out_weight, g, table, head_table, expand, tri, collective_id
+    heads, starts, x, weight, out_weight, g, smalls, collective_id
 ):
     micros, rows, model_width = g.shape
     chunks = x.shape[1] // rows
@@ -1065,11 +1096,8 @@
             whole(weight),
             whole(out_weight),
             ANY,
-            whole(table),
-            whole(head_table),
-            whole(expand),
-            whole(tri),
-        ],
+        ]
+        + [whole(item) for item in smalls],
         out_specs=[
             row_block(columns),
             row_block(width),
@@ -1081,6 +1109,9 @@
             constant((8, conv_width)),
             constant((8, width)),
             constant((8, LANES)),
+            constant((2 * LANES, width)),
+            constant((2 * width, LANES)),
+            constant((rows, rows)),
             ANY,
             ANY,
         ],
@@ -1095,12 +1126,16 @@
             jax.ShapeDtypeStruct((8, conv_width), F32),
             jax.ShapeDtypeStruct((8, width), F32),
             jax.ShapeDtypeStruct((8, LANES), F32),
+            jax.ShapeDtypeStruct((2 * LANES, width), BF16),
+            jax.ShapeDtypeStruct((2 * width, LANES), BF16),
+            jax.ShapeDtypeStruct((rows, rows), BF16),
             jax.ShapeDtypeStruct((micros, chunks * rows, model_width), BF16),
             jax.ShapeDtypeStruct((chunks // 2, block, model_width), BF16),
         ],
         scratch_shapes=[
             pltpu.VMEM((micros, rows + 8, conv_width), F32),
             pltpu.VMEM((micros, STATE, width), F32),
+            pltpu.VMEM((8, INNER), F32),
         ]
         + line_sems(chunks // 2, micros)
         + pair_scratch(chunks // 2, block, model_width),
@@ -1111,7 +1146,7 @@
             flops=60 * 10**9, bytes_accessed=150 * 10**6, transcendentals=0
         ),
         name="mixer_forward",
-    )(starts, x, weight, out_weight, g, table, head_table, expand, tri)
+    )(starts, x, weight, out_weight, g, *smalls)
 
 
 def run_cross(g, out_weight, gg, sums, collective_id):
@@ -1224,19 +1259,6 @@
         ),
         name="mixer_backward",
     )(starts, active, proj, dnorm, mixed, states, tails, sums, weight, *shared)
-
-
-def tables(heads, rows):
-    width = heads * HEAD_DIM
-    expand = (
-        jnp.arange(LANES)[:, None] == jnp.arange(width)[None, :] // HEAD_DIM
-    ).astype(BF16)
-    tri = (jnp.arange(rows)[:, None] >= jnp.arange(rows)[None, :]).astype(BF16)
-    return (
-        jnp.concatenate([expand, expand], axis=0),
-        jnp.concatenate([expand.T, expand.T], axis=0),
-        tri,
-    )
 
 
 def gather_kernel(
@@ -1549,6 +1571,34 @@
     for turn in range(tiles - LAST, tiles):
         rows_in.each(turn, combine)
 
+    for turn in range(1, width_total):
+        small_hop(turn, True).wait_recv()
+        small_hop(turn, False).wait_send()
+    total = small_slots[0]
+    for group in range(1, width_total):
+        total = total + small_slots[group]
+    small_stage[...] = total
+
+    def last_hop(turn, from_peer):
+        peer = lax.rem(me + turn, seq_total)
+        owner = peer if from_peer else me
+        return remote(
+            small_stage,
+            small_out.at[owner],
+            last_send.at[peer],
+            last_receive.at[owner],
+            {"seq": peer},
+        )
+
+    def last_start(turn, carry):
+        last_hop(turn, False).start()
+        return carry
+
+    lax.fori_loop(1, seq_total, last_start, 0)
+    small_out[me] = small_stage[...]
+
+    out_grad.finish(shard_out_ref)
+
     def bc_arrive(turn, carry):
         source = lax.rem(me + turn, seq_total)
         both(
@@ -1574,71 +1624,6 @@
         bc_total[:, at : at + heads] = bc_ref[source, :, 2 * STATE : 2 * STATE + heads]
     bc_home(mine, "start")
 
-    for turn in range(1, width_total):
-        small_hop(turn, True).wait_recv()
-        small_hop(turn, False).wait_send()
-    total = small_slots[0]
-    for group in range(1, width_total):
-        total = total + small_slots[group]
-    small_stage[...] = total
-
-    def last_hop(turn, from_peer):
-        peer = lax.rem(me + turn, seq_total)
-        owner = peer if from_peer else me
-        return remote(
-            small_stage,
-            small_out.at[owner],
-            last_send.at[peer],
-            last_receive.at[owner],
-            {"seq": peer},
-        )
-
-    def last_start(turn, carry):
-        last_hop(turn, False).start()
-        return carry
-
-    lax.fori_loop(1, seq_total, last_start, 0)
-    small_out[me] = small_stage[...]
-
-    def sent(block, carry):
-        meeting.sent(block)
-        pieces_of(block, "send")
-        return carry
-
-    lax.fori_loop(0, seq_total, sent, 0)
-
-    first = (mine * shard) // width
-
-    def landed(slot, carry):
-        number = first + slot
-        source = lax.rem(number, seq_total)
-
-        @pl.when((number < 2 * seq_total) & (number * width < (mine + 1) * shard))
-        def _():
-            for group in range(width_total):
-                both(
-                    (source == me) & (mine == group),
-                    sum_z.at[me],
-                    zx_ref.at[slot, group],
-                    zx_send.at[0, me],
-                    zx_receive.at[slot, group],
-                    {"width": group, "seq": source},
-                    "receive",
-                )
-
-        return carry
-
-    lax.fori_loop(0, slots, landed, 0)
-
-    bc_home(mine, "send")
-
-    @pl.when(mine == width_total - 1)
-    def _():
-        for source in range(width_total):
-            bc_home(source, "receive")
-
-    out_grad.finish(shard_out_ref)
-
     def last_end(turn, carry):
         last_hop(turn, False).wait_send()
         last_hop(turn, True).wait_recv()
@@ -1646,23 +1631,6 @@
 
     lax.fori_loop(1, seq_total, last_end, 0)
 
-    edge = (slots - -(-(2 * STATE + HEADS) // width)) * width
-    for group in range(width_total):
-        for slot in range(slots):
-            line_buffer[:, slot * width : (slot + 1) * width] = zx_ref[slot, group].astype(F32)
-
-        @pl.when(mine == width_total - 1)
-        def _():
-            line_buffer[:, edge : edge + 2 * STATE + HEADS] = bc_last[
-                group, :, : 2 * STATE + HEADS
-            ].astype(F32)
-
-        total_lanes = line_buffer.shape[1]
-        start = lax.rem(mine * shard, jnp.int32(width))
-        rolled = pltpu.roll(
-            line_buffer[...], lax.rem(total_lanes - start, jnp.int32(total_lanes)), 1
-        )
-        shard_in_ref[group * quarter : (group + 1) * quarter, :] = rolled[:, :shard]
     def small_add(source, total):
         return total + small_out[source]
 
@@ -1680,6 +1648,60 @@
         head_out[:, source * heads : (source + 1) * heads] = small_out[
             source, :, conv_end : conv_end + heads
         ]
+
+    first = (mine * shard) // width
+
+    def landed(slot, carry):
+        number = first + slot
+        source = lax.rem(number, seq_total)
+
+        @pl.when((number < 2 * seq_total) & (number * width < (mine + 1) * shard))
+        def _():
+            for group in range(width_total):
+                both(
+                    (source == me) & (mine == group),
+                    sum_z.at[me],
+                    zx_ref.at[slot, group],
+                    zx_send.at[0, me],
+                    zx_receive.at[slot, group],
+                    {"width": group, "seq": source},
+                    "receive",
+                )
+
+        return carry
+
+    lax.fori_loop(0, slots, landed, 0)
+
+    @pl.when(mine == width_total - 1)
+    def _():
+        for source in range(width_total):
+            bc_home(source, "receive")
+
+    edge = (slots - -(-(2 * STATE + HEADS) // width)) * width
+    for group in range(width_total):
+        for slot in range(slots):
+            line_buffer[:, slot * width : (slot + 1) * width] = zx_ref[slot, group].astype(F32)
+
+        @pl.when(mine == width_total - 1)
+        def _():
+            line_buffer[:, edge : edge + 2 * STATE + HEADS] = bc_last[
+                group, :, : 2 * STATE + HEADS
+            ].astype(F32)
+
+        total_lanes = line_buffer.shape[1]
+        start = lax.rem(mine * shard, jnp.int32(width))
+        rolled = pltpu.roll(
+            line_buffer[...], lax.rem(total_lanes - start, jnp.int32(total_lanes)), 1
+        )
+        shard_in_ref[group * quarter : (group + 1) * quarter, :] = rolled[:, :shard].astype(BF16)
+
+    def sent(block, carry):
+        meeting.sent(block)
+        pieces_of(block, "send")
+        return carry
+
+    lax.fori_loop(0, seq_total, sent, 0)
+    bc_home(mine, "send")
 
 
 def bring_home(normed, dproj, columns, smalls, in_gain, grad, gnorm, heads, collective_id):
@@ -1705,7 +1727,7 @@
         in_specs=[ANY] + [vmem] * 6 + [ANY, vmem],
         out_specs=[vmem] * 7,
         out_shape=[
-            jax.ShapeDtypeStruct((depth, shard), F32),
+            jax.ShapeDtypeStruct((depth, shard), BF16),
             jax.ShapeDtypeStruct((seq_total // width_total * width, model_width // seq_total), F32),
             jax.ShapeDtypeStruct((TAPS, CONV), F32),
             jax.ShapeDtypeStruct((1, CONV), F32),
@@ -1801,37 +1823,19 @@
     pieces = jnp.concatenate([bc, xs, gates, dts], axis=2).transpose(1, 0, 2)
     all_normed, columns = gather_rows(normed, pieces, 0)
 
-    def lane_pad(value):
-        return jnp.pad(value, (0, CONV - INNER))[None]
-
-    table = jnp.concatenate(
-        [
-            conv_weight,
-            conv_bias[None],
-            lane_pad(gate_gain),
-            lane_pad(jnp.repeat(skip_gain, HEAD_DIM)),
-            jnp.zeros((1, CONV), F32),
-        ],
-        axis=0,
+    smalls = [
+        conv_weight,
+        conv_bias[None],
+        gate_gain[None],
+        skip_gain[None],
+        step_bias[None],
+        decay_log[None],
+    ]
+    forward = run_forward(
+        heads, starts[0], all_normed, columns, out_weight, grads, smalls, 3
     )
-    head_table = jnp.pad(
-        jnp.stack([step_bias, -jnp.exp(decay_log)]), ((0, 6), (0, LANES - HEADS))
-    )
-    expand, gather, tri = tables(heads, rows)
-
-    proj, gg, branch, mixed, states, tails, sums, taps, cols, head, all_grad, _ = run_forward(
-        heads,
-        starts[0],
-        all_normed,
-        columns,
-        out_weight,
-        grads,
-        table,
-        head_table,
-        expand,
-        tri,
-        3,
-    )
+    proj, gg, branch, mixed, states, tails, sums = forward[:7]
+    taps, cols, head, expand, gather, tri, all_grad = forward[7:14]
     chip_wise = dict(axis_index_groups=chip_groups(seq_total), scatter_dimension=0, tiled=True)
     branch = lax.psum_scatter(branch, "seq", **chip_wise)
     dnorm, sums = run_cross(all_grad, out_weight, gg, sums, 1)
@@ -1879,7 +1883,7 @@
         output.astype(BF16).reshape(shape),
         hidden_grads.astype(BF16).reshape(shape),
         in_gain_sum.reshape(-1),
-        shard_in,
+        shard_in.astype(F32),
         taps_sum,
         bias_sum[0],
         head_sums[1],

time: 456 us -> 450 us (0.987)
  no operation moved by 1% of the time
where the time goes in v6:
time: 450 us; the launch traced here: 449 us
  Pallas kernels  404 us (90%)
  local copies, waits for them, and re-layouts  17.7 us (4%)
  between operations  14.3 us (3%)
  other arithmetic  12.1 us (3%)
    pallas_call x1, Pallas kernels, bring_home(): pl.pallas_call(partial(home_kernel, layout), in_specs=[ANY] + [vmem] * 6...  137 us
    pallas_call x1, Pallas kernels, gather_rows(): pl.pallas_call(gather_kernel, in_specs=[ANY] * 2, out_specs=[ANY] * 2, ou...  100 us
    pallas_call x1, Pallas kernels, run_forward(): pl.pallas_call(partial(forward_kernel, micros, heads), grid=(chunks,), in...  79.3 us
    pallas_call x1, Pallas kernels, run_backward(): pl.pallas_call(partial(backward_kernel, micros, heads), grid=(chunks,), i...  63.7 us
    pallas_call x1, Pallas kernels, run_cross(): pl.pallas_call(cross_kernel, grid=(chunks,), in_specs=[row_block(model_wi...  23.6 us
  transfers between devices with their start and end apart: 2, of which 0 were waited for; matrix products, arithmetic and copies ran while one was open for 1% of the time, Pallas kernels for 50%

profile of v6, /device:TPU:0, one launch (start us, length us, event | category | flops | bytes accessed | tf_op | source)
XLA Modules:
  0.0 448.7 jit_solution(7799496196227900371)
XLA Ops:
  7.2 0.0 reduce-scatter.3.cloned.1.call-start
  7.2 1.5 fusion.6
  8.8 0.6 copy-done.14
  9.3 1.4 broadcast_in_dim.30.conv_bias_ref
  10.7 0.8 dynamic-slice_bitcast_fusion
  11.5 0.9 dynamic-slice
  12.4 0.1 copy.25
  12.5 0.1 copy.28
  12.6 2.3 fusion.12
  14.9 0.0 copy-start
  14.9 0.0 copy-start.6
  14.9 1.1 copy.29
  16.0 0.3 copy.30
  16.4 1.3 fusion.8.x_ref
  17.7 0.0 copy-done.4
  17.7 1.2 fusion.10.w_ref
  18.9 100.5 %gather_rows.1 = (bf16[2,1024,2048]{2,1,0:T(8,128)(2,1)}, bf16[2048,1408]{1,0:T(8,128)(2,1)}) custom-call(bf16[2,128,2048]{2,1,0:T(8,128)(2,1)} %fusion.8.x_ref, bf16[8,64,1408]{2,1,0:T(8,128)(2,1)} %fusion.10.w_ref), custom_call_target="tpu_custom_call" | custom-call | flops 80000000000 | bytes 200000000 | tf_op jit(solution)/shard_map/gather_rows/pallas_call | solution.py:1350
  119.4 79.3 %mixer_forward.1 = (bf16[2,1024,1408]{2,1,0:T(8,128)(2,1)}, bf16[2,1024,512]{2,1,0:T(8,128)(2,1)}, bf16[4,256,2048]{2,1,0:T(8,128)(2,1)}, f32[2,1024,512]{2,1,0:...) custom-call(s32[2,4]{1,0:T(2,128)} %bitcast.56, ...), custom_call_target="tpu_custom_call" | custom-call | flops 60000002048 | bytes 150000000 | tf_op jit(solution)/shard_map/mixer_forward/pallas_call | solution.py:1090
  198.8 0.0 reduce-scatter.3.cloned.1.call-update
  198.8 0.2 reduce-scatter.5.cloned.1.call-start
  199.0 23.6 %cross_sums.1 = (f32[2,1024,512]{2,1,0:T(8,128)}, f32[8,8,128]{2,1,0:T(8,128)}) custom-call(bf16[2,1024,2048]{2,1,0:T(8,128)(2,1)} %get-tuple-element.48.g_ref.grad_ref, bf16[512,2048]{1,0:T(8,128)(2,1)} %out_weight_ref.3, bf16[2,1024,512]{2,1,0:T(8,128)(2,1)} %get-tuple-element.49.gg_ref, f32[8,8,128]{2,1,0:T(8,128)} %get-tuple-element.50.sums_ref), custom_call_target="tpu_custom_call" | custom-call | flops 12000000000 | bytes 16000000 | tf_op jit(solution)/shard_map/cross_sums/pallas_call | solution.py:1160
  222.6 63.7 %mixer_backward.1 = (bf16[2,1024,1408]{2,1,0:T(8,128)(2,1)}, bf16[4,256,2048]{2,1,0:T(8,128)(2,1)}, f32[8,768]{1,0:T(8,128)}, f32[8,512]{1,0:T(8,128)}, f32[8,128]{1,0:T(8,128)}, /*index=5*/bf16[4,256,2048]{2,1,0:T(8,128)(2,1)}) custom-call(s32[2,4]{1,0:T(2,128)} %bitcast.57, f32[1]{0:T(128)} %bitcast.1.active_ref, ...), custom_call_target="tpu_custom_call" | custom-call | flops 60000002048 | bytes 60000000 | tf_op jit(solution)/shard_map/mixer_backward/pallas_call | solution.py:1217
  286.4 0.0 copy-start.7
  286.4 0.0 reduce-scatter.5.cloned.1.call-update
  286.4 0.7 copy-done.7
  287.1 0.6 reshape.123.in_gain_ref
  287.7 0.8 slice.28
  288.5 1.8 multiply_convert_fusion.gnorm_ref
  290.3 0.6 dynamic-slice_bitcast_fusion.1
  290.9 137.2 %bring_home.1 = (bf16[256,2128]{1,0:T(8,128)(2,1)}, f32[1024,256]{1,0:T(8,128)}, f32[4,4352]{1,0:T(4,128)}, f32[1,4352]{1,0:T(1,128)}, f32[1,4096]{1,0:T(1,128)}, /*index=5*/f32[8,64]{1,0:T(8,128)}, f32[8,256]{1,0:T(8,128)}) custom-call(bf16[2,1024,2048]{2,1,0:T(8,128)(2,1)} %get-tuple-element.45.x_ref.normed_ref, ...), custom_call_target="tpu_custom_call" | custom-call | flops 149999992832 | bytes 33554432 | tf_op jit(solution)/shard_map/bring_home/pallas_call | solution.py:1725
  428.1 0.0 copy-start.15
  428.1 0.0 reduce-scatter.5.cloned.1.call-done
  428.2 1.3 copy.36
  429.5 0.0 copy-done.8
  429.5 1.6 fusion.3
  431.1 0.0 copy-done.15
  431.1 0.0 copy-start.10
  431.1 0.0 copy-start.2
  431.1 0.0 copy-start.13
  431.1 0.0 copy-start.16
  431.2 1.3 slice_bitcast_fusion
  432.5 2.6 copy.31
  435.1 0.0 copy-done.10
  435.1 0.7 reduce.1
  435.8 3.9 fusion.5
  439.7 0.6 copy.40
  440.3 0.6 copy.41
  440.9 1.0 copy.42
  (26 shorter events, 0.1 us)
Async XLA Ops:
  7.2 283.7 %reduce-scatter.3.cloned.1.call-start = ((), (), s32[]{:S(2)}) async-start(), calls=%async_computation.2 | async-start | bytes 5242880 | tf_op jit(solution)/shard_map/reduce_scatter | solution.py:1840
  8.7 0.6 copy-start.14
  9.3 7.1 %copy-start.12 = (f32[2,128]{1,0:T(2,128)}, f32[2,128]{1,0:T(2,128)S(1)}, u32[]{:S(2)}) copy-start(f32[2,128]{1,0:T(2,128)S(1)} %add_rsqrt_fusion.1) | copy-start | bytes 3076
  14.9 1.5 copy-start
  14.9 1.5 copy-start.6
  16.0 1.7 copy-start.4
  198.8 229.4 %reduce-scatter.5.cloned.1.call-start = ((), (), s32[]{:S(2)}) async-start(), calls=%async_computation.3 | async-start | bytes 5242880 | tf_op jit(solution)/shard_map/reduce_scatter | solution.py:1862
  286.4 0.7 copy-start.7
  286.4 2.1 copy-start.3
  290.9 138.6 %copy-start.1 = (bf16[1,2,128,2048]{3,2,1,0:T(8,128)(2,1)S(1)}, bf16[1,2,128,2048]{3,2,1,0:T(8,128)(2,1)}, u32[]{:S(2)}) copy-start(bf16[1,2,128,2048]{3,2,1,0:T(8,128)(2,1)} %param.12) | copy-start | bytes 3145732
  290.9 138.6 %copy-start.8 = (f32[2048]{0:T(1024)S(1)}, f32[2048]{0:T(1024)}, u32[]{:S(2)}) copy-start(f32[2048]{0:T(1024)} %param.14) | copy-start | bytes 24580
  428.1 3.0 copy-start.15
  431.1 4.0 copy-start.10
  431.1 4.6 %copy-start.2 = (bf16[1,256,2048]{2,1,0:T(8,128)(2,1)S(1)}, bf16[1,256,2048]{2,1,0:T(8,128)(2,1)}, u32[]{:S(2)}) copy-start(bf16[1,256,2048]{2,1,0:T(8,128)(2,1)} %reduce-scatter.5.cloned.1.call-done) | copy-start | bytes 3145732
  431.1 4.6 %copy-start.13 = (f32[2,128]{1,0:T(2,128)S(1)}, f32[2,128]{1,0:T(2,128)}, u32[]{:S(2)}) copy-start(f32[2,128]{1,0:T(2,128)} %copy-done.12) | copy-start | bytes 3076
  431.1 4.6 %copy-start.16 = (f32[2,128]{1,0:T(2,128)S(1)}, f32[2,128]{1,0:T(2,128)}, u32[]{:S(2)}) copy-start(f32[2,128]{1,0:T(2,128)} %dynamic-slice_bitcast_fusion.1) | copy-start | bytes 3076
  435.7 3.9 copy-start.9
  435.7 4.6 %copy-start.11 = (f32[1,4096]{1,0:T(1,128)S(1)}, f32[1,4096]{1,0:T(1,128)}, u32[]{:S(2)}) copy-start(f32[1,4096]{1,0:T(1,128)} %get-tuple-element.77) | copy-start | bytes 49156
  435.8 5.2 %copy-start.5 = (f32[1024,256]{1,0:T(8,128)S(1)}, f32[1024,256]{1,0:T(8,128)}, u32[]{:S(2)}) copy-start(f32[1024,256]{1,0:T(8,128)} %get-tuple-element.129) | copy-start | bytes 3145732
Sparse Core Ops, SparseCore 0:
  198.9 80.5 reduce-scatter.2
  286.5 105.0 reduce-scatter.4

commit v7 on v6

--- a/solution.py
+++ b/solution.py
@@ -63,7 +63,12 @@
 ANY = pl.BlockSpec(memory_space=pl.ANY)
 
 
-def greet(axes):
+def hear(axes):
+    waits = sum(lax.axis_size(axis) - 1 for axis in axes)
+    pl.semaphore_wait(pltpu.get_barrier_semaphore(), waits)
+
+
+def greet(axes, hear=True):
     barrier = pltpu.get_barrier_semaphore()
     waits = 0
     for axis in axes:
@@ -80,7 +85,8 @@
 
         lax.fori_loop(1, count, hello, 0)
         waits += count - 1
-    pl.semaphore_wait(barrier, waits)
+    if hear:
+        pl.semaphore_wait(barrier, waits)
 
 
 def remote(source, target, send, receive, device):
@@ -212,7 +218,7 @@
 LAST = 4
 
 
-def greet_all():
+def call_all():
     seq_total, width_total = lax.axis_size("seq"), lax.axis_size("width")
     count = seq_total * width_total
     place = lax.axis_index("width") * seq_total + lax.axis_index("seq")
@@ -229,7 +235,11 @@
         return carry
 
     lax.fori_loop(1, count, hello, 0)
-    pl.semaphore_wait(barrier, count - 1)
+
+
+def hear_all():
+    count = lax.axis_size("seq") * lax.axis_size("width")
+    pl.semaphore_wait(pltpu.get_barrier_semaphore(), count - 1)
 
 
 def both(is_here, source, target, send, receive, device, action):
@@ -406,6 +416,7 @@
             part = mm_tn(self.gnorm[micro, rows, :], block)
             self.acc[...] = part if chunk == 0 else self.acc[...] + part
             self.tiles.used(turn, chunk)
+        pl.when(turn == 0)(hear_all)
         for item in range(self.tiles.per_tile):
             block = self.tiles.turned(turn) * self.tiles.per_tile + item
             for group in range(self.width_total):
@@ -777,7 +788,7 @@
 
     @pl.when(chunk == 0)
     def _():
-        greet(("seq",))
+        greet(("seq",), hear=False)
 
     grads = g_ref[...].reshape(micros * rows, model_width)
     dnorm = mm_nt(grads, out_weight_ref[...])
@@ -796,6 +807,8 @@
 
     @pl.when(chunk == chunks - 1)
     def _():
+        hear(("seq",))
+
         def copy(turn, owner):
             peer = lax.rem(me + turn, chunks)
             return remote(
@@ -866,7 +879,6 @@
         pl.semaphore_signal(
             barrier, inc=1, device_id={"seq": pairs.sibling}, device_id_type=MESH
         )
-        pl.semaphore_wait(barrier, 1)
 
     position = chunks - 1 - step_index
 
@@ -903,6 +915,10 @@
         )
     d_rows = dproj_ref[...].reshape(micros * rows, dproj_ref.shape[2])
     partial_rows = mm_nt(d_rows, weight_ref[...]).astype(BF16)
+
+    @pl.when(step_index == 0)
+    def _():
+        pl.semaphore_wait(pltpu.get_barrier_semaphore(), 1)
 
     @pl.when((lax.rem(position, 2) == 1) & (step_index >= 2))
     def _():
@@ -1432,7 +1448,7 @@
     meeting = Meeting(stage, arrived, last_arrived, in_sems)
     out_grad = OutGrad(grad_ref, gnorm_ref, out_refs)
     out_grad.tiles.begin()
-    greet_all()
+    call_all()
 
     def out_multiply(turn, carry):
         out_grad.multiply(turn)

time: 450 us -> 443 us (0.984)
  Pallas kernels: 404 us -> 398 us
  transfers between devices with their start and end apart: 2 -> 2, of which waited for: 0 -> 0; matrix products, arithmetic and copies ran while one was open for 1% -> 1% of each run, Pallas kernels for 50% -> 49%
where the time goes in v7:
time: 443 us
  Pallas kernels  398 us (90%)
  local copies, waits for them, and re-layouts  17.7 us (4%)
  between operations  14.3 us (3%)
  other arithmetic  12.1 us (3%)
    pallas_call x1, Pallas kernels, bring_home(): pl.pallas_call(partial(home_kernel, layout), in_specs=[ANY] + [vmem] * 6...  135 us
    pallas_call x1, Pallas kernels, gather_rows(): pl.pallas_call(gather_kernel, in_specs=[ANY] * 2, out_specs=[ANY] * 2, ou...  100 us
    pallas_call x1, Pallas kernels, run_forward(): pl.pallas_call(partial(forward_kernel, micros, heads), grid=(chunks,), in...  79.3 us
    pallas_call x1, Pallas kernels, run_backward(): pl.pallas_call(partial(backward_kernel, micros, heads), grid=(chunks,), i...  62.1 us
    pallas_call x1, Pallas kernels, run_cross(): pl.pallas_call(cross_kernel, grid=(chunks,), in_specs=[row_block(model_wi...  21.3 us
  transfers between devices with their start and end apart: 2, of which 0 were waited for; matrix products, arithmetic and copies ran while one was open for 1% of the time, Pallas kernels for 49%

profile of v7, /device:TPU:0, one launch (start us, length us, event | category | flops | bytes accessed | tf_op | source)
XLA Modules:
  0.0 442.6 jit_solution(8548459410292160219)
XLA Ops:
  7.2 0.0 reduce-scatter.3.cloned.1.call-start
  7.2 1.5 fusion.6
  8.8 0.6 copy-done.14
  9.3 1.4 broadcast_in_dim.30.conv_bias_ref
  10.7 0.8 dynamic-slice_bitcast_fusion
  11.5 0.9 dynamic-slice
  12.4 0.1 copy.25
  12.5 0.1 copy.28
  12.6 2.3 fusion.12
  14.9 0.0 copy-start
  14.9 0.0 copy-start.6
  14.9 1.1 copy.29
  16.0 0.3 copy.30
  16.4 0.0 copy-done.12
  16.4 0.0 copy-done
  16.4 0.0 copy-done.6
  16.4 1.3 fusion.8.x_ref
  17.7 1.2 fusion.10.w_ref
  18.9 100.5 %gather_rows.1 = (bf16[2,1024,2048]{2,1,0:T(8,128)(2,1)}, bf16[2048,1408]{1,0:T(8,128)(2,1)}) custom-call(bf16[2,128,2048]{2,1,0:T(8,128)(2,1)} %fusion.8.x_ref, bf16[8,64,1408]{2,1,0:T(8,128)(2,1)} %fusion.10.w_ref), custom_call_target="tpu_custom_call" | custom-call | flops 80000000000 | bytes 200000000 | tf_op jit(solution)/shard_map/gather_rows/pallas_call | solution.py:1366
  119.4 79.3 %mixer_forward.1 = (bf16[2,1024,1408]{2,1,0:T(8,128)(2,1)}, bf16[2,1024,512]{2,1,0:T(8,128)(2,1)}, bf16[4,256,2048]{2,1,0:T(8,128)(2,1)}, f32[2,1024,512]{2,1,0:...) custom-call(s32[2,4]{1,0:T(2,128)} %bitcast.56, ...), custom_call_target="tpu_custom_call" | custom-call | flops 60000002048 | bytes 150000000 | tf_op jit(solution)/shard_map/mixer_forward/pallas_call | solution.py:1106
  198.8 0.0 reduce-scatter.3.cloned.1.call-update
  198.8 0.2 reduce-scatter.5.cloned.1.call-start
  199.0 21.3 %cross_sums.1 = (f32[2,1024,512]{2,1,0:T(8,128)}, f32[8,8,128]{2,1,0:T(8,128)}) custom-call(bf16[2,1024,2048]{2,1,0:T(8,128)(2,1)} %get-tuple-element.48.g_ref.grad_ref, bf16[512,2048]{1,0:T(8,128)(2,1)} %out_weight_ref.3, bf16[2,1024,512]{2,1,0:T(8,128)(2,1)} %get-tuple-element.49.gg_ref, f32[8,8,128]{2,1,0:T(8,128)} %get-tuple-element.50.sums_ref), custom_call_target="tpu_custom_call" | custom-call | flops 12000000000 | bytes 16000000 | tf_op jit(solution)/shard_map/cross_sums/pallas_call | solution.py:1176
  220.4 62.1 %mixer_backward.1 = (bf16[2,1024,1408]{2,1,0:T(8,128)(2,1)}, bf16[4,256,2048]{2,1,0:T(8,128)(2,1)}, f32[8,768]{1,0:T(8,128)}, f32[8,512]{1,0:T(8,128)}, f32[8,128]{1,0:T(8,128)}, /*index=5*/bf16[4,256,2048]{2,1,0:T(8,128)(2,1)}) custom-call(s32[2,4]{1,0:T(2,128)} %bitcast.57, f32[1]{0:T(128)} %bitcast.1.active_ref, ...), custom_call_target="tpu_custom_call" | custom-call | flops 60000002048 | bytes 60000000 | tf_op jit(solution)/shard_map/mixer_backward/pallas_call | solution.py:1233
  282.5 0.0 copy-start.7
  282.5 0.0 reduce-scatter.5.cloned.1.call-update
  282.5 0.7 copy-done.7
  283.2 0.6 reshape.123.in_gain_ref
  283.8 0.8 slice.28
  284.6 1.8 multiply_convert_fusion.gnorm_ref
  286.4 0.6 dynamic-slice_bitcast_fusion.1
  287.0 135.0 %bring_home.1 = (bf16[256,2128]{1,0:T(8,128)(2,1)}, f32[1024,256]{1,0:T(8,128)}, f32[4,4352]{1,0:T(4,128)}, f32[1,4352]{1,0:T(1,128)}, f32[1,4096]{1,0:T(1,128)}, /*index=5*/f32[8,64]{1,0:T(8,128)}, f32[8,256]{1,0:T(8,128)}) custom-call(bf16[2,1024,2048]{2,1,0:T(8,128)(2,1)} %get-tuple-element.45.x_ref.normed_ref, ...), custom_call_target="tpu_custom_call" | custom-call | flops 149999992832 | bytes 33554432 | tf_op jit(solution)/shard_map/bring_home/pallas_call | solution.py:1741
  422.0 0.0 copy-start.15
  422.0 0.0 reduce-scatter.5.cloned.1.call-done
  422.0 1.3 copy.36
  423.3 0.0 copy-done.1
  423.4 1.6 fusion.3
  425.0 0.0 copy-start.13
  425.0 0.0 copy-start.16
  425.1 1.3 slice_bitcast_fusion
  426.4 2.6 copy.31
  429.0 0.7 reduce.1
  429.6 0.0 copy-done.13
  429.7 3.9 fusion.5
  433.6 0.0 copy-done.9
  433.6 0.6 copy.40
  434.2 0.6 copy.41
  434.8 1.0 copy.42
  (26 shorter events, 0.1 us)
Async XLA Ops:
  7.2 279.8 %reduce-scatter.3.cloned.1.call-start = ((), (), s32[]{:S(2)}) async-start(), calls=%async_computation.2 | async-start | bytes 5242880 | tf_op jit(solution)/shard_map/reduce_scatter | solution.py:1856
  8.7 0.6 copy-start.14
  9.3 7.1 %copy-start.12 = (f32[2,128]{1,0:T(2,128)}, f32[2,128]{1,0:T(2,128)S(1)}, u32[]{:S(2)}) copy-start(f32[2,128]{1,0:T(2,128)S(1)} %add_rsqrt_fusion.1) | copy-start | bytes 3076
  14.9 1.5 copy-start
  14.9 1.5 copy-start.6
  16.0 1.7 copy-start.4
  198.8 223.3 %reduce-scatter.5.cloned.1.call-start = ((), (), s32[]{:S(2)}) async-start(), calls=%async_computation.3 | async-start | bytes 5242880 | tf_op jit(solution)/shard_map/reduce_scatter | solution.py:1878
  282.5 0.7 copy-start.7
  282.5 2.1 copy-start.3
  287.0 136.4 %copy-start.1 = (bf16[1,2,128,2048]{3,2,1,0:T(8,128)(2,1)S(1)}, bf16[1,2,128,2048]{3,2,1,0:T(8,128)(2,1)}, u32[]{:S(2)}) copy-start(bf16[1,2,128,2048]{3,2,1,0:T(8,128)(2,1)} %param.12) | copy-start | bytes 3145732
  287.0 136.4 %copy-start.8 = (f32[2048]{0:T(1024)S(1)}, f32[2048]{0:T(1024)}, u32[]{:S(2)}) copy-start(f32[2048]{0:T(1024)} %param.14) | copy-start | bytes 24580
  422.0 3.0 copy-start.15
  425.0 4.0 copy-start.10
  425.0 4.6 %copy-start.2 = (bf16[1,256,2048]{2,1,0:T(8,128)(2,1)S(1)}, bf16[1,256,2048]{2,1,0:T(8,128)(2,1)}, u32[]{:S(2)}) copy-start(bf16[1,256,2048]{2,1,0:T(8,128)(2,1)} %reduce-scatter.5.cloned.1.call-done) | copy-start | bytes 3145732
  425.0 4.6 %copy-start.13 = (f32[2,128]{1,0:T(2,128)S(1)}, f32[2,128]{1,0:T(2,128)}, u32[]{:S(2)}) copy-start(f32[2,128]{1,0:T(2,128)} %copy-done.12) | copy-start | bytes 3076
  425.0 4.6 %copy-start.16 = (f32[2,128]{1,0:T(2,128)S(1)}, f32[2,128]{1,0:T(2,128)}, u32[]{:S(2)}) copy-start(f32[2,128]{1,0:T(2,128)} %dynamic-slice_bitcast_fusion.1) | copy-start | bytes 3076
  429.6 3.9 copy-start.9
  429.6 4.6 %copy-start.11 = (f32[1,4096]{1,0:T(1,128)S(1)}, f32[1,4096]{1,0:T(1,128)}, u32[]{:S(2)}) copy-start(f32[1,4096]{1,0:T(1,128)} %get-tuple-element.77) | copy-start | bytes 49156
  429.6 5.2 %copy-start.5 = (f32[1024,256]{1,0:T(8,128)S(1)}, f32[1024,256]{1,0:T(8,128)}, u32[]{:S(2)}) copy-start(f32[1024,256]{1,0:T(8,128)} %get-tuple-element.129) | copy-start | bytes 3145732
Sparse Core Ops, SparseCore 0:
  198.9 80.5 reduce-scatter.2
  282.6 104.5 reduce-scatter.4

commit v8 on v7

--- a/solution.py
+++ b/solution.py
@@ -1392,12 +1392,12 @@
 def home_kernel(
     layout,
     normed_ref,
-    columns_ref,
+    columns_far,
     gconv_ref,
     gcols_ref,
     ghead_ref,
     in_gain_ref,
-    dproj_ref,
+    dproj_far,
     grad_ref,
     gnorm_ref,
     shard_in_ref,
@@ -1435,6 +1435,9 @@
     bc_last,
     bc_last_send,
     bc_last_receive,
+    columns_ref,
+    dproj_ref,
+    bring,
     *out_refs,
 ):
     seq_total, width_total, quarter, width, slots, shard, heads = layout
@@ -1448,6 +1451,10 @@
     meeting = Meeting(stage, arrived, last_arrived, in_sems)
     out_grad = OutGrad(grad_ref, gnorm_ref, out_refs)
     out_grad.tiles.begin()
+    dproj_in = pltpu.make_async_copy(dproj_far, dproj_ref, bring.at[0])
+    columns_in = pltpu.make_async_copy(columns_far, columns_ref, bring.at[1])
+    dproj_in.start()
+    columns_in.start()
     call_all()
 
     def out_multiply(turn, carry):
@@ -1465,6 +1472,8 @@
 
     rows_in.begin()
     lax.fori_loop(0, tiles, out_multiply, 0)
+    dproj_in.wait()
+    columns_in.wait()
 
     conv_end = conv_width + width
     small_stage[:, :conv_width] = gconv_ref[...]
@@ -1740,7 +1749,7 @@
     vmem = pl.BlockSpec(memory_space=pltpu.VMEM)
     return pl.pallas_call(
         partial(home_kernel, layout),
-        in_specs=[ANY] + [vmem] * 6 + [ANY, vmem],
+        in_specs=[ANY, ANY] + [vmem] * 4 + [ANY, ANY, vmem],
         out_specs=[vmem] * 7,
         out_shape=[
             jax.ShapeDtypeStruct((depth, shard), BF16),
@@ -1780,6 +1789,9 @@
             pltpu.VMEM((width_total, quarter, rest), BF16),
             dma((1,)),
             dma((width_total,)),
+            pltpu.VMEM(columns.shape, BF16),
+            pltpu.VMEM(dproj.shape, BF16),
+            dma((2,)),
         ]
         + out_grad_scratch(heads, group_rows, model_width),
         compiler_params=pltpu.CompilerParams(

time: 443 us -> 443 us (level)
  no operation moved by 1% of the time
where the time goes in v8:
time: 443 us
  Pallas kernels  398 us (90%)
  local copies, waits for them, and re-layouts  17.7 us (4%)
  between operations  14.3 us (3%)
  other arithmetic  12.1 us (3%)
    pallas_call x1, Pallas kernels, bring_home(): pl.pallas_call(partial(home_kernel, layout), in_specs=[ANY, ANY] + [vmem]...  135 us
    pallas_call x1, Pallas kernels, gather_rows(): pl.pallas_call(gather_kernel, in_specs=[ANY] * 2, out_specs=[ANY] * 2, ou...  100 us
    pallas_call x1, Pallas kernels, run_forward(): pl.pallas_call(partial(forward_kernel, micros, heads), grid=(chunks,), in...  79.3 us
    pallas_call x1, Pallas kernels, run_backward(): pl.pallas_call(partial(backward_kernel, micros, heads), grid=(chunks,), i...  62.1 us
    pallas_call x1, Pallas kernels, run_cross(): pl.pallas_call(cross_kernel, grid=(chunks,), in_specs=[row_block(model_wi...  21.3 us
  transfers between devices with their start and end apart: 2, of which 0 were waited for; matrix products, arithmetic and copies ran while one was open for 1% of the time, Pallas kernels for 49%

profile of v8, /device:TPU:0, one launch (start us, length us, event | category | flops | bytes accessed | tf_op | source)
XLA Modules:
  0.0 442.6 jit_solution(11838864633905691017)
XLA Ops:
  7.2 0.0 reduce-scatter.3.cloned.1.call-start
  7.2 1.5 fusion.6
  8.8 0.6 copy-done.14
  9.3 1.4 broadcast_in_dim.30.conv_bias_ref
  10.7 0.8 dynamic-slice_bitcast_fusion
  11.5 0.9 dynamic-slice
  12.4 0.1 copy.25
  12.5 0.1 copy.28
  12.6 2.3 fusion.12
  14.9 0.0 copy-start
  14.9 0.0 copy-start.6
  14.9 1.1 copy.29
  16.0 0.3 copy.30
  16.4 0.0 copy-done.12
  16.4 0.0 copy-done
  16.4 0.0 copy-done.6
  16.4 1.3 fusion.8.x_ref
  17.7 1.2 fusion.10.w_ref
  18.9 100.5 %gather_rows.1 = (bf16[2,1024,2048]{2,1,0:T(8,128)(2,1)}, bf16[2048,1408]{1,0:T(8,128)(2,1)}) custom-call(bf16[2,128,2048]{2,1,0:T(8,128)(2,1)} %fusion.8.x_ref, bf16[8,64,1408]{2,1,0:T(8,128)(2,1)} %fusion.10.w_ref), custom_call_target="tpu_custom_call" | custom-call | flops 80000000000 | bytes 200000000 | tf_op jit(solution)/shard_map/gather_rows/pallas_call | solution.py:1366
  119.4 79.3 %mixer_forward.1 = (bf16[2,1024,1408]{2,1,0:T(8,128)(2,1)}, bf16[2,1024,512]{2,1,0:T(8,128)(2,1)}, bf16[4,256,2048]{2,1,0:T(8,128)(2,1)}, f32[2,1024,512]{2,1,0:...) custom-call(s32[2,4]{1,0:T(2,128)} %bitcast.56, ...), custom_call_target="tpu_custom_call" | custom-call | flops 60000002048 | bytes 150000000 | tf_op jit(solution)/shard_map/mixer_forward/pallas_call | solution.py:1106
  198.8 0.0 reduce-scatter.3.cloned.1.call-update
  198.8 0.2 reduce-scatter.5.cloned.1.call-start
  199.0 21.3 %cross_sums.1 = (f32[2,1024,512]{2,1,0:T(8,128)}, f32[8,8,128]{2,1,0:T(8,128)}) custom-call(bf16[2,1024,2048]{2,1,0:T(8,128)(2,1)} %get-tuple-element.48.g_ref.grad_ref, bf16[512,2048]{1,0:T(8,128)(2,1)} %out_weight_ref.3, bf16[2,1024,512]{2,1,0:T(8,128)(2,1)} %get-tuple-element.49.gg_ref, f32[8,8,128]{2,1,0:T(8,128)} %get-tuple-element.50.sums_ref), custom_call_target="tpu_custom_call" | custom-call | flops 12000000000 | bytes 16000000 | tf_op jit(solution)/shard_map/cross_sums/pallas_call | solution.py:1176
  220.4 62.1 %mixer_backward.1 = (bf16[2,1024,1408]{2,1,0:T(8,128)(2,1)}, bf16[4,256,2048]{2,1,0:T(8,128)(2,1)}, f32[8,768]{1,0:T(8,128)}, f32[8,512]{1,0:T(8,128)}, f32[8,128]{1,0:T(8,128)}, /*index=5*/bf16[4,256,2048]{2,1,0:T(8,128)(2,1)}) custom-call(s32[2,4]{1,0:T(2,128)} %bitcast.57, f32[1]{0:T(128)} %bitcast.1.active_ref, ...), custom_call_target="tpu_custom_call" | custom-call | flops 60000002048 | bytes 60000000 | tf_op jit(solution)/shard_map/mixer_backward/pallas_call | solution.py:1233
  282.5 0.0 copy-start.7
  282.5 0.0 copy-start.3
  282.5 0.0 reduce-scatter.5.cloned.1.call-update
  282.5 0.7 copy-done.7
  283.2 0.6 reshape.123.in_gain_ref
  283.8 0.8 slice.28
  284.6 1.8 multiply_convert_fusion.gnorm_ref
  286.4 0.6 dynamic-slice_bitcast_fusion.1
  287.0 135.1 %bring_home.1 = (bf16[256,2128]{1,0:T(8,128)(2,1)}, f32[1024,256]{1,0:T(8,128)}, f32[4,4352]{1,0:T(4,128)}, f32[1,4352]{1,0:T(1,128)}, f32[1,4096]{1,0:T(1,128)}, /*index=5*/f32[8,64]{1,0:T(8,128)}, f32[8,256]{1,0:T(8,128)}) custom-call(bf16[2,1024,2048]{2,1,0:T(8,128)(2,1)} %get-tuple-element.45.x_ref.normed_ref, ...), custom_call_target="tpu_custom_call" | custom-call | flops 149999992832 | bytes 33554432 | tf_op jit(solution)/shard_map/bring_home/pallas_call | solution.py:1750
  422.0 0.0 copy-start.15
  422.0 0.0 reduce-scatter.5.cloned.1.call-done
  422.1 1.3 copy.36
  423.4 1.6 fusion.3
  425.0 0.0 copy-done.15
  425.0 0.0 copy-start.13
  425.1 0.0 copy-start.16
  425.1 1.3 slice_bitcast_fusion
  426.4 2.6 copy.31
  429.0 0.7 reduce.1
  429.6 0.0 copy-done.16
  429.7 3.9 fusion.5
  433.6 0.6 copy.40
  434.2 0.6 copy.41
  434.8 1.0 copy.42
  (26 shorter events, 0.1 us)
Async XLA Ops:
  7.2 279.8 %reduce-scatter.3.cloned.1.call-start = ((), (), s32[]{:S(2)}) async-start(), calls=%async_computation.2 | async-start | bytes 5242880 | tf_op jit(solution)/shard_map/reduce_scatter | solution.py:1868
  8.7 0.6 copy-start.14
  9.3 7.1 %copy-start.12 = (f32[2,128]{1,0:T(2,128)}, f32[2,128]{1,0:T(2,128)S(1)}, u32[]{:S(2)}) copy-start(f32[2,128]{1,0:T(2,128)S(1)} %add_rsqrt_fusion.1) | copy-start | bytes 3076
  14.9 1.5 copy-start
  14.9 1.5 copy-start.6
  16.0 1.7 copy-start.4
  198.8 223.3 %reduce-scatter.5.cloned.1.call-start = ((), (), s32[]{:S(2)}) async-start(), calls=%async_computation.3 | async-start | bytes 5242880 | tf_op jit(solution)/shard_map/reduce_scatter | solution.py:1890
  282.5 0.7 copy-start.7
  282.5 2.1 copy-start.3
  287.0 136.4 %copy-start.1 = (bf16[1,2,128,2048]{3,2,1,0:T(8,128)(2,1)S(1)}, bf16[1,2,128,2048]{3,2,1,0:T(8,128)(2,1)}, u32[]{:S(2)}) copy-start(bf16[1,2,128,2048]{3,2,1,0:T(8,128)(2,1)} %param.12) | copy-start | bytes 3145732
  287.0 136.4 %copy-start.8 = (f32[2048]{0:T(1024)S(1)}, f32[2048]{0:T(1024)}, u32[]{:S(2)}) copy-start(f32[2048]{0:T(1024)} %param.14) | copy-start | bytes 24580
  422.0 3.0 copy-start.15
  425.0 4.0 copy-start.10
  425.0 4.6 %copy-start.2 = (bf16[1,256,2048]{2,1,0:T(8,128)(2,1)S(1)}, bf16[1,256,2048]{2,1,0:T(8,128)(2,1)}, u32[]{:S(2)}) copy-start(bf16[1,256,2048]{2,1,0:T(8,128)(2,1)} %reduce-scatter.5.cloned.1.call-done) | copy-start | bytes 3145732
  425.0 4.6 %copy-start.13 = (f32[2,128]{1,0:T(2,128)S(1)}, f32[2,128]{1,0:T(2,128)}, u32[]{:S(2)}) copy-start(f32[2,128]{1,0:T(2,128)} %copy-done.12) | copy-start | bytes 3076
  425.1 4.6 %copy-start.16 = (f32[2,128]{1,0:T(2,128)S(1)}, f32[2,128]{1,0:T(2,128)}, u32[]{:S(2)}) copy-start(f32[2,128]{1,0:T(2,128)} %dynamic-slice_bitcast_fusion.1) | copy-start | bytes 3076
  429.6 3.9 copy-start.9
  429.7 4.6 %copy-start.11 = (f32[1,4096]{1,0:T(1,128)S(1)}, f32[1,4096]{1,0:T(1,128)}, u32[]{:S(2)}) copy-start(f32[1,4096]{1,0:T(1,128)} %get-tuple-element.77) | copy-start | bytes 49156
  429.7 5.2 %copy-start.5 = (f32[1024,256]{1,0:T(8,128)S(1)}, f32[1024,256]{1,0:T(8,128)}, u32[]{:S(2)}) copy-start(f32[1024,256]{1,0:T(8,128)} %get-tuple-element.129) | copy-start | bytes 3145732
Sparse Core Ops, SparseCore 0:
  198.9 80.5 reduce-scatter.2
  282.6 107.9 reduce-scatter.4
